TPU v7x, 32 devices: a whole 2x2x4 slice. The times are simulated.
32 devices in a mesh: seq: 8 (over y, x, core), head: 4 (over z).
Axes of the slice: x: 2, y: 2, z: 4, core: 2. Of those that a mesh axis runs over, the one named last changes fastest.
Arguments:
- tokens: bfloat16 [8, 1024, 1024], P('seq', 'head'), may hold values from -6 to 6
- cotangent: bfloat16 [8, 1024, 1024], P('seq', 'head'), may hold values from -6 to 6
- time_embed: bfloat16 [8, 256], P('seq'), may hold values from -6 to 6
- lengths: int32 [8], P('seq'), may hold values from 32 to 1024, as said below
- key_mask: int32 [8, 1024], P('seq'), may hold values from 0 to 1, as said below
- time_weight: bfloat16 [256, 2048], P(('seq', 'head')), may hold values from -0.09375 to 0.09375
- gain_attn: bfloat16 [1024], P(('seq', 'head')), may hold values from 0.5 to 1.5
- qkv_weight: bfloat16 [1024, 3072], P(('seq', 'head')), may hold values from -0.1875 to 0.1875
- out_weight: bfloat16 [1024, 1024], P(('seq', 'head')), may hold values from -1.5 to 1.5
- gain_mlp: bfloat16 [1024], P(('seq', 'head')), may hold values from 0.5 to 1.5
- in_weight: bfloat16 [1024, 4096], P(('seq', 'head')), may hold values from -0.1875 to 0.1875
- down_weight: bfloat16 [4096, 1024], P(('seq', 'head')), may hold values from -0.09375 to 0.09375
Outputs:
- output: bfloat16 [8, 1024, 1024], P('seq', 'head')
- grad_tokens: bfloat16 [8, 1024, 1024], P('seq', 'head')
- grad_time_weight: float32 [256, 2048], P(('seq', 'head'))
- grad_gain_attn: float32 [1024], P(('seq', 'head'))
- grad_qkv_weight: float32 [1024, 3072], P(('seq', 'head'))
- grad_out_weight: float32 [1024, 1024], P(('seq', 'head'))
- grad_gain_mlp: float32 [1024], P(('seq', 'head'))
- grad_in_weight: float32 [1024, 4096], P(('seq', 'head'))
- grad_down_weight: float32 [4096, 1024], P(('seq', 'head'))
Inputs may be any that keep to these rules, and one draw needn't show every extreme that they name: `lengths`: the first sequence has 1024 tokens and the last 32. `key_mask`: position 0 of every sequence is 1.
All inputs are finite; a program needn't handle non-finite values.
Results may differ from a plain program's by a relative error of at most 0.015.
Values may be sent and summed in bfloat16 or wider, within the bound.
No kernel may reach another device: no remote copies, remote signals or barrier semaphores. Data moves between devices by JAX's collectives and lax.ppermute only.
A program may use at most 192 MiB of HBM per device.

v0:
```python
import math

import jax
import jax.numpy as jnp
from jax import lax
from jax.sharding import Mesh
from jax.sharding import PartitionSpec as P

HEADS = 16
HD = 64

epsilon = 1e-05
f32 = jnp.float32
bf16 = jnp.bfloat16


def dot(left, right):
    return jnp.dot(left, right, preferred_element_type=f32)


def dot_right_t(left, right):
    return lax.dot_general(left, right, (((1,), (1,)), ((), ())), preferred_element_type=f32)


def dot_left_t(left, right):
    return lax.dot_general(left, right, (((0,), (0,)), ((), ())), preferred_element_type=f32)


def whiten(field):
    centre = jnp.mean(field, axis=-1, keepdims=True)
    shifted = field - centre
    variance = jnp.mean(shifted * shifted, axis=-1, keepdims=True)
    inv_std = lax.rsqrt(variance + epsilon)
    return shifted * inv_std, inv_std


def whiten_back(d_normed, whitened, inv_std, scale_vec):
    d_scale = jnp.sum(d_normed * whitened, axis=0, keepdims=True)
    d_white = d_normed * scale_vec
    d_input = inv_std * (
        d_white
        - jnp.mean(d_white, axis=-1, keepdims=True)
        - whitened * jnp.mean(d_white * whitened, axis=-1, keepdims=True)
    )
    return d_input, d_scale


def rope_tables(positions, repeats):
    half_dim = HD // 2
    inverse_freq = jnp.power(10000.0, -jnp.arange(half_dim, dtype=f32) * 2.0 / HD)
    angles = positions.astype(f32)[:, None] * inverse_freq[None, :]
    return jnp.cos(angles)[:, None, :], jnp.sin(angles)[:, None, :]


def rotate(field, cosine, sine):
    rows, width = field.shape
    field = field.reshape(rows, width // HD, HD)
    half_dim = HD // 2
    first, second = field[..., :half_dim], field[..., half_dim:]
    turned = jnp.concatenate(
        [first * cosine - second * sine, second * cosine + first * sine], axis=-1
    )
    return turned.reshape(rows, width)


def attend_forward(query, key, value, bias):
    length = query.shape[0]
    block = min(512, length)
    scale = 1.0 / math.sqrt(HD)
    mixed, logs = [], []
    for at in range(0, length, block):
        scores = jnp.einsum("qhd,khd->hqk", query[at : at + block], key, preferred_element_type=f32)
        scores = jnp.where(bias[None, None, :], scores * scale, -1e30)
        row_max = jnp.max(scores, axis=-1, keepdims=True)
        weights = jnp.exp(scores - row_max)
        row_sum = jnp.sum(weights, axis=-1, keepdims=True)
        low = (weights / row_sum).astype(bf16)
        mixed.append(
            jnp.einsum("hqk,khd->qhd", low, value, preferred_element_type=f32).astype(bf16)
        )
        logs.append((row_max + jnp.log(row_sum))[..., 0])
    return jnp.concatenate(mixed, axis=0), jnp.concatenate(logs, axis=1)


def attend_backward(query, key, value, log_sum, d_out, bias):
    length = query.shape[0]
    block = min(512, length)
    scale = 1.0 / math.sqrt(HD)
    d_key = jnp.zeros(key.shape, f32)
    d_value = jnp.zeros(value.shape, f32)
    d_query = []
    for at in range(0, length, block):
        q_block, d_block = query[at : at + block], d_out[at : at + block]
        scores = jnp.einsum("qhd,khd->hqk", q_block, key, preferred_element_type=f32) * scale
        scores = jnp.where(bias[None, None, :], scores, -1e30)
        probs = jnp.exp(scores - log_sum[:, at : at + block, None])
        low = probs.astype(bf16)
        d_value = d_value + jnp.einsum("hqk,qhd->khd", low, d_block, preferred_element_type=f32)
        d_probs = jnp.einsum("qhd,khd->hqk", d_block, value, preferred_element_type=f32)
        row_dot = jnp.sum(d_probs * probs, axis=-1, keepdims=True)
        d_scores = (probs * (d_probs - row_dot)).astype(bf16)
        d_query.append(
            jnp.einsum("hqk,khd->qhd", d_scores, key, preferred_element_type=f32) * scale
        )
        d_key = d_key + scale * jnp.einsum(
            "hqk,qhd->khd", d_scores, q_block, preferred_element_type=f32
        )
    return jnp.concatenate(d_query, axis=0), d_key, d_value


def build(seq_size, head_size):
    plane_bits = (seq_size // 2).bit_length() - 1
    planes = seq_size // 2
    assert planes == 1 << plane_bits and seq_size >= 2 and head_size == 4

    def swap(x, axis, mask, size):
        return lax.ppermute(x, axis, [(i, i ^ mask) for i in range(size)])

    def pick(x, index, axis):
        return lax.dynamic_index_in_dim(x, index, axis, keepdims=False)

    def join(own, other, bit, axis=0):
        return jnp.where(
            bit == 0, jnp.stack([own, other], axis=axis), jnp.stack([other, own], axis=axis)
        )

    def per_device(
        tokens,
        cotangent,
        time_embed,
        lengths,
        key_mask,
        time_weight,
        gain_attn,
        qkv_weight,
        out_weight,
        gain_mlp,
        in_weight,
        down_weight,
    ):
        core, plane = lax.axis_index("core"), lax.axis_index("plane")
        group, side = lax.axis_index("group"), lax.axis_index("side")
        stays = core == group
        _, span, width = tokens.shape
        full_len = span * head_size
        hidden_cols = in_weight.shape[1]
        head_cols, ff_cols = width // 4, hidden_cols // 4
        forwards = tuple(range(plane_bits))
        backwards = tuple(reversed(forwards))
        where = {"c": core, "g": group, "t": side}
        where.update({bit: (plane >> bit) & 1 for bit in range(plane_bits)})
        natural = list(backwards) + ["c", "g", "t"]

        def send(x, axis):
            if axis in ("c", "g", "t"):
                name = {"c": "core", "g": "group", "t": "side"}[axis]
                return swap(x, name, 1, 2)
            return swap(x, "plane", 1 << axis, planes)

        def moved(x):
            return jnp.where(stays, x, lax.ppermute(x, ("core", "group"), [(1, 2), (2, 1)]))

        def after(x, first):
            return lax.optimization_barrier((x, first))[0]

        def gather(x, labels, axes):
            for axis in axes:
                x = join(x, send(x, axis), where[axis])
                labels = [axis] + labels
            return x, labels

        def in_order(x, labels):
            wanted = [axis for axis in natural if axis in labels]
            perm = [labels.index(axis) for axis in wanted]
            x = x.transpose(perm + list(range(len(perm), x.ndim)))
            return x.reshape(-1, x.shape[-1])

        def exchange(parts, axis):
            mine = where[axis]
            return join(pick(parts, mine, 0), send(pick(parts, 1 - mine, 0), axis), mine)

        def reduce_rows(x, labels, axes):
            labels = [axis for axis in natural if axis in labels]
            y = x.astype(bf16).reshape((2,) * len(labels) + (-1, x.shape[-1]))
            for step, axis in enumerate(axes):
                at, mine = labels.index(axis), where[axis]
                other = send(pick(y, 1 - mine, at), axis)
                y = pick(y, mine, at).astype(f32) + other.astype(f32)
                if step + 1 < len(axes):
                    y = y.astype(bf16)
                labels.remove(axis)
            return y

        chunk = out_weight.shape[0] * head_size
        aligned = (chunk % HD == 0) and (width // (2 * chunk)) % 2 == 0

        def qkv_split(w):
            rows = w.shape[0]
            if aligned:
                w = w.reshape(rows, 3, 2, -1, 2, chunk).transpose(4, 2, 0, 1, 3, 5)
            else:
                w = w.reshape(rows, 3, 2, 2, head_cols).transpose(2, 3, 0, 1, 4)
            return w.reshape(2, 2, rows, 3 * head_cols)

        def qkv_join(w):
            rows = w.shape[2]
            if aligned:
                w = w.reshape(2, 2, rows, 3, -1, chunk).transpose(2, 3, 1, 4, 0, 5)
            else:
                w = w.reshape(2, 2, rows, 3, head_cols).transpose(2, 3, 0, 1, 4)
            return w.reshape(rows, 3 * width)

        ff_rows = down_weight.shape[0]

        def in_split(w):
            rows = w.shape[0]
            w = w.reshape(rows, planes, 2, 2, 2, ff_rows).transpose(2, 4, 0, 1, 3, 5)
            return w.reshape(2, 2, rows, ff_cols)

        def in_join(w):
            rows = w.shape[2]
            w = w.reshape(2, 2, rows, planes, 2, ff_rows).transpose(2, 3, 0, 4, 1, 5)
            return w.reshape(rows, hidden_cols)

        def quad(parts):
            x = exchange(parts, "c")
            return exchange(x.transpose(1, 0, 2, 3), "t")

        def quad_back(x):
            x = exchange(x, "c")
            x = exchange(x.transpose(1, 0, 2, 3), "t")
            return x.transpose(1, 0, 2, 3)

        aux = jnp.concatenate(
            [
                key_mask.astype(f32),
                time_embed.astype(f32),
                jnp.broadcast_to(lengths.astype(f32)[:, None], (1, 128)),
            ],
            axis=1,
        )
        aux_other = send(aux, "c")
        aux_both = join(aux[0], aux_other[0], core)
        embed_both = aux_both[:, full_len : full_len + time_embed.shape[1]]
        aux_mine = pick(aux_both, group, 0)
        length = aux_mine[full_len + time_embed.shape[1]].astype(jnp.int32)
        usable = jnp.logical_and(
            aux_mine[:full_len] > 0, jnp.arange(full_len, dtype=jnp.int32) < length
        )

        piece = out_weight.shape[0]

        def out_heads(x):
            x = x.reshape(2, -1, piece, width)
            x = exchange(x, "t")
            return x.transpose(1, 0, 2, 3).reshape(head_cols, width)

        def out_pieces(x):
            x = x.reshape(-1, 2, piece, width).transpose(1, 0, 2, 3)
            return exchange(x, "t").reshape(head_cols, width)

        qkv_scaled = (qkv_weight.astype(f32) * gain_attn.astype(f32)[:, None]).astype(bf16)
        in_scaled = (in_weight.astype(f32) * gain_mlp.astype(f32)[:, None]).astype(bf16)
        qkv_quad = quad(qkv_split(qkv_scaled))
        w_qkv, labels = gather(qkv_quad, ["t", "c"], ["g"])
        gate = w_qkv
        cut = 3 * head_cols // 2
        w_qkv = jnp.concatenate(
            [
                in_order(*gather(w_qkv[..., :cut], labels, forwards)),
                in_order(*gather(w_qkv[..., cut:], labels, backwards)),
            ],
            axis=1,
        )
        in_quad = quad(in_split(after(in_scaled, qkv_quad)))
        rows_in = 4 * in_weight.shape[0]
        packs = [in_quad.reshape(rows_in, width), down_weight] + ([out_weight] if aligned else [])
        packs = lax.all_gather(jnp.concatenate(packs), ("plane", "group"), axis=0)
        w_in = packs[:, :rows_in].reshape(planes, 2, 2, 2, -1, width)
        w_in = w_in.transpose(0, 3, 1, 2, 4, 5).reshape(width, ff_cols)
        w_down = packs[:, rows_in : rows_in + ff_rows].reshape(ff_cols, width)
        if aligned:
            w_out = out_heads(packs[:, rows_in + ff_rows :])
        else:
            w_out, labels = gather(out_weight, [], ("c", "t", "g") + forwards)
            w_out = lax.dynamic_slice_in_dim(
                in_order(w_out, labels), (2 * core + side) * head_cols, head_cols, 0
            )

        t_rows, labels = gather(after(time_weight, qkv_quad), [], forwards[:1])
        t_rows = in_order(*gather(after(t_rows, gate), labels, forwards[1:]))
        embed_rows = pick(
            pick(embed_both.reshape(2, planes, 2, head_size, -1), core, 2), 2 * group + side, 2
        ).reshape(2, -1)
        part = jnp.dot(
            embed_rows, t_rows.astype(f32), precision=lax.Precision.HIGHEST
        )
        part_mine = pick(part, group, 0) + send(pick(part, 1 - group, 0), "g")
        part_mine = part_mine + send(part_mine, "t")
        scales = 1.0 + (part_mine + send(part_mine, "c"))
        scale_attn, scale_mlp = scales[None, :width], scales[None, width:]

        blocks = (
            side + 2 * core,
            side + 2 - 2 * core,
            1 - side + 2 * core,
            1 - side + 2 - 2 * core,
        )
        steps = jnp.arange(span, dtype=jnp.int32)
        valid = (blocks[0] * span + steps < length).astype(f32)[:, None]
        cosine, sine = rope_tables(jnp.concatenate([block * span + steps for block in blocks]), 0)
        usable_blocks = usable.reshape(head_size, span)
        bias = jnp.concatenate([pick(usable_blocks, block, 0) for block in blocks])

        def gather_four(x):
            across = send(x, "t")
            return jnp.concatenate([x, send(x, "c"), across, send(across, "c")])

        def sum_four(x):
            x = x.reshape(2, 2, span, width)
            x = x[:, 0] + send(x[:, 1].astype(bf16), "c").astype(f32)
            return x[0] + send(x[1].astype(bf16), "t").astype(f32)

        inputs = moved(tokens[0]).astype(f32)
        upstream = moved(after(cotangent[0], gate)).astype(f32)
        white_a, inv_a = whiten(inputs)
        all_a = gather_four((white_a * scale_attn).astype(bf16))
        packed = dot(all_a, w_qkv)
        head_shape = (full_len, head_cols // HD, HD)
        query = rotate(packed[:, :head_cols], cosine, sine).astype(bf16).reshape(head_shape)
        key = rotate(packed[:, head_cols : 2 * head_cols], cosine, sine).astype(bf16)
        key = key.reshape(head_shape)
        value = packed[:, 2 * head_cols :].astype(bf16).reshape(head_shape)
        mixed, log_sum = attend_forward(query, key, value, bias)
        mixed = mixed.reshape(full_len, head_cols)

        hidden = inputs + valid * sum_four(dot(mixed, w_out))
        white_m, inv_m = whiten(hidden)
        all_m = gather_four((white_m * scale_mlp).astype(bf16))
        upper = dot(all_m, w_in)
        phi = 0.5 * (1.0 + lax.erf(upper / math.sqrt(2.0)))
        activation = (upper * phi).astype(bf16)
        slope = phi + upper * jnp.exp(-0.5 * upper * upper) / math.sqrt(2.0 * math.pi)
        activation, slope = lax.optimization_barrier((activation, slope))
        output = hidden + valid * sum_four(dot(activation, w_down))
        output = moved(output.astype(bf16))[None]

        all_d = gather_four((valid * upstream).astype(bf16))
        d_upper = (dot_right_t(all_d, w_down) * slope).astype(bf16)
        down_axes = [axis for axis in natural if axis not in ("c", "t")]
        grad_down = dot_left_t(activation, all_d).astype(bf16).reshape(planes, 2 * ff_rows, width)
        d_normed_m = sum_four(dot_right_t(d_upper, w_in))
        grad_in = dot_left_t(all_m, d_upper).astype(bf16).reshape(planes, 2 * rows_in, width)
        both = lax.psum_scatter(
            jnp.concatenate([grad_in, grad_down], axis=1), "plane", scatter_dimension=0, tiled=True
        )[0]
        both_in = both[: 2 * rows_in].reshape(2, 2, 2, -1, width).transpose(1, 0, 2, 3, 4)
        both = jnp.concatenate(
            [both_in.reshape(2, rows_in, width), both[2 * rows_in :].reshape(2, ff_rows, width)],
            axis=1,
        )
        both = pick(both, group, 0).astype(f32) + send(pick(both, 1 - group, 0), "g").astype(f32)
        in_sums = both[:rows_in].reshape(2, 2, -1, width)
        sum_down = both[rows_in:]
        d_from_m, d_scale_m = whiten_back(d_normed_m, white_m, inv_m, scale_mlp)
        d_hidden = upstream + d_from_m
        all_da = gather_four((valid * d_hidden).astype(bf16))
        grad_out = dot_left_t(mixed, all_da).astype(bf16)
        if aligned:
            out_rows = out_pieces(grad_out).reshape(planes, -1, width)
            out_rows = lax.psum_scatter(out_rows, "plane", scatter_dimension=0, tiled=True)
            sum_out = reduce_rows(out_rows[0], ["g"], ["g"])
        else:
            padded = lax.dynamic_update_slice_in_dim(
                jnp.zeros((width, width), bf16), grad_out, (2 * core + side) * head_cols, 0
            )
            sum_out = reduce_rows(padded, natural, forwards + ("g", "t", "c"))
        d_mixed = dot_right_t(all_da, w_out).astype(bf16).reshape(head_shape)
        d_query, d_key, d_value = attend_backward(query, key, value, log_sum, d_mixed, bias)
        d_packed = jnp.concatenate(
            [
                rotate(
                    d_query.astype(bf16).astype(f32).reshape(full_len, head_cols), cosine, -sine
                ).astype(bf16),
                rotate(
                    d_key.astype(bf16).astype(f32).reshape(full_len, head_cols), cosine, -sine
                ).astype(bf16),
                d_value.astype(bf16).reshape(full_len, head_cols),
            ],
            axis=1,
        )
        grad_qkv = dot_left_t(all_a, d_packed)
        qkv_sums = jnp.concatenate(
            [
                reduce_rows(grad_qkv[:, :cut], natural, forwards + ("g",)),
                reduce_rows(grad_qkv[:, cut:], natural, backwards + ("g",)),
            ],
            axis=-1,
        )
        d_normed_a = sum_four(dot_right_t(d_packed, w_qkv))
        d_from_a, d_scale_a = whiten_back(d_normed_a, white_a, inv_a, scale_attn)
        grad_tokens = moved((d_hidden + d_from_a).astype(bf16))[None]

        raw_qkv = qkv_join(quad_back(qkv_sums.astype(bf16))).astype(f32)
        raw_in = in_join(quad_back(in_sums.astype(bf16))).astype(f32)
        sum_gain_a = jnp.sum(raw_qkv * qkv_weight.astype(f32), axis=1)
        sum_gain_m = jnp.sum(raw_in * in_weight.astype(f32), axis=1)
        sum_qkv = raw_qkv * gain_attn.astype(f32)[:, None]
        sum_in = raw_in * gain_mlp.astype(f32)[:, None]

        d_scale = jnp.concatenate([d_scale_a, d_scale_m], axis=1)
        d_scale = d_scale + send(d_scale, "c")
        d_scale = d_scale + send(d_scale, "t")
        d_both = join(d_scale[0], send(d_scale, "g")[0], group)
        rows_time = lax.dot_general(
            embed_rows,
            d_both,
            (((0,), (0,)), ((), ())),
            precision=lax.Precision.HIGHEST,
            preferred_element_type=f32,
        ).reshape((2,) * plane_bits + (-1, 2 * width))
        alive = list(backwards)
        for axis in backwards:
            at, mine = alive.index(axis), where[axis]
            rows_time = pick(rows_time, mine, at) + send(pick(rows_time, 1 - mine, at), axis)
            alive.remove(axis)
        return (
            output,
            grad_tokens,
            rows_time,
            sum_gain_a,
            sum_qkv,
            sum_out,
            sum_gain_m,
            sum_in,
            sum_down,
        )

    return per_device


def solution(mesh):
    seq_size, head_size = mesh.shape["seq"], mesh.shape["head"]
    own_mesh = Mesh(
        mesh.devices.reshape(seq_size // 2, 2, 2, head_size // 2),
        ("plane", "core", "group", "side"),
    )
    seq, head = ("plane", "core"), ("group", "side")
    rows, both, flat = P(seq + head, None), P(seq, head, None), P(seq + head)
    return jax.shard_map(
        build(seq_size, head_size),
        mesh=own_mesh,
        in_specs=(
            both,
            both,
            P(seq, None),
            P(seq),
            P(seq, None),
            rows,
            flat,
            rows,
            rows,
            flat,
            rows,
            rows,
        ),
        out_specs=(both, both, rows, flat, rows, rows, flat, rows, rows),
        check_vma=False,
    )
```

profile of v0, /device:TPU:0, one launch (start us, length us, event | category | flops | bytes accessed | tf_op | source)
XLA Modules:
  0.0 454.9 jit_solution(11364442724456246167)
XLA Ops:
  14.8 3.1 collective-permute-start.3
  18.0 3.9 collective-permute-done.3
  21.9 7.2 %collective-permute-start.5 = (bf16[2,2,32,768]{3,2,0,1:T(8,128)(2,1)S(1)}, bf16[2,2,32,768]{3,2,0,1:T(8,128)(2,1)S(1)}, u32[]{:S(2)}, u32[]{:S(2)}) collective-permute-start(bf16[2,2,32,768]{3,2,0,1:T(8,128)(2,1)S(1)} %maximum_select_fusion.14), channel_id=1, source_target_pairs={{0,2},{2,0},{1,3},{3,1},{4,6},{6,4},{5,7},{7,5},{8,10},{10,8},{9,1... | collective-permute-start | bytes 589832 | tf_op jit(solution)/shard_map/ppermute | solution.py:117
  33.3 6.3 %collective-permute-done.5 = bf16[2,2,32,768]{3,2,0,1:T(8,128)(2,1)S(1)} collective-permute-done((bf16[2,2,32,768]{3,2,0,1:T(8,128)(2,1)S(1)}, bf16[2,2,32,768]{3,2,0,1:T(8,128)(2,1)S(1)}, u32[]{:S(2)}, u32[]{:S(2)}) %collective-permute-start.5) | collective-permute-done | bytes 196640 | tf_op jit(solution)/shard_map/ppermute | solution.py:117
  44.9 3.9 collective-permute-done.7
  49.0 3.4 collective-permute-done.8
  59.3 5.4 %collective-permute-done.15 = bf16[2,2,2,32,384]{4,3,1,0,2:T(8,128)(2,1)S(1)} collective-permute-done((bf16[2,2,2,32,384]{4,3,1,0,2:T(8,128)(2,1)S(1)}, bf16[2,2,2,32,384]{4,3,1,0,2:T(8,128)(2,1)S(1)}, u32[]{:S(2)}, u32[]{:S(2)}) %collective-permute-start.15) | collective-permute-done | bytes 196640 | tf_op jit(solution)/shard_map/ppermute | solution.py:117
  67.0 7.5 %collective-permute-done.11 = bf16[256,1024]{1,0:T(8,128)(2,1)S(1)} collective-permute-done((bf16[256,1024]{1,0:T(8,128)(2,1)S(1)}, bf16[256,1024]{1,0:T(8,128)(2,1)S(1)}, u32[]{:S(2)}, u32[]{:S(2)}) %collective-permute-start.11) | collective-permute-done | bytes 524320 | tf_op jit(solution)/shard_map/ppermute | solution.py:117
  74.6 6.8 %collective-permute-done.16 = bf16[2,2,2,2,32,384]{5,4,2,1,3,0:T(8,128)(2,1)S(1)} collective-permute-done((bf16[2,2,2,2,32,384]{5,4,2,1,3,0:T(8,128)(2,1)S(1)}, bf16[2,2,2,2,32,384]{5,4,2,1,3,0:T(8,128)(2,1)S(1)}, u32[]{:S(2)}, u32[]{:S(2)}) %collective-permute-start.16) | collective-permute-done | bytes 393248 | tf_op jit(solution)/shard_map/ppermute | solution.py:117
  83.6 1.9 fusion.72
  87.3 2.3 fusion.16
  90.7 4.1 fusion
  94.8 2.5 fusion.48
  97.3 32.6 %all-gather.3.cloned.1.call-done = bf16[2304,1024]{1,0:T(8,128)(2,1)} async-done(((bf16[288,1024]{1,0:T(8,128)(2,1)}), bf16[2304,1024]{1,0:T(8,128)(2,1)}) %all-gather.3.cloned.1.call-update) | async-done | bytes 4718608 | tf_op jit(solution)/shard_map/all_gather | solution.py:278
  131.8 4.7 %fusion.49 = bf16[512,4,64]{0,2,1:T(8,128)(2,1)S(1)} fusion(bf16[1024,4,64]{0,2,1:T(8,128)(2,1)S(1)} %bitcast.327, f32[4,512]{1,0:T(4,128)S(1)} %get-tuple-element.30, f32[4,512]{1,0:T(4,128)S(1)} %get-tuple-element.32, f32[4,512,1024]{2,1,0:T(8,128)} %copy-done, pred[1024]{0:T(1024)(128)(4,1)S(1)} %pad_add_fusion), kind=kOutput, calls=%fused_computation.91 | convolution fusion | flops 279052288 | bytes 9192448 | tf_op jit(solution)/shard_map/hqk,khd->qhd/dot_general | solution.py:79
  136.9 3.1 collective-permute-done.19
  143.0 1.8 collective-permute-done.20
  145.7 19.3 %collective-permute-done.21 = bf16[256,1024]{1,0:T(8,128)(2,1)S(1)} collective-permute-done((bf16[256,1024]{1,0:T(8,128)(2,1)S(1)}, bf16[256,1024]{1,0:T(8,128)(2,1)S(1)}, u32[]{:S(2)}, u32[]{:S(2)}) %collective-permute-start.21) | collective-permute-done | bytes 524320 | tf_op jit(solution)/shard_map/ppermute | solution.py:117
  166.1 2.0 collective-permute-start.30
  168.1 12.8 %collective-permute-done.23 = bf16[256,1024]{1,0:T(8,128)(2,1)S(1)} collective-permute-done((bf16[256,1024]{1,0:T(8,128)(2,1)S(1)}, bf16[256,1024]{1,0:T(8,128)(2,1)S(1)}, u32[]{:S(2)}, u32[]{:S(2)}) %collective-permute-start.23) | collective-permute-done | bytes 524320 | tf_op jit(solution)/shard_map/ppermute | solution.py:117
  182.1 8.4 %collective-permute-done.30 = bf16[256,1024]{1,0:T(8,128)(2,1)S(1)} collective-permute-done((bf16[256,1024]{1,0:T(8,128)(2,1)S(1)}, bf16[256,1024]{1,0:T(8,128)(2,1)S(1)}, u32[]{:S(2)}, u32[]{:S(2)}) %collective-permute-start.30) | collective-permute-done | bytes 524320 | tf_op jit(solution)/shard_map/ppermute | solution.py:117
  190.6 3.4 fusion.7
  194.2 2.4 multiply_convert_fusion.2
  196.6 2.4 fusion.22
  199.7 2.3 fusion.24
  203.2 1.8 collective-permute-done.25
  205.9 11.8 %collective-permute-done.33 = bf16[256,1024]{1,0:T(8,128)(2,1)S(1)} collective-permute-done((bf16[256,1024]{1,0:T(8,128)(2,1)S(1)}, bf16[256,1024]{1,0:T(8,128)(2,1)S(1)}, u32[]{:S(2)}, u32[]{:S(2)}) %collective-permute-start.33) | collective-permute-done | bytes 524320 | tf_op jit(solution)/shard_map/ppermute | solution.py:117
  218.2 10.2 %collective-permute-done.26 = bf16[256,1024]{1,0:T(8,128)(2,1)S(1)} collective-permute-done((bf16[256,1024]{1,0:T(8,128)(2,1)S(1)}, bf16[256,1024]{1,0:T(8,128)(2,1)S(1)}, u32[]{:S(2)}, u32[]{:S(2)}) %collective-permute-start.26) | collective-permute-done | bytes 524320 | tf_op jit(solution)/shard_map/ppermute | solution.py:117
  228.4 1.9 multiply_convert_fusion.4
  230.6 13.5 %collective-permute-done.35 = bf16[256,1024]{1,0:T(8,128)(2,1)} collective-permute-done((bf16[256,1024]{1,0:T(8,128)(2,1)}, bf16[256,1024]{1,0:T(8,128)(2,1)}, u32[]{:S(2)}, u32[]{:S(2)}) %collective-permute-start.35) | collective-permute-done | bytes 524320 | tf_op jit(solution)/shard_map/ppermute | solution.py:117
  244.1 2.2 collective-permute-done.36
  246.3 2.4 convolution_convert_fusion.3
  249.2 8.0 %collective-permute-done.53 = bf16[4,32,1024]{2,1,0:T(8,128)(2,1)S(1)} collective-permute-done((bf16[4,32,1024]{2,1,0:T(8,128)(2,1)S(1)}, bf16[4,32,1024]{2,1,0:T(8,128)(2,1)S(1)}, u32[]{:S(2)}, u32[]{:S(2)}) %collective-permute-start.53) | collective-permute-done | bytes 262176 | tf_op jit(solution)/shard_map/ppermute | solution.py:117
  258.2 4.8 %convolution_convert_fusion.1 = bf16[1024,1024]{1,0:T(8,128)(2,1)S(1)} fusion(bf16[1024,1024]{1,0:T(8,128)(2,1)} %copy-done.55, bf16[256,1024]{1,0:T(8,128)(2,1)} %copy-done.48, bf16[256,1024]{1,0:T(8,128)(2,1)} %copy-done.46, bf16[256,1024]{1,0:T(8,128)(2,1)} %copy-done.47, bf16[256,1024]{1,0:T(8,128)(2,1)} %copy-done.21), kind=kOutput, calls=%fused_computation.54 | convolution fusion | flops 2156920832 | bytes 6291456 | tf_op jit(solution)/shard_map/dot_general | solution.py:26
  263.0 2.4 convolution_convert_fusion
  265.4 2.4 pad_maximum_fusion
  267.8 1.6 collective-permute-start.27
  269.5 2.4 convolution_convert_fusion.4
  272.6 4.6 %fusion.149 = f32[4,512,1024]{2,1,0:T(8,128)} fusion(bf16[512,4,64]{0,2,1:T(8,128)(2,1)S(1)} %bitcast.364, bf16[1024,4,64]{0,2,1:T(8,128)(2,1)S(1)} %bitcast.328), kind=kOutput, calls=%fused_computation.344 | convolution fusion | flops 268435456 | bytes 9175040 | tf_op jit(solution)/shard_map/qhd,khd->hqk/dot_general | solution.py:99
  277.3 13.1 %multiply_reduce_fusion = (f32[4,512]{1,0:T(4,128)}, f32[4,512]{1,0:T(4,128)}, f32[4,512,1024]{2,1,0:T(8,128)}) fusion(f32[4,512]{1,0:T(4,128)S(1)} %log_add_fusion, f32[4,512,1024]{2,1,0:T(8,128)S(1)} %bitcast.322, pred[1024]{0:T(1024)(128)(4,1)S(1)} %pad_add_fusion, f32[4,512,1024]{2,1,0:T(8,128)} %fusion.149, f32[4,512]{1,0:T(4,128)S(1)} %log_add_fusion.1, ...), kind=kOutput, calls=%fused_computation.1 | convolution fusion | flops 289402880 | bytes 34374656 | tf_op jit(solution)/shard_map/qhd,khd->hqk/dot_general | solution.py:99
  290.5 9.3 %multiply_convert_fusion = (bf16[4,512,1024]{2,1,0:T(8,128)(2,1)S(1)}, bf16[4,512,1024]{2,1,0:T(8,128)(2,1)S(1)}) fusion(f32[4,512,1024]{2,1,0:T(8,128)} %get-tuple-element.114, f32[4,512]{1,0:T(4,128)} %get-tuple-element.27, f32[4,512]{1,0:T(4,128)S(1)} %log_add_fusion, f32[4,512,1024]{2,1,0:T(8,128)S(1)} %bitcast.322, pred[1024]{0:T(1024)(128)(4,1)S(1)} %pad_add_fusion, ...), kind=kLoop, calls=%fused_computation | loop fusion | flops 25165824 | bytes 41976832 | tf_op jit(solution)/shard_map/convert_element_type | solution.py:101
  302.0 1.9 fusion.8
  306.2 2.3 fusion.30
  310.0 1.9 fusion.71
  311.9 1.9 convolution_convert_fusion.2
  314.0 2.0 collective-permute-start.48
  318.8 8.4 %collective-permute-done.48 = bf16[2,2,2,2,32,384]{5,4,3,2,1,0:T(8,128)(2,1)S(1)} collective-permute-done((bf16[2,2,2,2,32,384]{5,4,3,2,1,0:T(8,128)(2,1)S(1)}, bf16[2,2,2,2,32,384]{5,4,3,2,1,0:T(8,128)(2,1)S(1)}, u32[]{:S(2)}, u32[]{:S(2)}) %collective-permute-start.48) | collective-permute-done | bytes 393248 | tf_op jit(solution)/shard_map/ppermute | solution.py:117
  328.5 2.6 collective-permute-done.45
  331.4 7.3 %collective-permute-done.49 = bf16[2,2,2,32,384]{4,3,2,1,0:T(8,128)(2,1)S(1)} collective-permute-done((bf16[2,2,2,32,384]{4,3,2,1,0:T(8,128)(2,1)S(1)}, bf16[2,2,2,32,384]{4,3,2,1,0:T(8,128)(2,1)S(1)}, u32[]{:S(2)}, u32[]{:S(2)}) %collective-permute-start.49) | collective-permute-done | bytes 196640 | tf_op jit(solution)/shard_map/ppermute | solution.py:117
  338.8 2.2 collective-permute-done.46
  341.9 5.8 %collective-permute-done.50 = bf16[2,2,32,384]{3,2,1,0:T(8,128)(2,1)S(1)} collective-permute-done((bf16[2,2,32,384]{3,2,1,0:T(8,128)(2,1)S(1)}, bf16[2,2,32,384]{3,2,1,0:T(8,128)(2,1)S(1)}, u32[]{:S(2)}, u32[]{:S(2)}) %collective-permute-start.50) | collective-permute-done | bytes 98336 | tf_op jit(solution)/shard_map/ppermute | solution.py:117
  351.2 4.0 collective-permute-done.52
  356.8 2.2 fusion.18
  362.5 2.5 broadcast_multiply_fusion.1
  365.0 7.8 %collective-permute-done.54 = bf16[32,1024]{1,0:T(8,128)(2,1)S(1)} collective-permute-done((bf16[32,1024]{1,0:T(8,128)(2,1)S(1)}, bf16[32,1024]{1,0:T(8,128)(2,1)S(1)}, u32[]{:S(2)}, u32[]{:S(2)}) %collective-permute-start.54) | collective-permute-done | bytes 65568 | tf_op jit(solution)/shard_map/ppermute | solution.py:117
  374.4 20.1 %all-reduce.4.cloned.1.call-done = bf16[4,512,1024]{2,1,0:T(8,128)(2,1)} async-done(((bf16[4,512,1024]{2,1,0:T(8,128)(2,1)}), bf16[4,512,1024]{2,1,0:T(8,128)(2,1)}) %all-reduce.4.cloned.1.call-update) | async-done | bytes 4194320
  394.4 2.1 constant_dynamic-slice_fusion.15
  397.3 2.5 collective-permute-start.55
  401.4 10.5 %collective-permute-done.41 = f32[1,2048]{1,0:T(1,128)S(1)} collective-permute-done((f32[1,2048]{1,0:T(1,128)S(1)}, f32[1,2048]{1,0:T(1,128)S(1)}, u32[]{:S(2)}, u32[]{:S(2)}) %collective-permute-start.41) | collective-permute-done | bytes 8224 | tf_op jit(solution)/shard_map/ppermute | solution.py:117
  411.9 2.5 collective-permute-start.42
  414.4 9.8 %collective-permute-done.42 = f32[1,2048]{1,0:T(1,128)S(1)} collective-permute-done((f32[1,2048]{1,0:T(1,128)S(1)}, f32[1,2048]{1,0:T(1,128)S(1)}, u32[]{:S(2)}, u32[]{:S(2)}) %collective-permute-start.42) | collective-permute-done | bytes 8224 | tf_op jit(solution)/shard_map/ppermute | solution.py:117
  427.3 2.5 collective-permute-done.43
  431.7 2.4 collective-permute-done.44
  437.5 7.5 %collective-permute-done.57 = bf16[2,32,1024]{2,1,0:T(8,128)(2,1)S(1)} collective-permute-done((bf16[2,32,1024]{2,1,0:T(8,128)(2,1)S(1)}, bf16[2,32,1024]{2,1,0:T(8,128)(2,1)S(1)}, u32[]{:S(2)}, u32[]{:S(2)}) %collective-permute-start.57) | collective-permute-done | bytes 131104 | tf_op jit(solution)/shard_map/ppermute | solution.py:117
  (377 shorter events, 78.9 us)
Async XLA Ops:
  7.2 122.8 %all-gather.3.cloned.1.call-start = ((), (), s32[]{:S(2)}) async-start(), calls=%async_computation.1 | async-start | bytes 5308416 | tf_op jit(solution)/shard_map/all_gather | solution.py:278
  9.3 5.4 %collective-permute-start.2 = (bf16[2,32,768]{2,1,0:T(8,128)(2,1)S(1)}, bf16[2,32,768]{2,1,0:T(8,128)(2,1)S(1)}, u32[]{:S(2)}, u32[]{:S(2)}) collective-permute-start(bf16[2,32,768]{2,1,0:T(8,128)(2,1)S(1)} %get-tuple-element.102), channel_id=1, source_target_pairs={{0,4},{4,0},{1,5},{5,1},{2,6},{6,2},{3,7},{7,3},{8,12},{12,8},{9,1... | collective-permute-start | bytes 294920 | tf_op jit(solution)/shard_map/ppermute | solution.py:117
  11.9 2.6 collective-permute-start.1
  12.0 42.9 %collective-permute-start = (bf16[256,1024]{1,0:T(8,128)(2,1)}, bf16[256,1024]{1,0:T(8,128)(2,1)S(1)}, u32[]{:S(2)}, u32[]{:S(2)}) collective-permute-start(bf16[256,1024]{1,0:T(8,128)(2,1)} %bitcast.378), channel_id=1, source_target_pairs={{2,4},{4,2},{3,5},{5,3},{10,12},{12,10},{11,13},{13,11},{18,20},{2... | collective-permute-start | bytes 1572872 | tf_op jit(solution)/shard_map/ppermute | solution.py:161
  14.8 7.1 %collective-permute-start.3 = (bf16[2,32,768]{2,1,0:T(8,128)(2,1)S(1)}, bf16[2,32,768]{2,1,0:T(8,128)(2,1)S(1)}, u32[]{:S(2)}, u32[]{:S(2)}) collective-permute-start(bf16[2,32,768]{2,1,0:T(8,128)(2,1)S(1)} %get-tuple-element.99), channel_id=1, source_target_pairs={{0,1},{1,0},{2,3},{3,2},{4,5},{5,4},{6,7},{7,6},{8,9},{9,8},{10,11... | collective-permute-start | bytes 294920 | tf_op jit(solution)/shard_map/ppermute | solution.py:117
  21.9 17.6 %collective-permute-start.5 = (bf16[2,2,32,768]{3,2,0,1:T(8,128)(2,1)S(1)}, bf16[2,2,32,768]{3,2,0,1:T(8,128)(2,1)S(1)}, u32[]{:S(2)}, u32[]{:S(2)}) collective-permute-start(bf16[2,2,32,768]{3,2,0,1:T(8,128)(2,1)S(1)} %maximum_select_fusion.14), channel_id=1, source_target_pairs={{0,2},{2,0},{1,3},{3,1},{4,6},{6,4},{5,7},{7,5},{8,10},{10,8},{9,1... | collective-permute-start | bytes 589832 | tf_op jit(solution)/shard_map/ppermute | solution.py:117
  29.1 4.1 collective-permute-start.4
  31.2 1.4 collective-permute-start.17
  32.6 9.6 %collective-permute-start.18 = (bf16[2,32,1024]{2,1,0:T(8,128)(2,1)S(1)}, bf16[2,32,1024]{2,1,0:T(8,128)(2,1)S(1)}, u32[]{:S(2)}, u32[]{:S(2)}) collective-permute-start(bf16[2,32,1024]{2,1,0:T(8,128)(2,1)S(1)} %get-tuple-element.89), channel_id=1, source_target_pairs={{0,1},{1,0},{2,3},{3,2},{4,5},{5,4},{6,7},{7,6},{8,9},{9,8},{10,11... | collective-permute-start | bytes 393224 | tf_op jit(solution)/shard_map/ppermute | solution.py:117
  39.6 4.3 collective-permute-start.6
  43.2 317.0 %reduce-scatter.4.cloned.1.call-start = ((), (), s32[]{:S(2)}) async-start(), calls=%async_computation.3 | async-start | bytes 655360
  44.1 4.6 %collective-permute-start.7 = (f32[2048]{0:T(1024)S(1)}, f32[2048]{0:T(1024)S(1)}, u32[]{:S(2)}, u32[]{:S(2)}) collective-permute-start(f32[2048]{0:T(1024)S(1)} %bitcast.412), channel_id=1, source_target_pairs={{0,2},{2,0},{1,3},{3,1},{4,6},{6,4},{5,7},{7,5},{8,10},{10,8},{9,1... | collective-permute-start | bytes 24584 | tf_op jit(solution)/shard_map/ppermute | solution.py:117
  48.8 3.7 collective-permute-start.8
  52.4 2.5 collective-permute-start.9
  55.8 18.6 %collective-permute-start.11 = (bf16[256,1024]{1,0:T(8,128)(2,1)S(1)}, bf16[256,1024]{1,0:T(8,128)(2,1)S(1)}, u32[]{:S(2)}, u32[]{:S(2)}) collective-permute-start(bf16[256,1024]{1,0:T(8,128)(2,1)S(1)} %fusion.50), channel_id=1, source_target_pairs={{0,1},{1,0},{2,3},{3,2},{4,5},{5,4},{6,7},{7,6},{8,9},{9,8},{10,11... | collective-permute-start | bytes 1572872 | tf_op jit(solution)/shard_map/ppermute | solution.py:117
  56.3 9.1 %collective-permute-start.13 = (bf16[2,2,2,32,384]{4,3,1,0,2:T(8,128)(2,1)S(1)}, bf16[2,2,2,32,384]{4,3,1,0,2:T(8,128)(2,1)S(1)}, u32[]{:S(2)}, u32[]{:S(2)}) collective-permute-start(bf16[2,2,2,32,384]{4,3,1,0,2:T(8,128)(2,1)S(1)} %get-tuple-element.79), channel_id=1, source_target_pairs={{0,8},{8,0},{16,24},{24,16},{1,9},{9,1},{17,25},{25,17},{2,10},{10... | collective-permute-start | bytes 589832 | tf_op jit(solution)/shard_map/ppermute | solution.py:117
  57.6 7.0 %collective-permute-start.15 = (bf16[2,2,2,32,384]{4,3,1,0,2:T(8,128)(2,1)S(1)}, bf16[2,2,2,32,384]{4,3,1,0,2:T(8,128)(2,1)S(1)}, u32[]{:S(2)}, u32[]{:S(2)}) collective-permute-start(bf16[2,2,2,32,384]{4,3,1,0,2:T(8,128)(2,1)S(1)} %get-tuple-element.78), channel_id=1, source_target_pairs={{0,16},{8,24},{16,0},{24,8},{1,17},{9,25},{17,1},{25,9},{2,18},{10... | collective-permute-start | bytes 589832 | tf_op jit(solution)/shard_map/ppermute | solution.py:117
  59.2 23.5 %collective-permute-start.10 = (bf16[256,1024]{1,0:T(8,128)(2,1)S(1)}, bf16[256,1024]{1,0:T(8,128)(2,1)S(1)}, u32[]{:S(2)}, u32[]{:S(2)}) collective-permute-start(bf16[256,1024]{1,0:T(8,128)(2,1)S(1)} %fusion.50), channel_id=1, source_target_pairs={{0,4},{4,0},{1,5},{5,1},{2,6},{6,2},{3,7},{7,3},{8,12},{12,8},{9,1... | collective-permute-start | bytes 1572872 | tf_op jit(solution)/shard_map/ppermute | solution.py:117
  64.7 16.7 %collective-permute-start.16 = (bf16[2,2,2,2,32,384]{5,4,2,1,3,0:T(8,128)(2,1)S(1)}, bf16[2,2,2,2,32,384]{5,4,2,1,3,0:T(8,128)(2,1)S(1)}, u32[]{:S(2)}, u32[]{:S(2)}) collective-permute-start(bf16[2,2,2,2,32,384]{5,4,2,1,3,0:T(8,128)(2,1)S(1)} %maximum_select_fusion.8), channel_id=1, source_target_pairs={{0,8},{8,0},{16,24},{24,16},{1,9},{9,1},{17,25},{25,17},{2,10},{10... | collective-permute-start | bytes 1179656 | tf_op jit(solution)/shard_map/ppermute | solution.py:117
  65.4 17.1 %collective-permute-start.14 = (bf16[2,2,2,2,32,384]{5,4,2,1,3,0:T(8,128)(2,1)S(1)}, bf16[2,2,2,2,32,384]{5,4,2,1,3,0:T(8,128)(2,1)S(1)}, u32[]{:S(2)}, u32[]{:S(2)}) collective-permute-start(bf16[2,2,2,2,32,384]{5,4,2,1,3,0:T(8,128)(2,1)S(1)} %maximum_select_fusion.6), channel_id=1, source_target_pairs={{0,16},{8,24},{16,0},{24,8},{1,17},{9,25},{17,1},{25,9},{2,18},{10... | collective-permute-start | bytes 1179656 | tf_op jit(solution)/shard_map/ppermute | solution.py:117
  74.4 8.3 %collective-permute-start.12 = (bf16[256,1024]{1,0:T(8,128)(2,1)S(1)}, bf16[256,1024]{1,0:T(8,128)(2,1)S(1)}, u32[]{:S(2)}, u32[]{:S(2)}) collective-permute-start(bf16[256,1024]{1,0:T(8,128)(2,1)S(1)} %collective-permute-done.11), channel_id=1, source_target_pairs={{0,4},{4,0},{1,5},{5,1},{2,6},{6,2},{3,7},{7,3},{8,12},{12,8},{9,1... | collective-permute-start | bytes 1572872 | tf_op jit(solution)/shard_map/ppermute | solution.py:117
  131.8 8.2 %collective-permute-start.19 = (bf16[4,32,1024]{2,1,0:T(8,128)(2,1)}, bf16[4,32,1024]{2,1,0:T(8,128)(2,1)}, u32[]{:S(2)}, u32[]{:S(2)}) collective-permute-start(bf16[4,32,1024]{2,1,0:T(8,128)(2,1)} %get-tuple-element.71), channel_id=1, source_target_pairs={{0,1},{1,0},{2,3},{3,2},{4,5},{5,4},{6,7},{7,6},{8,9},{9,8},{10,11... | collective-permute-start | bytes 786440 | tf_op jit(solution)/shard_map/ppermute | solution.py:117
  142.1 2.7 collective-permute-start.20
  142.2 3.5 collective-permute-start.28
  145.4 19.7 %collective-permute-start.21 = (bf16[256,1024]{1,0:T(8,128)(2,1)S(1)}, bf16[256,1024]{1,0:T(8,128)(2,1)S(1)}, u32[]{:S(2)}, u32[]{:S(2)}) collective-permute-start(bf16[256,1024]{1,0:T(8,128)(2,1)S(1)} %fusion.78), channel_id=1, source_target_pairs={{0,1},{1,0},{2,3},{3,2},{4,5},{5,4},{6,7},{7,6},{8,9},{9,8},{10,11... | collective-permute-start | bytes 1572872 | tf_op jit(solution)/shard_map/ppermute | solution.py:117
  166.0 14.9 %collective-permute-start.23 = (bf16[256,1024]{1,0:T(8,128)(2,1)S(1)}, bf16[256,1024]{1,0:T(8,128)(2,1)S(1)}, u32[]{:S(2)}, u32[]{:S(2)}) collective-permute-start(bf16[256,1024]{1,0:T(8,128)(2,1)S(1)} %multiply_convert_fusion.5), channel_id=1, source_target_pairs={{0,1},{1,0},{2,3},{3,2},{4,5},{5,4},{6,7},{7,6},{8,9},{9,8},{10,11... | collective-permute-start | bytes 1572872 | tf_op jit(solution)/shard_map/ppermute | solution.py:117
  166.1 24.5 %collective-permute-start.30 = (bf16[256,1024]{1,0:T(8,128)(2,1)S(1)}, bf16[256,1024]{1,0:T(8,128)(2,1)S(1)}, u32[]{:S(2)}, u32[]{:S(2)}) collective-permute-start(bf16[256,1024]{1,0:T(8,128)(2,1)S(1)} %get-tuple-element.112), channel_id=1, source_target_pairs={{0,1},{1,0},{2,3},{3,2},{4,5},{5,4},{6,7},{7,6},{8,9},{9,8},{10,11... | collective-permute-start | bytes 1572872 | tf_op jit(solution)/shard_map/ppermute | solution.py:117
  168.1 22.5 %collective-permute-start.22 = (bf16[256,1024]{1,0:T(8,128)(2,1)S(1)}, bf16[256,1024]{1,0:T(8,128)(2,1)S(1)}, u32[]{:S(2)}, u32[]{:S(2)}) collective-permute-start(bf16[256,1024]{1,0:T(8,128)(2,1)S(1)} %multiply_convert_fusion.5), channel_id=1, source_target_pairs={{0,4},{4,0},{1,5},{5,1},{2,6},{6,2},{3,7},{7,3},{8,12},{12,8},{9,1... | collective-permute-start | bytes 1572872 | tf_op jit(solution)/shard_map/ppermute | solution.py:117
  180.8 9.8 %collective-permute-start.24 = (bf16[256,1024]{1,0:T(8,128)(2,1)S(1)}, bf16[256,1024]{1,0:T(8,128)(2,1)S(1)}, u32[]{:S(2)}, u32[]{:S(2)}) collective-permute-start(bf16[256,1024]{1,0:T(8,128)(2,1)S(1)} %collective-permute-done.23), channel_id=1, source_target_pairs={{0,4},{4,0},{1,5},{5,1},{2,6},{6,2},{3,7},{7,3},{8,12},{12,8},{9,1... | collective-permute-start | bytes 1572872 | tf_op jit(solution)/shard_map/ppermute | solution.py:117
  181.6 12.5 %collective-permute-start.29 = (bf16[256,1024]{1,0:T(8,128)(2,1)S(1)}, bf16[256,1024]{1,0:T(8,128)(2,1)S(1)}, u32[]{:S(2)}, u32[]{:S(2)}) collective-permute-start(bf16[256,1024]{1,0:T(8,128)(2,1)S(1)} %get-tuple-element.112), channel_id=1, source_target_pairs={{0,4},{4,0},{1,5},{5,1},{2,6},{6,2},{3,7},{7,3},{8,12},{12,8},{9,1... | collective-permute-start | bytes 1572872 | tf_op jit(solution)/shard_map/ppermute | solution.py:117
  190.6 3.6 collective-permute-start.31
  199.1 3.2 collective-permute-start.32
  202.2 2.7 collective-permute-start.25
  202.8 14.9 %collective-permute-start.33 = (bf16[256,1024]{1,0:T(8,128)(2,1)S(1)}, bf16[256,1024]{1,0:T(8,128)(2,1)S(1)}, u32[]{:S(2)}, u32[]{:S(2)}) collective-permute-start(bf16[256,1024]{1,0:T(8,128)(2,1)S(1)} %fusion.80), channel_id=1, source_target_pairs={{0,1},{1,0},{2,3},{3,2},{4,5},{5,4},{6,7},{7,6},{8,9},{9,8},{10,11... | collective-permute-start | bytes 1572872 | tf_op jit(solution)/shard_map/ppermute | solution.py:117
  205.5 22.9 %collective-permute-start.26 = (bf16[256,1024]{1,0:T(8,128)(2,1)S(1)}, bf16[256,1024]{1,0:T(8,128)(2,1)S(1)}, u32[]{:S(2)}, u32[]{:S(2)}) collective-permute-start(bf16[256,1024]{1,0:T(8,128)(2,1)S(1)} %fusion.79), channel_id=1, source_target_pairs={{0,1},{1,0},{2,3},{3,2},{4,5},{5,4},{6,7},{7,6},{8,9},{9,8},{10,11... | collective-permute-start | bytes 1572872 | tf_op jit(solution)/shard_map/ppermute | solution.py:117
  230.3 13.8 %collective-permute-start.35 = (bf16[256,1024]{1,0:T(8,128)(2,1)}, bf16[256,1024]{1,0:T(8,128)(2,1)}, u32[]{:S(2)}, u32[]{:S(2)}) collective-permute-start(bf16[256,1024]{1,0:T(8,128)(2,1)} %get-tuple-element.37), channel_id=1, source_target_pairs={{0,1},{1,0},{2,3},{3,2},{4,5},{5,4},{6,7},{7,6},{8,9},{9,8},{10,11... | collective-permute-start | bytes 1572872 | tf_op jit(solution)/shard_map/ppermute | solution.py:117
  230.6 13.5 %collective-permute-start.34 = (bf16[256,1024]{1,0:T(8,128)(2,1)}, bf16[256,1024]{1,0:T(8,128)(2,1)}, u32[]{:S(2)}, u32[]{:S(2)}) collective-permute-start(bf16[256,1024]{1,0:T(8,128)(2,1)} %get-tuple-element.37), channel_id=1, source_target_pairs={{0,4},{4,0},{1,5},{5,1},{2,6},{6,2},{3,7},{7,3},{8,12},{12,8},{9,1... | collective-permute-start | bytes 1572872 | tf_op jit(solution)/shard_map/ppermute | solution.py:117
  244.1 2.3 collective-permute-start.36
  248.8 8.4 %collective-permute-start.53 = (bf16[4,32,1024]{2,1,0:T(8,128)(2,1)S(1)}, bf16[4,32,1024]{2,1,0:T(8,128)(2,1)S(1)}, u32[]{:S(2)}, u32[]{:S(2)}) collective-permute-start(bf16[4,32,1024]{2,1,0:T(8,128)(2,1)S(1)} %get-tuple-element.67), channel_id=1, source_target_pairs={{0,1},{1,0},{2,3},{3,2},{4,5},{5,4},{6,7},{7,6},{8,9},{9,8},{10,11... | collective-permute-start | bytes 786440 | tf_op jit(solution)/shard_map/ppermute | solution.py:117
  258.1 136.3 %all-reduce.4.cloned.1.call-start = ((), (), s32[]{:S(2)}) async-start(), calls=%async_computation.2 | async-start | bytes 8388608
  267.8 82.5 %collective-permute-start.27 = (bf16[256,1024]{1,0:T(8,128)(2,1)S(1)}, bf16[256,1024]{1,0:T(8,128)(2,1)}, u32[]{:S(2)}, u32[]{:S(2)}) collective-permute-start(bf16[256,1024]{1,0:T(8,128)(2,1)S(1)} %get-tuple-element.61), channel_id=1, source_target_pairs={{2,4},{4,2},{3,5},{5,3},{10,12},{12,10},{11,13},{13,11},{18,20},{2... | collective-permute-start | bytes 1572872 | tf_op jit(solution)/shard_map/ppermute | solution.py:161
  314.0 13.2 %collective-permute-start.48 = (bf16[2,2,2,2,32,384]{5,4,3,2,1,0:T(8,128)(2,1)S(1)}, bf16[2,2,2,2,32,384]{5,4,3,2,1,0:T(8,128)(2,1)S(1)}, u32[]{:S(2)}, u32[]{:S(2)}) collective-permute-start(bf16[2,2,2,2,32,384]{5,4,3,2,1,0:T(8,128)(2,1)S(1)} %dynamic-slice_bitcast_fusion), channel_id=1, source_target_pairs={{0,16},{8,24},{16,0},{24,8},{1,17},{9,25},{17,1},{25,9},{2,18},{10... | collective-permute-start | bytes 1179656 | tf_op jit(solution)/shard_map/ppermute | solution.py:117
  316.2 15.0 %collective-permute-start.45 = (bf16[2,2,2,2,32,384]{5,4,3,1,2,0:T(8,128)(2,1)S(1)}, bf16[2,2,2,2,32,384]{5,4,3,1,2,0:T(8,128)(2,1)S(1)}, u32[]{:S(2)}, u32[]{:S(2)}) collective-permute-start(bf16[2,2,2,2,32,384]{5,4,3,1,2,0:T(8,128)(2,1)S(1)} %bitcast.385), channel_id=1, source_target_pairs={{0,8},{8,0},{16,24},{24,16},{1,9},{9,1},{17,25},{25,17},{2,10},{10... | collective-permute-start | bytes 1179656 | tf_op jit(solution)/shard_map/ppermute | solution.py:117
  318.8 38.0 %collective-permute-start.37 = (bf16[2,256,1024]{2,1,0:T(8,128)(2,1)}, bf16[2,256,1024]{2,1,0:T(8,128)(2,1)}, u32[]{:S(2)}, u32[]{:S(2)}) collective-permute-start(bf16[2,256,1024]{2,1,0:T(8,128)(2,1)} %fusion.62), channel_id=1, source_target_pairs={{0,4},{4,0},{1,5},{5,1},{2,6},{6,2},{3,7},{7,3},{8,12},{12,8},{9,1... | collective-permute-start | bytes 3145736 | tf_op jit(solution)/shard_map/ppermute | solution.py:117
  327.4 11.3 %collective-permute-start.49 = (bf16[2,2,2,32,384]{4,3,2,1,0:T(8,128)(2,1)S(1)}, bf16[2,2,2,32,384]{4,3,2,1,0:T(8,128)(2,1)S(1)}, u32[]{:S(2)}, u32[]{:S(2)}) collective-permute-start(bf16[2,2,2,32,384]{4,3,2,1,0:T(8,128)(2,1)S(1)} %dynamic-slice_bitcast_fusion.4), channel_id=1, source_target_pairs={{0,8},{8,0},{16,24},{24,16},{1,9},{9,1},{17,25},{25,17},{2,10},{10... | collective-permute-start | bytes 589832 | tf_op jit(solution)/shard_map/ppermute | solution.py:117
  331.3 9.8 %collective-permute-start.46 = (bf16[2,2,2,32,384]{4,3,2,0,1:T(8,128)(2,1)S(1)}, bf16[2,2,2,32,384]{4,3,2,0,1:T(8,128)(2,1)S(1)}, u32[]{:S(2)}, u32[]{:S(2)}) collective-permute-start(bf16[2,2,2,32,384]{4,3,2,0,1:T(8,128)(2,1)S(1)} %dynamic-slice_bitcast_fusion.5), channel_id=1, source_target_pairs={{0,16},{8,24},{16,0},{24,8},{1,17},{9,25},{17,1},{25,9},{2,18},{10... | collective-permute-start | bytes 589832 | tf_op jit(solution)/shard_map/ppermute | solution.py:117
  338.8 9.0 %collective-permute-start.50 = (bf16[2,2,32,384]{3,2,1,0:T(8,128)(2,1)S(1)}, bf16[2,2,32,384]{3,2,1,0:T(8,128)(2,1)S(1)}, u32[]{:S(2)}, u32[]{:S(2)}) collective-permute-start(bf16[2,2,32,384]{3,2,1,0:T(8,128)(2,1)S(1)} %dynamic-slice_bitcast_fusion.15), channel_id=1, source_target_pairs={{0,2},{2,0},{1,3},{3,1},{4,6},{6,4},{5,7},{7,5},{8,10},{10,8},{9,1... | collective-permute-start | bytes 294920 | tf_op jit(solution)/shard_map/ppermute | solution.py:117
  341.2 7.6 %collective-permute-start.47 = (bf16[2,2,32,384]{3,2,1,0:T(8,128)(2,1)S(1)}, bf16[2,2,32,384]{3,2,1,0:T(8,128)(2,1)S(1)}, u32[]{:S(2)}, u32[]{:S(2)}) collective-permute-start(bf16[2,2,32,384]{3,2,1,0:T(8,128)(2,1)S(1)} %dynamic-slice_bitcast_fusion.16), channel_id=1, source_target_pairs={{0,2},{2,0},{1,3},{3,1},{4,6},{6,4},{5,7},{7,5},{8,10},{10,8},{9,1... | collective-permute-start | bytes 294920 | tf_op jit(solution)/shard_map/ppermute | solution.py:117
  348.8 1.4 collective-permute-start.51
  350.3 4.9 %collective-permute-start.52 = (bf16[2,32,768]{2,1,0:T(8,128)(2,1)S(1)}, bf16[2,32,768]{2,1,0:T(8,128)(2,1)S(1)}, u32[]{:S(2)}, u32[]{:S(2)}) collective-permute-start(bf16[2,32,768]{2,1,0:T(8,128)(2,1)S(1)} %get-tuple-element.93), channel_id=1, source_target_pairs={{0,1},{1,0},{2,3},{3,2},{4,5},{5,4},{6,7},{7,6},{8,9},{9,8},{10,11... | collective-permute-start | bytes 294920 | tf_op jit(solution)/shard_map/ppermute | solution.py:117
  356.8 39.8 %copy-start.25 = (f32[1024]{0:T(1024)S(1)}, f32[1024]{0:T(1024)}, u32[]{:S(2)}) copy-start(f32[1024]{0:T(1024)} %copy-done.24) | copy-start | bytes 12292
  356.8 39.8 %copy-start.29 = (f32[256]{0:T(256)S(1)}, f32[256]{0:T(256)}, u32[]{:S(2)}) copy-start(f32[256]{0:T(256)} %copy-done.28) | copy-start | bytes 3076
  356.8 39.8 %copy-start.31 = (f32[256]{0:T(256)S(1)}, f32[256]{0:T(256)}, u32[]{:S(2)}) copy-start(f32[256]{0:T(256)} %copy-done.30) | copy-start | bytes 3076
  359.9 36.7 %collective-permute-start.38 = (bf16[256,1024]{1,0:T(8,128)(2,1)}, bf16[256,1024]{1,0:T(8,128)(2,1)S(1)}, u32[]{:S(2)}, u32[]{:S(2)}) collective-permute-start(bf16[256,1024]{1,0:T(8,128)(2,1)} %fusion.81), channel_id=1, source_target_pairs={{0,1},{1,0},{2,3},{3,2},{4,5},{5,4},{6,7},{7,6},{8,9},{9,8},{10,11... | collective-permute-start | bytes 1572872 | tf_op jit(solution)/shard_map/ppermute | solution.py:117
  361.1 11.8 %collective-permute-start.54 = (bf16[32,1024]{1,0:T(8,128)(2,1)S(1)}, bf16[32,1024]{1,0:T(8,128)(2,1)S(1)}, u32[]{:S(2)}, u32[]{:S(2)}) collective-permute-start(bf16[32,1024]{1,0:T(8,128)(2,1)S(1)} %dynamic-slice_bitcast_fusion.21), channel_id=1, source_target_pairs={{0,2},{2,0},{1,3},{3,1},{4,6},{6,4},{5,7},{7,5},{8,10},{10,8},{9,1... | collective-permute-start | bytes 196616 | tf_op jit(solution)/shard_map/ppermute | solution.py:117
  397.2 2.6 collective-permute-start.40
  397.3 34.0 %collective-permute-start.55 = (bf16[256,1024]{1,0:T(8,128)(2,1)S(1)}, bf16[256,1024]{1,0:T(8,128)(2,1)S(1)}, u32[]{:S(2)}, u32[]{:S(2)}) collective-permute-start(bf16[256,1024]{1,0:T(8,128)(2,1)S(1)} %fusion.83), channel_id=1, source_target_pairs={{0,2},{2,0},{1,3},{3,1},{4,6},{6,4},{5,7},{7,5},{8,10},{10,8},{9,1... | collective-permute-start | bytes 1572872 | tf_op jit(solution)/shard_map/ppermute | solution.py:117
  399.8 12.0 %collective-permute-start.41 = (f32[1,2048]{1,0:T(1,128)S(1)}, f32[1,2048]{1,0:T(1,128)S(1)}, u32[]{:S(2)}, u32[]{:S(2)}) collective-permute-start(f32[1,2048]{1,0:T(1,128)S(1)} %fusion.137), channel_id=1, source_target_pairs={{0,1},{1,0},{2,3},{3,2},{4,5},{5,4},{6,7},{7,6},{8,9},{9,8},{10,11... | collective-permute-start | bytes 24584 | tf_op jit(solution)/shard_map/ppermute | solution.py:117
  411.9 12.3 %collective-permute-start.42 = (f32[1,2048]{1,0:T(1,128)S(1)}, f32[1,2048]{1,0:T(1,128)S(1)}, u32[]{:S(2)}, u32[]{:S(2)}) collective-permute-start(f32[1,2048]{1,0:T(1,128)S(1)} %add.361), channel_id=1, source_target_pairs={{0,2},{2,0},{1,3},{3,1},{4,6},{6,4},{5,7},{7,5},{8,10},{10,8},{9,1... | collective-permute-start | bytes 24584 | tf_op jit(solution)/shard_map/ppermute | solution.py:117
  424.7 5.1 %collective-permute-start.43 = (f32[2,8,2048]{2,1,0:T(8,128)S(1)}, f32[2,8,2048]{2,1,0:T(8,128)S(1)}, u32[]{:S(2)}, u32[]{:S(2)}) collective-permute-start(f32[2,8,2048]{2,1,0:T(8,128)S(1)} %dynamic-slice_bitcast_fusion.9), channel_id=1, source_target_pairs={{0,16},{8,24},{16,0},{24,8},{1,17},{9,25},{17,1},{25,9},{2,18},{10... | collective-permute-start | bytes 393224 | tf_op jit(solution)/shard_map/ppermute | solution.py:117
  426.6 10.1 %collective-permute-start.39 = (bf16[256,1024]{1,0:T(8,128)(2,1)S(1)}, bf16[256,1024]{1,0:T(8,128)(2,1)S(1)}, u32[]{:S(2)}, u32[]{:S(2)}) collective-permute-start(bf16[256,1024]{1,0:T(8,128)(2,1)S(1)} %fusion.55), channel_id=1, source_target_pairs={{2,4},{4,2},{3,5},{5,3},{10,12},{12,10},{11,13},{13,11},{18,20},{2... | collective-permute-start | bytes 1572872 | tf_op jit(solution)/shard_map/ppermute | solution.py:161
  429.8 4.3 collective-permute-start.44
  431.6 4.0 collective-permute-start.56
  435.7 9.4 %collective-permute-start.57 = (bf16[2,32,1024]{2,1,0:T(8,128)(2,1)S(1)}, bf16[2,32,1024]{2,1,0:T(8,128)(2,1)S(1)}, u32[]{:S(2)}, u32[]{:S(2)}) collective-permute-start(bf16[2,32,1024]{2,1,0:T(8,128)(2,1)S(1)} %get-tuple-element.81), channel_id=1, source_target_pairs={{0,1},{1,0},{2,3},{3,2},{4,5},{5,4},{6,7},{7,6},{8,9},{9,8},{10,11... | collective-permute-start | bytes 393224 | tf_op jit(solution)/shard_map/ppermute | solution.py:117
  (60 other events, 689.3 us)
Sparse Core Ops, SparseCore 0:
  43.3 86.5 all-gather.2
  258.2 24.0 reduce-scatter.3
  285.6 108.7 all-reduce.3
where the time goes:
time: 464 us; the launch traced here: 455 us
  waiting for transfers between devices  260 us (56%)
  matrix products  66.6 us (14%)
  starting transfers between devices  47.6 us (10%)
  other arithmetic  43.9 us (9%)
  local copies, waits for them, and re-layouts  19.6 us (4%)
  between operations  17.4 us (4%)
    ppermute x54, waiting for transfers between devices, swap(): return lax.ppermute(x, axis, [(i, i ^ mask) for i in range(size)])  207 us
    ppermute x54, starting transfers between devices, swap(): return lax.ppermute(x, axis, [(i, i ^ mask) for i in range(size)])  43.6 us
    all_gather x1, waiting for transfers between devices, per_device(): packs = lax.all_gather(jnp.concatenate(packs), ('plane', 'group'), axis=0)  32.6 us
    unnamed x5, waiting for transfers between devices  20.1 us
    dot_general x2, matrix products, attend_backward(): jnp.einsum('qhd,khd->hqk', d_block, value, preferred_element_type=f32)  17.8 us
    dot_general x4, matrix products, dot_left_t(): lax.dot_general(left, right, (((0,), (0,)), ((), ())), preferred_element_...  11.4 us
  transfers between devices with their start and end apart: 61, of which 39 were waited for; matrix products, arithmetic and copies ran while one was open for 23% of the time, Pallas kernels for 0%

commit v1 on v0

--- a/solution.py
+++ b/solution.py
@@ -161,7 +161,7 @@
             return jnp.where(stays, x, lax.ppermute(x, ("core", "group"), [(1, 2), (2, 1)]))
 
         def after(x, first):
-            return lax.optimization_barrier((x, first))[0]
+            return lax.optimization_barrier((x, first))
 
         def gather(x, labels, axes):
             for axis in axes:
@@ -224,7 +224,7 @@
 
         def quad(parts):
             x = exchange(parts, "c")
-            return exchange(x.transpose(1, 0, 2, 3), "t")
+            return exchange(x.transpose(1, 0, 2, 3), "t"), x
 
         def quad_back(x):
             x = exchange(x, "c")
@@ -261,9 +261,10 @@
 
         qkv_scaled = (qkv_weight.astype(f32) * gain_attn.astype(f32)[:, None]).astype(bf16)
         in_scaled = (in_weight.astype(f32) * gain_mlp.astype(f32)[:, None]).astype(bf16)
-        qkv_quad = quad(qkv_split(qkv_scaled))
+        qkv_quad, _ = quad(qkv_split(qkv_scaled))
+        time_rows, qkv_quad = after(time_weight, qkv_quad)
         w_qkv, labels = gather(qkv_quad, ["t", "c"], ["g"])
-        gate = w_qkv
+        later, w_qkv = after(cotangent[0], w_qkv)
         cut = 3 * head_cols // 2
         w_qkv = jnp.concatenate(
             [
@@ -272,7 +273,7 @@
             ],
             axis=1,
         )
-        in_quad = quad(in_split(after(in_scaled, qkv_quad)))
+        in_quad, _ = quad(in_split(in_scaled))
         rows_in = 4 * in_weight.shape[0]
         packs = [in_quad.reshape(rows_in, width), down_weight] + ([out_weight] if aligned else [])
         packs = lax.all_gather(jnp.concatenate(packs), ("plane", "group"), axis=0)
@@ -287,8 +288,8 @@
                 in_order(w_out, labels), (2 * core + side) * head_cols, head_cols, 0
             )
 
-        t_rows, labels = gather(after(time_weight, qkv_quad), [], forwards[:1])
-        t_rows = in_order(*gather(after(t_rows, gate), labels, forwards[1:]))
+        t_rows, labels = gather(time_rows, [], forwards[:1])
+        t_rows = in_order(*gather(t_rows, labels, forwards[1:]))
         embed_rows = pick(
             pick(embed_both.reshape(2, planes, 2, head_size, -1), core, 2), 2 * group + side, 2
         ).reshape(2, -1)
@@ -322,7 +323,10 @@
             return x[0] + send(x[1].astype(bf16), "t").astype(f32)
 
         inputs = moved(tokens[0]).astype(f32)
-        upstream = moved(after(cotangent[0], gate)).astype(f32)
+        w_qkv, upstream = after(w_qkv, moved(later))
+        upstream = upstream.astype(f32)
+        all_d = gather_four((valid * upstream).astype(bf16))
+        w_out, all_d = after(w_out, all_d)
         white_a, inv_a = whiten(inputs)
         all_a = gather_four((white_a * scale_attn).astype(bf16))
         packed = dot(all_a, w_qkv)
@@ -342,18 +346,16 @@
         activation = (upper * phi).astype(bf16)
         slope = phi + upper * jnp.exp(-0.5 * upper * upper) / math.sqrt(2.0 * math.pi)
         activation, slope = lax.optimization_barrier((activation, slope))
-        output = hidden + valid * sum_four(dot(activation, w_down))
-        output = moved(output.astype(bf16))[None]
-
-        all_d = gather_four((valid * upstream).astype(bf16))
+        mlp_part = dot(activation, w_down).astype(bf16)
+
         d_upper = (dot_right_t(all_d, w_down) * slope).astype(bf16)
         down_axes = [axis for axis in natural if axis not in ("c", "t")]
         grad_down = dot_left_t(activation, all_d).astype(bf16).reshape(planes, 2 * ff_rows, width)
         d_normed_m = sum_four(dot_right_t(d_upper, w_in))
         grad_in = dot_left_t(all_m, d_upper).astype(bf16).reshape(planes, 2 * rows_in, width)
-        both = lax.psum_scatter(
-            jnp.concatenate([grad_in, grad_down], axis=1), "plane", scatter_dimension=0, tiled=True
-        )[0]
+        sum_d = lax.psum_scatter(grad_down, "plane", scatter_dimension=0, tiled=True)[0]
+        sum_i = lax.psum_scatter(grad_in, "plane", scatter_dimension=0, tiled=True)[0]
+        both = jnp.concatenate([sum_i, sum_d])
         both_in = both[: 2 * rows_in].reshape(2, 2, 2, -1, width).transpose(1, 0, 2, 3, 4)
         both = jnp.concatenate(
             [both_in.reshape(2, rows_in, width), both[2 * rows_in :].reshape(2, ff_rows, width)],
@@ -365,11 +367,12 @@
         d_from_m, d_scale_m = whiten_back(d_normed_m, white_m, inv_m, scale_mlp)
         d_hidden = upstream + d_from_m
         all_da = gather_four((valid * d_hidden).astype(bf16))
+        all_da, mlp_part = after(all_da, mlp_part)
         grad_out = dot_left_t(mixed, all_da).astype(bf16)
+        output = hidden + valid * sum_four(mlp_part.astype(f32))
+        output = moved(output.astype(bf16))[None]
         if aligned:
-            out_rows = out_pieces(grad_out).reshape(planes, -1, width)
-            out_rows = lax.psum_scatter(out_rows, "plane", scatter_dimension=0, tiled=True)
-            sum_out = reduce_rows(out_rows[0], ["g"], ["g"])
+            sum_out = reduce_rows(out_pieces(grad_out), down_axes, forwards + ("g",))
         else:
             padded = lax.dynamic_update_slice_in_dim(
                 jnp.zeros((width, width), bf16), grad_out, (2 * core + side) * head_cols, 0
@@ -389,7 +392,12 @@
             ],
             axis=1,
         )
-        grad_qkv = dot_left_t(all_a, d_packed)
+        grad_qkv = dot_left_t(all_a, d_packed).astype(bf16)
+        part = dot_right_t(d_packed, w_qkv).reshape(2, 2, span, width)
+        from_core = send(part[:, 1].astype(bf16), "c")
+        from_core, grad_qkv = after(from_core, grad_qkv)
+        part = part[:, 0] + from_core.astype(f32)
+        d_normed_a = part[0] + send(part[1].astype(bf16), "t").astype(f32)
         qkv_sums = jnp.concatenate(
             [
                 reduce_rows(grad_qkv[:, :cut], natural, forwards + ("g",)),
@@ -397,7 +405,6 @@
             ],
             axis=-1,
         )
-        d_normed_a = sum_four(dot_right_t(d_packed, w_qkv))
         d_from_a, d_scale_a = whiten_back(d_normed_a, white_a, inv_a, scale_attn)
         grad_tokens = moved((d_hidden + d_from_a).astype(bf16))[None]
 

time: 464 us -> 418 us (0.901); the launches traced: 455 us -> 414 us
  waiting for transfers between devices: 260 us -> 192 us
  other arithmetic: 43.9 us -> 56.9 us
  starting transfers between devices: 47.6 us -> 54.7 us
  matrix products: 66.6 us -> 73.3 us
    ppermute x54 -> x56, waiting for transfers between devices: 207 us -> 166 us  [swap(): return lax.ppermute(x, axis, [(i, i ^ mask) for i in range(size)])]
    unnamed x5, waiting for transfers between devices: 20.1 us -> 0.07 us
    dot_general x4, matrix products: 8.37 us -> 17.4 us  [dot(): return jnp.dot(left, right, preferred_element_type=f32)]
    ppermute x54 -> x56, starting transfers between devices: 43.6 us -> 50.5 us  [swap(): return lax.ppermute(x, axis, [(i, i ^ mask) for i in range(size)])]
    all_gather x1, waiting for transfers between devices: 32.6 us -> 26.3 us  [per_device(): packs = lax.all_gather(jnp.concatenate(packs), ('plane', 'group'), axis=0)]
  transfers between devices with their start and end apart: 61 -> 63, of which waited for: 39 -> 38; matrix products, arithmetic and copies ran while one was open for 23% -> 30% of each run, Pallas kernels for 0% -> 0%
where the time goes in v1:
time: 418 us; the launch traced here: 414 us
  waiting for transfers between devices  192 us (46%)
  matrix products  73.3 us (18%)
  other arithmetic  56.9 us (14%)
  starting transfers between devices  54.7 us (13%)
  local copies, waits for them, and re-layouts  19.9 us (5%)
  between operations  17.1 us (4%)
    ppermute x56, waiting for transfers between devices, swap(): return lax.ppermute(x, axis, [(i, i ^ mask) for i in range(size)])  166 us
    ppermute x56, starting transfers between devices, swap(): return lax.ppermute(x, axis, [(i, i ^ mask) for i in range(size)])  50.5 us
    all_gather x1, waiting for transfers between devices, per_device(): packs = lax.all_gather(jnp.concatenate(packs), ('plane', 'group'), axis=0)  26.3 us
    dot_general x4, matrix products, dot(): return jnp.dot(left, right, preferred_element_type=f32)  17.4 us
    dot_general x2, matrix products, attend_backward(): jnp.einsum('qhd,khd->hqk', d_block, value, preferred_element_type=f32)  15.8 us
    dot_general x4, matrix products, dot_left_t(): lax.dot_general(left, right, (((0,), (0,)), ((), ())), preferred_element_...  11.3 us
    dot_general x4, matrix products, dot_right_t(): lax.dot_general(left, right, (((1,), (1,)), ((), ())), preferred_element_...  9.56 us
    convert_element_type x1, other arithmetic, attend_backward(): d_scores = (probs * (d_probs - row_dot)).astype(bf16)  8.81 us
  transfers between devices with their start and end apart: 63, of which 38 were waited for; matrix products, arithmetic and copies ran while one was open for 30% of the time, Pallas kernels for 0%

profile of v1, /device:TPU:0, one launch (start us, length us, event | category | flops | bytes accessed | tf_op | source)
XLA Modules:
  0.0 414.3 jit_solution(10325018535478187905)
XLA Ops:
  18.3 2.7 collective-permute-start.3
  21.0 3.5 collective-permute-done.3
  26.1 2.2 collective-permute-start.19
  28.5 1.6 collective-permute-start.5
  30.1 2.7 collective-permute-done.5
  33.1 8.1 %collective-permute-start.6 = (f32[2048]{0:T(1024)S(1)}, f32[2048]{0:T(1024)S(1)}, u32[]{:S(2)}, u32[]{:S(2)}) collective-permute-start(f32[2048]{0:T(1024)S(1)} %bitcast.426), channel_id=1, source_target_pairs={{0,2},{2,0},{1,3},{3,1},{4,6},{6,4},{5,7},{7,5},{8,10},{10,8},{9,1... | collective-permute-start | bytes 24584 | tf_op jit(solution)/shard_map/ppermute | solution.py:117
  41.3 1.7 collective-permute-done.6
  43.2 3.4 collective-permute-done.7
  47.8 1.7 collective-permute-done.12
  50.7 1.6 collective-permute-start.15
  54.6 3.1 collective-permute-start.9
  60.5 11.1 %collective-permute-done.16 = bf16[2,2,2,2,32,384]{5,4,2,1,3,0:T(8,128)(2,1)S(1)} collective-permute-done((bf16[2,2,2,2,32,384]{5,4,2,1,3,0:T(8,128)(2,1)S(1)}, bf16[2,2,2,2,32,384]{5,4,2,1,3,0:T(8,128)(2,1)S(1)}, u32[]{:S(2)}, u32[]{:S(2)}) %collective-permute-start.16) | collective-permute-done | bytes 393248 | tf_op jit(solution)/shard_map/ppermute | solution.py:117
  74.3 2.0 collective-permute-start.22
  79.5 17.8 %collective-permute-done.22 = bf16[256,1024]{1,0:T(8,128)(2,1)} collective-permute-done((bf16[256,1024]{1,0:T(8,128)(2,1)}, bf16[256,1024]{1,0:T(8,128)(2,1)}, u32[]{:S(2)}, u32[]{:S(2)}) %collective-permute-start.22) | collective-permute-done | bytes 524320 | tf_op jit(solution)/shard_map/ppermute | solution.py:117
  97.3 3.8 fusion.91
  103.0 2.3 fusion.16
  105.3 4.3 %fusion = (f32[4,512]{1,0:T(4,128)S(1)}, f32[4,512]{1,0:T(4,128)S(1)}) fusion(f32[4,512]{1,0:T(4,128)S(1)} %get-tuple-element.47, f32[4,512,1024]{2,1,0:T(8,128)S(1)} %get-tuple-element.122, pred[1024]{0:T(1024)(128)(4,1)S(1)} %pad_add_fusion, f32[4,512]{1,0:T(4,128)S(1)} %get-tuple-element.48, f32[4,512,1024]{2,1,0:T(8,128)S(1)} %fusion.100), kind=kLoop, calls=%fused_computation.12 | loop fusion | flops 16773120 | bytes 16811008 | tf_op jit(solution)/shard_map/reduce_sum | solution.py:76
  109.7 2.5 fusion.46
  112.2 2.5 fusion.45
  114.7 26.3 %all-gather.3.cloned.1.call-done = bf16[2304,1024]{1,0:T(8,128)(2,1)} async-done(((bf16[288,1024]{1,0:T(8,128)(2,1)}), bf16[2304,1024]{1,0:T(8,128)(2,1)}) %all-gather.3.cloned.1.call-update) | async-done | bytes 4718608 | tf_op jit(solution)/shard_map/all_gather | solution.py:279
  143.3 1.7 pad_maximum_fusion.1
  145.0 6.0 %collective-permute-done.20 = bf16[4,32,1024]{2,1,0:T(8,128)(2,1)} collective-permute-done((bf16[4,32,1024]{2,1,0:T(8,128)(2,1)}, bf16[4,32,1024]{2,1,0:T(8,128)(2,1)}, u32[]{:S(2)}, u32[]{:S(2)}) %collective-permute-start.20) | collective-permute-done | bytes 262176 | tf_op jit(solution)/shard_map/ppermute | solution.py:117
  153.2 2.6 collective-permute-done.24
  156.8 13.7 %collective-permute-done.25 = bf16[256,1024]{1,0:T(8,128)(2,1)S(1)} collective-permute-done((bf16[256,1024]{1,0:T(8,128)(2,1)S(1)}, bf16[256,1024]{1,0:T(8,128)(2,1)S(1)}, u32[]{:S(2)}, u32[]{:S(2)}) %collective-permute-start.25) | collective-permute-done | bytes 524320 | tf_op jit(solution)/shard_map/ppermute | solution.py:117
  171.7 12.8 %collective-permute-done.27 = bf16[256,1024]{1,0:T(8,128)(2,1)S(1)} collective-permute-done((bf16[256,1024]{1,0:T(8,128)(2,1)S(1)}, bf16[256,1024]{1,0:T(8,128)(2,1)S(1)}, u32[]{:S(2)}, u32[]{:S(2)}) %collective-permute-start.27) | collective-permute-done | bytes 524320 | tf_op jit(solution)/shard_map/ppermute | solution.py:117
  186.4 6.9 %fusion.7 = (f32[1024,1024]{1,0:T(8,128)S(1)}, bf16[1024,1024]{1,0:T(8,128)(2,1)}) fusion(bf16[1024,1024]{1,0:T(8,128)(2,1)S(1)} %bitcast.366, bf16[256,1024]{1,0:T(8,128)(2,1)S(1)} %collective-permute-done.28, bf16[256,1024]{1,0:T(8,128)(2,1)S(1)} %collective-permute-done.27, bf16[256,1024]{1,0:T(8,128)(2,1)S(1)} %collective-permute-done.26, ...), kind=kOutput, calls=%fused_computation.20 | convolution fusion | flops 2166358016 | bytes 10485760 | tf_op jit(solution)/shard_map/dot_general | solution.py:18
  193.3 2.4 multiply_convert_fusion.2
  195.7 3.7 convolution_convert_fusion.1
  199.6 4.6 %fusion.21 = f32[2,2,256,1024]{3,2,0,1:T(8,128)S(1)} fusion(bf16[1024,1024,1,1]{1,0,2,3:T(8,128)(2,1)} %bitcast.367, bf16[2,2,256,1024]{3,2,1,0:T(8,128)(2,1)} %bitcast.427), kind=kOutput, calls=%fused_computation.46 | convolution fusion | flops 2147483648 | bytes 8388608 | tf_op jit(solution)/shard_map/dot_general | solution.py:22
  204.6 2.5 collective-permute-done.29
  207.1 1.7 fusion.19
  208.8 2.1 fusion.74
  211.9 13.3 %collective-permute-done.30 = bf16[256,1024]{1,0:T(8,128)(2,1)} collective-permute-done((bf16[256,1024]{1,0:T(8,128)(2,1)}, bf16[256,1024]{1,0:T(8,128)(2,1)}, u32[]{:S(2)}, u32[]{:S(2)}) %collective-permute-start.30) | collective-permute-done | bytes 524320 | tf_op jit(solution)/shard_map/ppermute | solution.py:117
  225.2 1.9 multiply_reduce_fusion.2
  227.2 3.0 multiply_convert_fusion.4
  230.5 3.8 convolution_convert_fusion
  234.4 9.4 %collective-permute-done.32 = bf16[256,1024]{1,0:T(8,128)(2,1)S(1)} collective-permute-done((bf16[256,1024]{1,0:T(8,128)(2,1)}, bf16[256,1024]{1,0:T(8,128)(2,1)S(1)}, u32[]{:S(2)}, u32[]{:S(2)}) %collective-permute-start.32) | collective-permute-done | bytes 524320 | tf_op jit(solution)/shard_map/ppermute | solution.py:117
  243.8 5.9 %convolution_convert_fusion.2 = bf16[1024,1024]{1,0:T(8,128)(2,1)} fusion(bf16[1024,1024]{1,0:T(8,128)(2,1)} %get-tuple-element.32, bf16[1024,1024]{1,0:T(8,128)(2,1)} %bitcast.375), kind=kOutput, calls=%fused_computation.50 | convolution fusion | flops 2148532224 | bytes 6291456 | tf_op jit(solution)/shard_map/dot_general | solution.py:18
  252.5 5.6 %fusion.144 = f32[4,512,1024]{2,1,0:T(8,128)} fusion(bf16[512,4,64]{0,2,1:T(8,128)(2,1)S(1)} %bitcast.380, bf16[1024,4,64]{0,2,1:T(8,128)(2,1)S(1)} %bitcast.345), kind=kOutput, calls=%fused_computation.339 | convolution fusion | flops 268435456 | bytes 9175040 | tf_op jit(solution)/shard_map/qhd,khd->hqk/dot_general | solution.py:99
  258.2 3.1 fusion.8
  261.5 10.3 %multiply_reduce_fusion = (f32[4,512]{1,0:T(4,128)}, f32[4,512]{1,0:T(4,128)}, f32[4,512,1024]{2,1,0:T(8,128)}) fusion(f32[4,512]{1,0:T(4,128)S(1)} %log_add_fusion, f32[4,512,1024]{2,1,0:T(8,128)S(1)} %bitcast.338, pred[1024]{0:T(1024)(128)(4,1)S(1)} %copy-done.54, f32[4,512,1024]{2,1,0:T(8,128)} %fusion.144, f32[4,512]{1,0:T(4,128)S(1)} %log_add_fusion.1, ...), kind=kOutput, calls=%fused_computation.1 | convolution fusion | flops 289402880 | bytes 34374656 | tf_op jit(solution)/shard_map/qhd,khd->hqk/dot_general | solution.py:99
  271.7 8.8 %multiply_convert_fusion = (bf16[4,512,1024]{2,1,0:T(8,128)(2,1)S(1)}, bf16[4,512,1024]{2,1,0:T(8,128)(2,1)S(1)}) fusion(f32[4,512,1024]{2,1,0:T(8,128)} %get-tuple-element.123, f32[4,512]{1,0:T(4,128)} %get-tuple-element.43, f32[4,512]{1,0:T(4,128)S(1)} %log_add_fusion, f32[4,512,1024]{2,1,0:T(8,128)S(1)} %bitcast.338, pred[1024]{0:T(1024)(128)(4,1)S(1)} %copy-done.54, ...), kind=kLoop, calls=%fused_computation | loop fusion | flops 25165824 | bytes 41976832 | tf_op jit(solution)/shard_map/convert_element_type | solution.py:101
  284.9 2.5 fusion.27
  290.5 2.6 collective-permute-done.53
  294.2 1.8 fusion.70
  296.1 4.9 %collective-permute-done.54 = bf16[2,2,32,1024]{3,2,1,0:T(8,128)(2,1)S(1)} collective-permute-done((bf16[2,2,32,1024]{3,2,1,0:T(8,128)(2,1)S(1)}, bf16[2,2,32,1024]{3,2,1,0:T(8,128)(2,1)S(1)}, u32[]{:S(2)}, u32[]{:S(2)}) %collective-permute-start.54) | collective-permute-done | bytes 262176 | tf_op jit(solution)/shard_map/ppermute | solution.py:117
  302.3 3.8 collective-permute-done.55
  307.1 3.1 convolution_convert_fusion.3
  310.2 1.7 collective-permute-done.56
  318.4 1.7 collective-permute-start.38
  320.0 2.4 collective-permute-done.48
  328.6 1.9 fusion.78
  330.5 3.1 collective-permute-start.57
  333.6 2.4 fusion.63
  337.5 4.5 %collective-permute-done.38 = bf16[256,1024]{1,0:T(8,128)(2,1)} collective-permute-done((bf16[256,1024]{1,0:T(8,128)(2,1)}, bf16[256,1024]{1,0:T(8,128)(2,1)}, u32[]{:S(2)}, u32[]{:S(2)}) %collective-permute-start.38) | collective-permute-done | bytes 524320 | tf_op jit(solution)/shard_map/ppermute | solution.py:117
  342.1 1.6 fusion.53
  345.0 4.1 collective-permute-done.41
  349.1 4.8 %collective-permute-start.42 = (f32[1,2048]{1,0:T(1,128)S(1)}, f32[1,2048]{1,0:T(1,128)S(1)}, u32[]{:S(2)}, u32[]{:S(2)}) collective-permute-start(f32[1,2048]{1,0:T(1,128)S(1)} %add.372), channel_id=1, source_target_pairs={{0,2},{2,0},{1,3},{3,1},{4,6},{6,4},{5,7},{7,5},{8,10},{10,8},{9,1... | collective-permute-start | bytes 24584 | tf_op jit(solution)/shard_map/ppermute | solution.py:117
  355.5 8.5 %collective-permute-done.42 = f32[1,2048]{1,0:T(1,128)S(1)} collective-permute-done((f32[1,2048]{1,0:T(1,128)S(1)}, f32[1,2048]{1,0:T(1,128)S(1)}, u32[]{:S(2)}, u32[]{:S(2)}) %collective-permute-start.42) | collective-permute-done | bytes 8224 | tf_op jit(solution)/shard_map/ppermute | solution.py:117
  369.2 2.4 collective-permute-done.43
  371.7 13.9 %collective-permute-done.50 = bf16[2,2,32,384]{3,2,1,0:T(8,128)(2,1)S(1)} collective-permute-done((bf16[2,2,32,384]{3,2,1,0:T(8,128)(2,1)S(1)}, bf16[2,2,32,384]{3,2,1,0:T(8,128)(2,1)S(1)}, u32[]{:S(2)}, u32[]{:S(2)}) %collective-permute-start.50) | collective-permute-done | bytes 98336 | tf_op jit(solution)/shard_map/ppermute | solution.py:117
  388.2 3.1 collective-permute-done.44
  396.8 1.9 select_bitcast_fusion.1
  400.8 3.9 collective-permute-done.59
  (415 shorter events, 86.0 us)
Async XLA Ops:
  7.2 133.8 %all-gather.3.cloned.1.call-start = ((), (), s32[]{:S(2)}) async-start(), calls=%async_computation.2 | async-start | bytes 5308416 | tf_op jit(solution)/shard_map/all_gather | solution.py:279
  9.3 7.4 %collective-permute-start.1 = (f32[1,1408]{1,0:T(1,128)S(1)}, f32[1,1408]{1,0:T(1,128)S(1)}, u32[]{:S(2)}, u32[]{:S(2)}) collective-permute-start(f32[1,1408]{1,0:T(1,128)S(1)} %pad_maximum_fusion.21), channel_id=1, source_target_pairs={{0,4},{4,0},{1,5},{5,1},{2,6},{6,2},{3,7},{7,3},{8,12},{12,8},{9,1... | collective-permute-start | bytes 16904 | tf_op jit(solution)/shard_map/ppermute | solution.py:117
  12.0 6.3 %collective-permute-start.2 = (bf16[2,32,768]{2,1,0:T(8,128)(2,1)S(1)}, bf16[2,32,768]{2,1,0:T(8,128)(2,1)S(1)}, u32[]{:S(2)}, u32[]{:S(2)}) collective-permute-start(bf16[2,32,768]{2,1,0:T(8,128)(2,1)S(1)} %get-tuple-element.112), channel_id=1, source_target_pairs={{0,4},{4,0},{1,5},{5,1},{2,6},{6,2},{3,7},{7,3},{8,12},{12,8},{9,1... | collective-permute-start | bytes 294920 | tf_op jit(solution)/shard_map/ppermute | solution.py:117
  14.3 6.6 %collective-permute-start.18 = (bf16[2,32,1024]{2,1,0:T(8,128)(2,1)S(1)}, bf16[2,32,1024]{2,1,0:T(8,128)(2,1)S(1)}, u32[]{:S(2)}, u32[]{:S(2)}) collective-permute-start(bf16[2,32,1024]{2,1,0:T(8,128)(2,1)S(1)} %get-tuple-element.104), channel_id=1, source_target_pairs={{0,4},{4,0},{1,5},{5,1},{2,6},{6,2},{3,7},{7,3},{8,12},{12,8},{9,1... | collective-permute-start | bytes 393224 | tf_op jit(solution)/shard_map/ppermute | solution.py:117
  14.9 38.8 %collective-permute-start = (bf16[256,1024]{1,0:T(8,128)(2,1)S(1)}, bf16[256,1024]{1,0:T(8,128)(2,1)S(1)}, u32[]{:S(2)}, u32[]{:S(2)}) collective-permute-start(bf16[256,1024]{1,0:T(8,128)(2,1)S(1)} %bitcast.391), channel_id=1, source_target_pairs={{2,4},{4,2},{3,5},{5,3},{10,12},{12,10},{11,13},{13,11},{18,20},{2... | collective-permute-start | bytes 1572872 | tf_op jit(solution)/shard_map/ppermute | solution.py:161
  18.3 6.2 %collective-permute-start.3 = (bf16[2,32,768]{2,1,0:T(8,128)(2,1)S(1)}, bf16[2,32,768]{2,1,0:T(8,128)(2,1)S(1)}, u32[]{:S(2)}, u32[]{:S(2)}) collective-permute-start(bf16[2,32,768]{2,1,0:T(8,128)(2,1)S(1)} %get-tuple-element.110), channel_id=1, source_target_pairs={{0,1},{1,0},{2,3},{3,2},{4,5},{5,4},{6,7},{7,6},{8,9},{9,8},{10,11... | collective-permute-start | bytes 294920 | tf_op jit(solution)/shard_map/ppermute | solution.py:117
  24.5 4.0 collective-permute-start.4
  26.1 17.1 %collective-permute-start.19 = (bf16[2,32,1024]{2,1,0:T(8,128)(2,1)S(1)}, bf16[2,32,1024]{2,1,0:T(8,128)(2,1)S(1)}, u32[]{:S(2)}, u32[]{:S(2)}) collective-permute-start(bf16[2,32,1024]{2,1,0:T(8,128)(2,1)S(1)} %get-tuple-element.102), channel_id=1, source_target_pairs={{0,1},{1,0},{2,3},{3,2},{4,5},{5,4},{6,7},{7,6},{8,9},{9,8},{10,11... | collective-permute-start | bytes 393224 | tf_op jit(solution)/shard_map/ppermute | solution.py:117
  28.5 4.3 %collective-permute-start.5 = (bf16[2,8,2048]{2,1,0:T(8,128)(2,1)S(1)}, bf16[2,8,2048]{2,1,0:T(8,128)(2,1)S(1)}, u32[]{:S(2)}, u32[]{:S(2)}) collective-permute-start(bf16[2,8,2048]{2,1,0:T(8,128)(2,1)S(1)} %maximum_select_fusion.19), channel_id=1, source_target_pairs={{0,16},{8,24},{16,0},{24,8},{1,17},{9,25},{17,1},{25,9},{2,18},{10... | collective-permute-start | bytes 196616 | tf_op jit(solution)/shard_map/ppermute | solution.py:117
  33.1 9.9 %collective-permute-start.6 = (f32[2048]{0:T(1024)S(1)}, f32[2048]{0:T(1024)S(1)}, u32[]{:S(2)}, u32[]{:S(2)}) collective-permute-start(f32[2048]{0:T(1024)S(1)} %bitcast.426), channel_id=1, source_target_pairs={{0,2},{2,0},{1,3},{3,1},{4,6},{6,4},{5,7},{7,5},{8,10},{10,8},{9,1... | collective-permute-start | bytes 24584 | tf_op jit(solution)/shard_map/ppermute | solution.py:117
  41.2 129.3 %copy-start.50 = (f32[256]{0:T(256)}, f32[256]{0:T(256)S(1)}, u32[]{:S(2)}) copy-start(f32[256]{0:T(256)S(1)} %compare_convert_fusion) | copy-start | bytes 3076
  41.2 8.3 %collective-permute-start.12 = (bf16[2,2,32,768]{3,2,0,1:T(8,128)(2,1)S(1)}, bf16[2,2,32,768]{3,2,0,1:T(8,128)(2,1)S(1)}, u32[]{:S(2)}, u32[]{:S(2)}) collective-permute-start(bf16[2,2,32,768]{3,2,0,1:T(8,128)(2,1)S(1)} %maximum_select_fusion.14), channel_id=1, source_target_pairs={{0,2},{2,0},{1,3},{3,1},{4,6},{6,4},{5,7},{7,5},{8,10},{10,8},{9,1... | collective-permute-start | bytes 589832 | tf_op jit(solution)/shard_map/ppermute | solution.py:117
  43.0 3.7 collective-permute-start.7
  46.6 1.2 collective-permute-start.8
  47.5 279.9 %reduce-scatter.7.cloned.1.call-start = ((), (), s32[]{:S(2)}) async-start(), calls=%async_computation.3 | async-start | bytes 2621440
  49.6 10.9 %collective-permute-start.17 = (bf16[256,1024]{1,0:T(8,128)(2,1)S(1)}, bf16[256,1024]{1,0:T(8,128)(2,1)S(1)}, u32[]{:S(2)}, u32[]{:S(2)}) collective-permute-start(bf16[256,1024]{1,0:T(8,128)(2,1)S(1)} %bitcast.393), channel_id=1, source_target_pairs={{2,4},{4,2},{3,5},{5,3},{10,12},{12,10},{11,13},{13,11},{18,20},{2... | collective-permute-start | bytes 1572872 | tf_op jit(solution)/shard_map/ppermute | solution.py:161
  50.7 8.5 %collective-permute-start.15 = (bf16[2,2,2,32,384]{4,3,1,0,2:T(8,128)(2,1)S(1)}, bf16[2,2,2,32,384]{4,3,1,0,2:T(8,128)(2,1)S(1)}, u32[]{:S(2)}, u32[]{:S(2)}) collective-permute-start(bf16[2,2,2,32,384]{4,3,1,0,2:T(8,128)(2,1)S(1)} %get-tuple-element.91), channel_id=1, source_target_pairs={{0,16},{8,24},{16,0},{24,8},{1,17},{9,25},{17,1},{25,9},{2,18},{10... | collective-permute-start | bytes 589832 | tf_op jit(solution)/shard_map/ppermute | solution.py:117
  52.3 6.2 %collective-permute-start.13 = (bf16[2,2,2,32,384]{4,3,1,0,2:T(8,128)(2,1)S(1)}, bf16[2,2,2,32,384]{4,3,1,0,2:T(8,128)(2,1)S(1)}, u32[]{:S(2)}, u32[]{:S(2)}) collective-permute-start(bf16[2,2,2,32,384]{4,3,1,0,2:T(8,128)(2,1)S(1)} %get-tuple-element.92), channel_id=1, source_target_pairs={{0,8},{8,0},{16,24},{24,16},{1,9},{9,1},{17,25},{25,17},{2,10},{10... | collective-permute-start | bytes 589832 | tf_op jit(solution)/shard_map/ppermute | solution.py:117
  54.5 22.8 %collective-permute-start.10 = (bf16[256,1024]{1,0:T(8,128)(2,1)S(1)}, bf16[256,1024]{1,0:T(8,128)(2,1)}, u32[]{:S(2)}, u32[]{:S(2)}) collective-permute-start(bf16[256,1024]{1,0:T(8,128)(2,1)S(1)} %fusion.47), channel_id=1, source_target_pairs={{0,1},{1,0},{2,3},{3,2},{4,5},{5,4},{6,7},{7,6},{8,9},{9,8},{10,11... | collective-permute-start | bytes 1572872 | tf_op jit(solution)/shard_map/ppermute | solution.py:117
  54.6 42.6 %collective-permute-start.9 = (bf16[256,1024]{1,0:T(8,128)(2,1)S(1)}, bf16[256,1024]{1,0:T(8,128)(2,1)}, u32[]{:S(2)}, u32[]{:S(2)}) collective-permute-start(bf16[256,1024]{1,0:T(8,128)(2,1)S(1)} %fusion.47), channel_id=1, source_target_pairs={{0,4},{4,0},{1,5},{5,1},{2,6},{6,2},{3,7},{7,3},{8,12},{12,8},{9,1... | collective-permute-start | bytes 1572872 | tf_op jit(solution)/shard_map/ppermute | solution.py:117
  58.6 13.4 %collective-permute-start.14 = (bf16[2,2,2,2,32,384]{5,4,2,1,3,0:T(8,128)(2,1)S(1)}, bf16[2,2,2,2,32,384]{5,4,2,1,3,0:T(8,128)(2,1)S(1)}, u32[]{:S(2)}, u32[]{:S(2)}) collective-permute-start(bf16[2,2,2,2,32,384]{5,4,2,1,3,0:T(8,128)(2,1)S(1)} %maximum_select_fusion.6), channel_id=1, source_target_pairs={{0,16},{8,24},{16,0},{24,8},{1,17},{9,25},{17,1},{25,9},{2,18},{10... | collective-permute-start | bytes 1179656 | tf_op jit(solution)/shard_map/ppermute | solution.py:117
  59.3 12.3 %collective-permute-start.16 = (bf16[2,2,2,2,32,384]{5,4,2,1,3,0:T(8,128)(2,1)S(1)}, bf16[2,2,2,2,32,384]{5,4,2,1,3,0:T(8,128)(2,1)S(1)}, u32[]{:S(2)}, u32[]{:S(2)}) collective-permute-start(bf16[2,2,2,2,32,384]{5,4,2,1,3,0:T(8,128)(2,1)S(1)} %maximum_select_fusion.8), channel_id=1, source_target_pairs={{0,8},{8,0},{16,24},{24,16},{1,9},{9,1},{17,25},{25,17},{2,10},{10... | collective-permute-start | bytes 1179656 | tf_op jit(solution)/shard_map/ppermute | solution.py:117
  74.3 22.9 %collective-permute-start.22 = (bf16[256,1024]{1,0:T(8,128)(2,1)}, bf16[256,1024]{1,0:T(8,128)(2,1)}, u32[]{:S(2)}, u32[]{:S(2)}) collective-permute-start(bf16[256,1024]{1,0:T(8,128)(2,1)} %fusion.55), channel_id=1, source_target_pairs={{0,1},{1,0},{2,3},{3,2},{4,5},{5,4},{6,7},{7,6},{8,9},{9,8},{10,11... | collective-permute-start | bytes 1572872 | tf_op jit(solution)/shard_map/ppermute | solution.py:117
  77.3 19.9 %collective-permute-start.11 = (bf16[256,1024]{1,0:T(8,128)(2,1)}, bf16[256,1024]{1,0:T(8,128)(2,1)S(1)}, u32[]{:S(2)}, u32[]{:S(2)}) collective-permute-start(bf16[256,1024]{1,0:T(8,128)(2,1)} %collective-permute-done.10), channel_id=1, source_target_pairs={{0,4},{4,0},{1,5},{5,1},{2,6},{6,2},{3,7},{7,3},{8,12},{12,8},{9,1... | collective-permute-start | bytes 1572872 | tf_op jit(solution)/shard_map/ppermute | solution.py:117
  79.4 63.9 %collective-permute-start.21 = (bf16[256,1024]{1,0:T(8,128)(2,1)}, bf16[256,1024]{1,0:T(8,128)(2,1)}, u32[]{:S(2)}, u32[]{:S(2)}) collective-permute-start(bf16[256,1024]{1,0:T(8,128)(2,1)} %fusion.55), channel_id=1, source_target_pairs={{0,4},{4,0},{1,5},{5,1},{2,6},{6,2},{3,7},{7,3},{8,12},{12,8},{9,1... | collective-permute-start | bytes 1572872 | tf_op jit(solution)/shard_map/ppermute | solution.py:117
  97.2 46.1 %collective-permute-start.23 = (bf16[256,1024]{1,0:T(8,128)(2,1)}, bf16[256,1024]{1,0:T(8,128)(2,1)}, u32[]{:S(2)}, u32[]{:S(2)}) collective-permute-start(bf16[256,1024]{1,0:T(8,128)(2,1)} %collective-permute-done.22), channel_id=1, source_target_pairs={{0,4},{4,0},{1,5},{5,1},{2,6},{6,2},{3,7},{7,3},{8,12},{12,8},{9,1... | collective-permute-start | bytes 1572872 | tf_op jit(solution)/shard_map/ppermute | solution.py:117
  142.9 8.2 %collective-permute-start.20 = (bf16[4,32,1024]{2,1,0:T(8,128)(2,1)}, bf16[4,32,1024]{2,1,0:T(8,128)(2,1)}, u32[]{:S(2)}, u32[]{:S(2)}) collective-permute-start(bf16[4,32,1024]{2,1,0:T(8,128)(2,1)} %get-tuple-element.84), channel_id=1, source_target_pairs={{0,1},{1,0},{2,3},{3,2},{4,5},{5,4},{6,7},{7,6},{8,9},{9,8},{10,11... | collective-permute-start | bytes 786440 | tf_op jit(solution)/shard_map/ppermute | solution.py:117
  153.2 2.7 collective-permute-start.24
  156.4 14.0 %collective-permute-start.25 = (bf16[256,1024]{1,0:T(8,128)(2,1)S(1)}, bf16[256,1024]{1,0:T(8,128)(2,1)S(1)}, u32[]{:S(2)}, u32[]{:S(2)}) collective-permute-start(bf16[256,1024]{1,0:T(8,128)(2,1)S(1)} %fusion.73), channel_id=1, source_target_pairs={{0,1},{1,0},{2,3},{3,2},{4,5},{5,4},{6,7},{7,6},{8,9},{9,8},{10,11... | collective-permute-start | bytes 1572872 | tf_op jit(solution)/shard_map/ppermute | solution.py:117
  171.3 13.2 %collective-permute-start.27 = (bf16[256,1024]{1,0:T(8,128)(2,1)S(1)}, bf16[256,1024]{1,0:T(8,128)(2,1)S(1)}, u32[]{:S(2)}, u32[]{:S(2)}) collective-permute-start(bf16[256,1024]{1,0:T(8,128)(2,1)S(1)} %multiply_convert_fusion.5), channel_id=1, source_target_pairs={{0,1},{1,0},{2,3},{3,2},{4,5},{5,4},{6,7},{7,6},{8,9},{9,8},{10,11... | collective-permute-start | bytes 1572872 | tf_op jit(solution)/shard_map/ppermute | solution.py:117
  171.6 13.7 %collective-permute-start.26 = (bf16[256,1024]{1,0:T(8,128)(2,1)S(1)}, bf16[256,1024]{1,0:T(8,128)(2,1)S(1)}, u32[]{:S(2)}, u32[]{:S(2)}) collective-permute-start(bf16[256,1024]{1,0:T(8,128)(2,1)S(1)} %multiply_convert_fusion.5), channel_id=1, source_target_pairs={{0,4},{4,0},{1,5},{5,1},{2,6},{6,2},{3,7},{7,3},{8,12},{12,8},{9,1... | collective-permute-start | bytes 1572872 | tf_op jit(solution)/shard_map/ppermute | solution.py:117
  184.5 1.9 collective-permute-start.28
  199.5 129.0 %reduce-scatter.9.cloned.1.call-start = ((), (), s32[]{:S(2)}) async-start(), calls=%async_computation.4 | async-start | bytes 2621440
  204.4 2.7 collective-permute-start.29
  210.9 14.3 %collective-permute-start.30 = (bf16[256,1024]{1,0:T(8,128)(2,1)}, bf16[256,1024]{1,0:T(8,128)(2,1)}, u32[]{:S(2)}, u32[]{:S(2)}) collective-permute-start(bf16[256,1024]{1,0:T(8,128)(2,1)} %fusion.74), channel_id=1, source_target_pairs={{0,1},{1,0},{2,3},{3,2},{4,5},{5,4},{6,7},{7,6},{8,9},{9,8},{10,11... | collective-permute-start | bytes 1572872 | tf_op jit(solution)/shard_map/ppermute | solution.py:117
  230.2 13.6 %collective-permute-start.32 = (bf16[256,1024]{1,0:T(8,128)(2,1)}, bf16[256,1024]{1,0:T(8,128)(2,1)S(1)}, u32[]{:S(2)}, u32[]{:S(2)}) collective-permute-start(bf16[256,1024]{1,0:T(8,128)(2,1)} %get-tuple-element.53), channel_id=1, source_target_pairs={{0,1},{1,0},{2,3},{3,2},{4,5},{5,4},{6,7},{7,6},{8,9},{9,8},{10,11... | collective-permute-start | bytes 1572872 | tf_op jit(solution)/shard_map/ppermute | solution.py:117
  234.3 15.4 %collective-permute-start.31 = (bf16[256,1024]{1,0:T(8,128)(2,1)}, bf16[256,1024]{1,0:T(8,128)(2,1)S(1)}, u32[]{:S(2)}, u32[]{:S(2)}) collective-permute-start(bf16[256,1024]{1,0:T(8,128)(2,1)} %get-tuple-element.53), channel_id=1, source_target_pairs={{0,4},{4,0},{1,5},{5,1},{2,6},{6,2},{3,7},{7,3},{8,12},{12,8},{9,1... | collective-permute-start | bytes 1572872 | tf_op jit(solution)/shard_map/ppermute | solution.py:117
  243.8 5.9 %collective-permute-start.33 = (bf16[256,1024]{1,0:T(8,128)(2,1)S(1)}, bf16[256,1024]{1,0:T(8,128)(2,1)S(1)}, u32[]{:S(2)}, u32[]{:S(2)}) collective-permute-start(bf16[256,1024]{1,0:T(8,128)(2,1)S(1)} %collective-permute-done.32), channel_id=1, source_target_pairs={{0,4},{4,0},{1,5},{5,1},{2,6},{6,2},{3,7},{7,3},{8,12},{12,8},{9,1... | collective-permute-start | bytes 1572872 | tf_op jit(solution)/shard_map/ppermute | solution.py:117
  284.4 8.7 %collective-permute-start.53 = (bf16[4,32,1024]{2,1,0:T(8,128)(2,1)S(1)}, bf16[4,32,1024]{2,1,0:T(8,128)(2,1)S(1)}, u32[]{:S(2)}, u32[]{:S(2)}) collective-permute-start(bf16[4,32,1024]{2,1,0:T(8,128)(2,1)S(1)} %get-tuple-element.80), channel_id=1, source_target_pairs={{0,1},{1,0},{2,3},{3,2},{4,5},{5,4},{6,7},{7,6},{8,9},{9,8},{10,11... | collective-permute-start | bytes 786440 | tf_op jit(solution)/shard_map/ppermute | solution.py:117
  287.5 25.1 %collective-permute-start.34 = (bf16[2,256,1024]{2,1,0:T(8,128)(2,1)S(1)}, bf16[2,256,1024]{2,1,0:T(8,128)(2,1)S(1)}, u32[]{:S(2)}, u32[]{:S(2)}) collective-permute-start(bf16[2,256,1024]{2,1,0:T(8,128)(2,1)S(1)} %slice_bitcast_fusion.4), channel_id=1, source_target_pairs={{0,4},{4,0},{1,5},{5,1},{2,6},{6,2},{3,7},{7,3},{8,12},{12,8},{9,1... | collective-permute-start | bytes 3145736 | tf_op jit(solution)/shard_map/ppermute | solution.py:117
  293.2 7.8 %collective-permute-start.54 = (bf16[2,2,32,1024]{3,2,1,0:T(8,128)(2,1)S(1)}, bf16[2,2,32,1024]{3,2,1,0:T(8,128)(2,1)S(1)}, u32[]{:S(2)}, u32[]{:S(2)}) collective-permute-start(bf16[2,2,32,1024]{3,2,1,0:T(8,128)(2,1)S(1)} %dynamic-slice_bitcast_fusion.1), channel_id=1, source_target_pairs={{0,8},{8,0},{16,24},{24,16},{1,9},{9,1},{17,25},{25,17},{2,10},{10... | collective-permute-start | bytes 786440 | tf_op jit(solution)/shard_map/ppermute | solution.py:117
  301.1 5.0 %collective-permute-start.55 = (bf16[2,32,1024]{2,1,0:T(8,128)(2,1)S(1)}, bf16[2,32,1024]{2,1,0:T(8,128)(2,1)S(1)}, u32[]{:S(2)}, u32[]{:S(2)}) collective-permute-start(bf16[2,32,1024]{2,1,0:T(8,128)(2,1)S(1)} %dynamic-slice_bitcast_fusion.9), channel_id=1, source_target_pairs={{0,16},{8,24},{16,0},{24,8},{1,17},{9,25},{17,1},{25,9},{2,18},{10... | collective-permute-start | bytes 393224 | tf_op jit(solution)/shard_map/ppermute | solution.py:117
  302.2 11.7 %collective-permute-start.37 = (bf16[2,256,1024]{2,1,0:T(8,128)(2,1)S(1)}, bf16[2,256,1024]{2,1,0:T(8,128)(2,1)S(1)}, u32[]{:S(2)}, u32[]{:S(2)}) collective-permute-start(bf16[2,256,1024]{2,1,0:T(8,128)(2,1)S(1)} %fusion.58), channel_id=1, source_target_pairs={{0,4},{4,0},{1,5},{5,1},{2,6},{6,2},{3,7},{7,3},{8,12},{12,8},{9,1... | collective-permute-start | bytes 3145736 | tf_op jit(solution)/shard_map/ppermute | solution.py:117
  306.2 5.7 %collective-permute-start.56 = (bf16[32,1024]{1,0:T(8,128)(2,1)S(1)}, bf16[32,1024]{1,0:T(8,128)(2,1)S(1)}, u32[]{:S(2)}, u32[]{:S(2)}) collective-permute-start(bf16[32,1024]{1,0:T(8,128)(2,1)S(1)} %dynamic-slice_bitcast_fusion.21), channel_id=1, source_target_pairs={{0,2},{2,0},{1,3},{3,1},{4,6},{6,4},{5,7},{7,5},{8,10},{10,8},{9,1... | collective-permute-start | bytes 196616 | tf_op jit(solution)/shard_map/ppermute | solution.py:117
  313.9 19.7 %collective-permute-start.35 = (bf16[256,1024]{1,0:T(8,128)(2,1)}, bf16[256,1024]{1,0:T(8,128)(2,1)}, u32[]{:S(2)}, u32[]{:S(2)}) collective-permute-start(bf16[256,1024]{1,0:T(8,128)(2,1)} %fusion.75), channel_id=1, source_target_pairs={{0,1},{1,0},{2,3},{3,2},{4,5},{5,4},{6,7},{7,6},{8,9},{9,8},{10,11... | collective-permute-start | bytes 1572872 | tf_op jit(solution)/shard_map/ppermute | solution.py:117
  314.4 8.0 %collective-permute-start.48 = (bf16[2,2,2,2,32,384]{5,4,3,2,1,0:T(8,128)(2,1)S(1)}, bf16[2,2,2,2,32,384]{5,4,3,2,1,0:T(8,128)(2,1)S(1)}, u32[]{:S(2)}, u32[]{:S(2)}) collective-permute-start(bf16[2,2,2,2,32,384]{5,4,3,2,1,0:T(8,128)(2,1)S(1)} %dynamic-slice_bitcast_fusion), channel_id=1, source_target_pairs={{0,16},{8,24},{16,0},{24,8},{1,17},{9,25},{17,1},{25,9},{2,18},{10... | collective-permute-start | bytes 1179656 | tf_op jit(solution)/shard_map/ppermute | solution.py:117
  316.2 9.6 %collective-permute-start.45 = (bf16[2,2,2,2,32,384]{5,4,3,1,2,0:T(8,128)(2,1)S(1)}, bf16[2,2,2,2,32,384]{5,4,3,1,2,0:T(8,128)(2,1)S(1)}, u32[]{:S(2)}, u32[]{:S(2)}) collective-permute-start(bf16[2,2,2,2,32,384]{5,4,3,1,2,0:T(8,128)(2,1)S(1)} %bitcast.401), channel_id=1, source_target_pairs={{0,8},{8,0},{16,24},{24,16},{1,9},{9,1},{17,25},{25,17},{2,10},{10... | collective-permute-start | bytes 1179656 | tf_op jit(solution)/shard_map/ppermute | solution.py:117
  318.4 23.7 %collective-permute-start.38 = (bf16[256,1024]{1,0:T(8,128)(2,1)}, bf16[256,1024]{1,0:T(8,128)(2,1)}, u32[]{:S(2)}, u32[]{:S(2)}) collective-permute-start(bf16[256,1024]{1,0:T(8,128)(2,1)} %fusion.76), channel_id=1, source_target_pairs={{0,1},{1,0},{2,3},{3,2},{4,5},{5,4},{6,7},{7,6},{8,9},{9,8},{10,11... | collective-permute-start | bytes 1572872 | tf_op jit(solution)/shard_map/ppermute | solution.py:117
  323.3 42.0 %collective-permute-start.49 = (bf16[2,2,2,32,384]{4,3,2,1,0:T(8,128)(2,1)}, bf16[2,2,2,32,384]{4,3,2,1,0:T(8,128)(2,1)}, u32[]{:S(2)}, u32[]{:S(2)}) collective-permute-start(bf16[2,2,2,32,384]{4,3,2,1,0:T(8,128)(2,1)} %dynamic-slice_bitcast_fusion.4), channel_id=1, source_target_pairs={{0,8},{8,0},{16,24},{24,16},{1,9},{9,1},{17,25},{25,17},{2,10},{10... | collective-permute-start | bytes 589832 | tf_op jit(solution)/shard_map/ppermute | solution.py:117
  327.4 40.0 %collective-permute-start.46 = (bf16[2,2,2,32,384]{4,3,2,0,1:T(8,128)(2,1)}, bf16[2,2,2,32,384]{4,3,2,0,1:T(8,128)(2,1)}, u32[]{:S(2)}, u32[]{:S(2)}) collective-permute-start(bf16[2,2,2,32,384]{4,3,2,0,1:T(8,128)(2,1)} %dynamic-slice_bitcast_fusion.5), channel_id=1, source_target_pairs={{0,16},{8,24},{16,0},{24,8},{1,17},{9,25},{17,1},{25,9},{2,18},{10... | collective-permute-start | bytes 589832 | tf_op jit(solution)/shard_map/ppermute | solution.py:117
  330.5 64.9 %collective-permute-start.57 = (bf16[256,1024]{1,0:T(8,128)(2,1)}, bf16[256,1024]{1,0:T(8,128)(2,1)}, u32[]{:S(2)}, u32[]{:S(2)}) collective-permute-start(bf16[256,1024]{1,0:T(8,128)(2,1)} %fusion.78), channel_id=1, source_target_pairs={{0,2},{2,0},{1,3},{3,1},{4,6},{6,4},{5,7},{7,5},{8,10},{10,8},{9,1... | collective-permute-start | bytes 1572872 | tf_op jit(solution)/shard_map/ppermute | solution.py:117
  335.9 60.8 %collective-permute-start.36 = (bf16[256,1024]{1,0:T(8,128)(2,1)}, bf16[256,1024]{1,0:T(8,128)(2,1)}, u32[]{:S(2)}, u32[]{:S(2)}) collective-permute-start(bf16[256,1024]{1,0:T(8,128)(2,1)} %fusion.63), channel_id=1, source_target_pairs={{2,4},{4,2},{3,5},{5,3},{10,12},{12,10},{11,13},{13,11},{18,20},{2... | collective-permute-start | bytes 1572872 | tf_op jit(solution)/shard_map/ppermute | solution.py:161
  343.7 1.2 collective-permute-start.40
  344.9 4.2 %collective-permute-start.41 = (f32[1,2048]{1,0:T(1,128)S(1)}, f32[1,2048]{1,0:T(1,128)S(1)}, u32[]{:S(2)}, u32[]{:S(2)}) collective-permute-start(f32[1,2048]{1,0:T(1,128)S(1)} %fusion.132), channel_id=1, source_target_pairs={{0,1},{1,0},{2,3},{3,2},{4,5},{5,4},{6,7},{7,6},{8,9},{9,8},{10,11... | collective-permute-start | bytes 24584 | tf_op jit(solution)/shard_map/ppermute | solution.py:117
  349.1 14.8 %collective-permute-start.42 = (f32[1,2048]{1,0:T(1,128)S(1)}, f32[1,2048]{1,0:T(1,128)S(1)}, u32[]{:S(2)}, u32[]{:S(2)}) collective-permute-start(f32[1,2048]{1,0:T(1,128)S(1)} %add.372), channel_id=1, source_target_pairs={{0,2},{2,0},{1,3},{3,1},{4,6},{6,4},{5,7},{7,5},{8,10},{10,8},{9,1... | collective-permute-start | bytes 24584 | tf_op jit(solution)/shard_map/ppermute | solution.py:117
  364.0 35.2 %collective-permute-start.39 = (bf16[256,1024]{1,0:T(8,128)(2,1)S(1)}, bf16[256,1024]{1,0:T(8,128)(2,1)S(1)}, u32[]{:S(2)}, u32[]{:S(2)}) collective-permute-start(bf16[256,1024]{1,0:T(8,128)(2,1)S(1)} %fusion.52), channel_id=1, source_target_pairs={{2,4},{4,2},{3,5},{5,3},{10,12},{12,10},{11,13},{13,11},{18,20},{2... | collective-permute-start | bytes 1572872 | tf_op jit(solution)/shard_map/ppermute | solution.py:161
  365.3 6.4 %collective-permute-start.43 = (f32[2,8,2048]{2,1,0:T(8,128)S(1)}, f32[2,8,2048]{2,1,0:T(8,128)S(1)}, u32[]{:S(2)}, u32[]{:S(2)}) collective-permute-start(f32[2,8,2048]{2,1,0:T(8,128)S(1)} %dynamic-slice_bitcast_fusion.10), channel_id=1, source_target_pairs={{0,16},{8,24},{16,0},{24,8},{1,17},{9,25},{17,1},{25,9},{2,18},{10... | collective-permute-start | bytes 393224 | tf_op jit(solution)/shard_map/ppermute | solution.py:117
  367.4 18.2 %collective-permute-start.50 = (bf16[2,2,32,384]{3,2,1,0:T(8,128)(2,1)S(1)}, bf16[2,2,32,384]{3,2,1,0:T(8,128)(2,1)S(1)}, u32[]{:S(2)}, u32[]{:S(2)}) collective-permute-start(bf16[2,2,32,384]{3,2,1,0:T(8,128)(2,1)S(1)} %dynamic-slice_bitcast_fusion.16), channel_id=1, source_target_pairs={{0,2},{2,0},{1,3},{3,1},{4,6},{6,4},{5,7},{7,5},{8,10},{10,8},{9,1... | collective-permute-start | bytes 294920 | tf_op jit(solution)/shard_map/ppermute | solution.py:117
  371.7 14.9 %collective-permute-start.47 = (bf16[2,2,32,384]{3,2,1,0:T(8,128)(2,1)S(1)}, bf16[2,2,32,384]{3,2,1,0:T(8,128)(2,1)S(1)}, u32[]{:S(2)}, u32[]{:S(2)}) collective-permute-start(bf16[2,2,32,384]{3,2,1,0:T(8,128)(2,1)S(1)} %dynamic-slice_bitcast_fusion.17), channel_id=1, source_target_pairs={{0,2},{2,0},{1,3},{3,1},{4,6},{6,4},{5,7},{7,5},{8,10},{10,8},{9,1... | collective-permute-start | bytes 294920 | tf_op jit(solution)/shard_map/ppermute | solution.py:117
  386.7 1.4 collective-permute-start.51
  386.8 4.5 %collective-permute-start.44 = (f32[8,2048]{1,0:T(8,128)S(1)}, f32[8,2048]{1,0:T(8,128)S(1)}, u32[]{:S(2)}, u32[]{:S(2)}) collective-permute-start(f32[8,2048]{1,0:T(8,128)S(1)} %dynamic-slice_bitcast_fusion.22), channel_id=1, source_target_pairs={{0,8},{8,0},{16,24},{24,16},{1,9},{9,1},{17,25},{25,17},{2,10},{10... | collective-permute-start | bytes 196616 | tf_op jit(solution)/shard_map/ppermute | solution.py:117
  388.1 4.9 %collective-permute-start.52 = (bf16[2,32,768]{2,1,0:T(8,128)(2,1)S(1)}, bf16[2,32,768]{2,1,0:T(8,128)(2,1)S(1)}, u32[]{:S(2)}, u32[]{:S(2)}) collective-permute-start(bf16[2,32,768]{2,1,0:T(8,128)(2,1)S(1)} %get-tuple-element.106), channel_id=1, source_target_pairs={{0,1},{1,0},{2,3},{3,2},{4,5},{5,4},{6,7},{7,6},{8,9},{9,8},{10,11... | collective-permute-start | bytes 294920 | tf_op jit(solution)/shard_map/ppermute | solution.py:117
  396.7 2.0 collective-permute-start.58
  398.8 5.9 %collective-permute-start.59 = (bf16[2,32,1024]{2,1,0:T(8,128)(2,1)S(1)}, bf16[2,32,1024]{2,1,0:T(8,128)(2,1)S(1)}, u32[]{:S(2)}, u32[]{:S(2)}) collective-permute-start(bf16[2,32,1024]{2,1,0:T(8,128)(2,1)S(1)} %get-tuple-element.94), channel_id=1, source_target_pairs={{0,1},{1,0},{2,3},{3,2},{4,5},{5,4},{6,7},{7,6},{8,9},{9,8},{10,11... | collective-permute-start | bytes 393224 | tf_op jit(solution)/shard_map/ppermute | solution.py:117
  (76 other events, 1185.9 us)
Sparse Core Ops, SparseCore 0:
  47.6 93.3 all-gather.2
  199.6 34.4 reduce-scatter.6
  237.2 35.1 reduce-scatter.8

commit v2 on v1

--- a/solution.py
+++ b/solution.py
@@ -3,6 +3,8 @@
 import jax
 import jax.numpy as jnp
 from jax import lax
+from jax.experimental import pallas as pl
+from jax.experimental.pallas import tpu as pltpu
 from jax.sharding import Mesh
 from jax.sharding import PartitionSpec as P
 
@@ -45,67 +47,138 @@
     return d_input, d_scale
 
 
-def rope_tables(positions, repeats):
+PAIR = 2 * HD
+
+
+def rope_tables(positions):
     half_dim = HD // 2
     inverse_freq = jnp.power(10000.0, -jnp.arange(half_dim, dtype=f32) * 2.0 / HD)
-    angles = positions.astype(f32)[:, None] * inverse_freq[None, :]
-    return jnp.cos(angles)[:, None, :], jnp.sin(angles)[:, None, :]
-
-
-def rotate(field, cosine, sine):
-    rows, width = field.shape
-    field = field.reshape(rows, width // HD, HD)
-    half_dim = HD // 2
-    first, second = field[..., :half_dim], field[..., half_dim:]
-    turned = jnp.concatenate(
-        [first * cosine - second * sine, second * cosine + first * sine], axis=-1
+    angles = positions.astype(f32)[:, None] * jnp.tile(inverse_freq, PAIR // half_dim)[None, :]
+    return jnp.cos(angles), jnp.sin(angles)
+
+
+def turn(field, cosine, sine, sign):
+    lane = lax.broadcasted_iota(jnp.int32, field.shape, 1)
+    first = lane % HD < HD // 2
+    other = jnp.where(
+        first, -pltpu.roll(field, PAIR - HD // 2, 1), pltpu.roll(field, HD // 2, 1)
     )
-    return turned.reshape(rows, width)
-
-
-def attend_forward(query, key, value, bias):
+    return field * cosine + other * sine * sign
+
+
+def only(field, head):
+    lane = lax.broadcasted_iota(jnp.int32, field.shape, 1)
+    return jnp.where(lane // HD == head, field, jnp.zeros_like(field))
+
+
+def attend_forward_kernel(
+    q_in, k_in, v_in, cosine, sine, usable, q_out, k_out, v_out, mixed, logs
+):
+    block = min(256, q_in.shape[0])
+    scale = 1.0 / math.sqrt(HD)
+    q_out[...] = turn(q_in[...], cosine[...], sine[...], 1.0).astype(bf16)
+    k_out[...] = turn(k_in[...], cosine[...], sine[...], 1.0).astype(bf16)
+    v_out[...] = v_in[...].astype(bf16)
+    fits = usable[...] > 0
+
+    def step(at, _):
+        rows = pl.ds(pl.multiple_of(at * block, block), block)
+        query, key, value = q_out[rows, :], k_out[...], v_out[...]
+        total = jnp.zeros((block, PAIR), f32)
+        log = []
+        for head in range(2):
+            scores = dot_right_t(only(query, head), key) * scale
+            scores = jnp.where(fits, scores, -1e30)
+            row_max = jnp.max(scores, axis=-1, keepdims=True)
+            weights = jnp.exp(scores - row_max)
+            row_sum = jnp.sum(weights, axis=-1, keepdims=True)
+            low = (weights * (1.0 / row_sum)).astype(bf16)
+            total = total + dot(low, only(value, head))
+            log.append(jnp.broadcast_to(row_max + jnp.log(row_sum), (block, PAIR)))
+        lane = lax.broadcasted_iota(jnp.int32, (block, PAIR), 1)
+        mixed[rows, :] = total.astype(bf16)
+        logs[rows, :] = jnp.where(lane < HD, log[0], log[1])
+        return 0
+
+    lax.fori_loop(0, q_in.shape[0] // block, step, 0)
+
+
+def attend_backward_kernel(
+    q_in, k_in, v_in, logs, d_mixed, cosine, sine, usable, dq_out, dk_out, dv_out, d_key, d_value
+):
+    block = min(256, q_in.shape[0])
+    scale = 1.0 / math.sqrt(HD)
+    fits = usable[...] > 0
+    d_key[...] = jnp.zeros_like(d_key)
+    d_value[...] = jnp.zeros_like(d_value)
+
+    def step(at, _):
+        rows = pl.ds(pl.multiple_of(at * block, block), block)
+        query, key, value, d_block = q_in[rows, :], k_in[...], v_in[...], d_mixed[rows, :]
+        log = logs[rows, :]
+        d_query = jnp.zeros((block, PAIR), f32)
+        for head in range(2):
+            q_head, d_head = only(query, head), only(d_block, head)
+            scores = dot_right_t(q_head, key) * scale
+            scores = jnp.where(fits, scores, -1e30)
+            probs = jnp.exp(scores - log[:, head * HD : head * HD + 1])
+            d_value[...] += dot_left_t(probs.astype(bf16), d_head)
+            d_probs = dot_right_t(d_head, value)
+            row_dot = jnp.sum(d_probs * probs, axis=-1, keepdims=True)
+            d_scores = (probs * (d_probs - row_dot)).astype(bf16)
+            d_query = d_query + dot(d_scores, only(key, head))
+            d_key[...] += dot_left_t(d_scores, q_head)
+        d_query = (d_query * scale).astype(bf16).astype(f32)
+        dq_out[rows, :] = turn(d_query, cosine[rows, :], sine[rows, :], -1.0).astype(bf16)
+        return 0
+
+    lax.fori_loop(0, q_in.shape[0] // block, step, 0)
+    turned = (d_key[...] * scale).astype(bf16).astype(f32)
+    dk_out[...] = turn(turned, cosine[...], sine[...], -1.0).astype(bf16)
+    dv_out[...] = d_value[...].astype(bf16)
+
+
+def attend_forward(packed, cosine, sine, usable):
+    length, pairs = packed.shape[0], packed.shape[1] // (3 * PAIR)
+    column = lambda first: pl.BlockSpec((length, PAIR), lambda i: (0, first + i))
+    fixed = pl.BlockSpec((length, PAIR), lambda i: (0, 0))
+    row = pl.BlockSpec((1, length), lambda i: (0, 0))
+    low = jax.ShapeDtypeStruct((length, pairs * PAIR), bf16)
+    return pl.pallas_call(
+        attend_forward_kernel,
+        grid=(pairs,),
+        in_specs=[column(0), column(pairs), column(2 * pairs), fixed, fixed, row],
+        out_specs=[column(0)] * 5,
+        out_shape=[low] * 4 + [jax.ShapeDtypeStruct((length, pairs * PAIR), f32)],
+        compiler_params=pltpu.CompilerParams(vmem_limit_bytes=40 << 20),
+        cost_estimate=pl.CostEstimate(
+            flops=pairs * 16 * length * length * PAIR,
+            bytes_accessed=length * pairs * PAIR * 24,
+            transcendentals=pairs * 2 * length * length,
+        ),
+    )(packed, packed, packed, cosine, sine, usable)
+
+
+def attend_backward(query, key, value, logs, d_mixed, cosine, sine, usable, pair):
     length = query.shape[0]
-    block = min(512, length)
-    scale = 1.0 / math.sqrt(HD)
-    mixed, logs = [], []
-    for at in range(0, length, block):
-        scores = jnp.einsum("qhd,khd->hqk", query[at : at + block], key, preferred_element_type=f32)
-        scores = jnp.where(bias[None, None, :], scores * scale, -1e30)
-        row_max = jnp.max(scores, axis=-1, keepdims=True)
-        weights = jnp.exp(scores - row_max)
-        row_sum = jnp.sum(weights, axis=-1, keepdims=True)
-        low = (weights / row_sum).astype(bf16)
-        mixed.append(
-            jnp.einsum("hqk,khd->qhd", low, value, preferred_element_type=f32).astype(bf16)
-        )
-        logs.append((row_max + jnp.log(row_sum))[..., 0])
-    return jnp.concatenate(mixed, axis=0), jnp.concatenate(logs, axis=1)
-
-
-def attend_backward(query, key, value, log_sum, d_out, bias):
-    length = query.shape[0]
-    block = min(512, length)
-    scale = 1.0 / math.sqrt(HD)
-    d_key = jnp.zeros(key.shape, f32)
-    d_value = jnp.zeros(value.shape, f32)
-    d_query = []
-    for at in range(0, length, block):
-        q_block, d_block = query[at : at + block], d_out[at : at + block]
-        scores = jnp.einsum("qhd,khd->hqk", q_block, key, preferred_element_type=f32) * scale
-        scores = jnp.where(bias[None, None, :], scores, -1e30)
-        probs = jnp.exp(scores - log_sum[:, at : at + block, None])
-        low = probs.astype(bf16)
-        d_value = d_value + jnp.einsum("hqk,qhd->khd", low, d_block, preferred_element_type=f32)
-        d_probs = jnp.einsum("qhd,khd->hqk", d_block, value, preferred_element_type=f32)
-        row_dot = jnp.sum(d_probs * probs, axis=-1, keepdims=True)
-        d_scores = (probs * (d_probs - row_dot)).astype(bf16)
-        d_query.append(
-            jnp.einsum("hqk,khd->qhd", d_scores, key, preferred_element_type=f32) * scale
-        )
-        d_key = d_key + scale * jnp.einsum(
-            "hqk,qhd->khd", d_scores, q_block, preferred_element_type=f32
-        )
-    return jnp.concatenate(d_query, axis=0), d_key, d_value
+    column = pl.BlockSpec((length, PAIR), lambda i: (0, pair))
+    fixed = pl.BlockSpec((length, PAIR), lambda i: (0, 0))
+    row = pl.BlockSpec((1, length), lambda i: (0, 0))
+    low = jax.ShapeDtypeStruct((length, PAIR), bf16)
+    return pl.pallas_call(
+        attend_backward_kernel,
+        grid=(1,),
+        in_specs=[column] * 5 + [fixed, fixed, row],
+        out_specs=[fixed] * 3,
+        out_shape=[low] * 3,
+        scratch_shapes=[pltpu.VMEM((length, PAIR), f32)] * 2,
+        compiler_params=pltpu.CompilerParams(vmem_limit_bytes=40 << 20),
+        cost_estimate=pl.CostEstimate(
+            flops=40 * length * length * PAIR,
+            bytes_accessed=length * PAIR * 24,
+            transcendentals=2 * length * length,
+        ),
+    )(query, key, value, logs, d_mixed, cosine, sine, usable)
 
 
 def build(seq_size, head_size):
@@ -265,6 +338,7 @@
         time_rows, qkv_quad = after(time_weight, qkv_quad)
         w_qkv, labels = gather(qkv_quad, ["t", "c"], ["g"])
         later, w_qkv = after(cotangent[0], w_qkv)
+        out_later, w_qkv = after(out_weight, w_qkv)
         cut = 3 * head_cols // 2
         w_qkv = jnp.concatenate(
             [
@@ -275,13 +349,14 @@
         )
         in_quad, _ = quad(in_split(in_scaled))
         rows_in = 4 * in_weight.shape[0]
-        packs = [in_quad.reshape(rows_in, width), down_weight] + ([out_weight] if aligned else [])
-        packs = lax.all_gather(jnp.concatenate(packs), ("plane", "group"), axis=0)
+        packs = jnp.concatenate([in_quad.reshape(rows_in, width), down_weight])
+        packs = lax.all_gather(packs, ("plane", "group"), axis=0)
         w_in = packs[:, :rows_in].reshape(planes, 2, 2, 2, -1, width)
         w_in = w_in.transpose(0, 3, 1, 2, 4, 5).reshape(width, ff_cols)
         w_down = packs[:, rows_in : rows_in + ff_rows].reshape(ff_cols, width)
         if aligned:
-            w_out = out_heads(packs[:, rows_in + ff_rows :])
+            w_out = in_order(*gather(out_later, [], ("g",) + forwards))
+            w_out = out_heads(w_out)
         else:
             w_out, labels = gather(out_weight, [], ("c", "t", "g") + forwards)
             w_out = lax.dynamic_slice_in_dim(
@@ -309,9 +384,10 @@
         )
         steps = jnp.arange(span, dtype=jnp.int32)
         valid = (blocks[0] * span + steps < length).astype(f32)[:, None]
-        cosine, sine = rope_tables(jnp.concatenate([block * span + steps for block in blocks]), 0)
+        cosine, sine = rope_tables(jnp.concatenate([block * span + steps for block in blocks]))
         usable_blocks = usable.reshape(head_size, span)
-        bias = jnp.concatenate([pick(usable_blocks, block, 0) for block in blocks])
+        usable_row = jnp.concatenate([pick(usable_blocks, block, 0) for block in blocks])
+        usable_row = usable_row.astype(f32)[None, :]
 
         def gather_four(x):
             across = send(x, "t")
@@ -325,18 +401,15 @@
         inputs = moved(tokens[0]).astype(f32)
         w_qkv, upstream = after(w_qkv, moved(later))
         upstream = upstream.astype(f32)
-        all_d = gather_four((valid * upstream).astype(bf16))
-        w_out, all_d = after(w_out, all_d)
+        own_d = (valid * upstream).astype(bf16)
+        across_d, core_d = send(own_d, "t"), send(own_d, "c")
         white_a, inv_a = whiten(inputs)
         all_a = gather_four((white_a * scale_attn).astype(bf16))
         packed = dot(all_a, w_qkv)
-        head_shape = (full_len, head_cols // HD, HD)
-        query = rotate(packed[:, :head_cols], cosine, sine).astype(bf16).reshape(head_shape)
-        key = rotate(packed[:, head_cols : 2 * head_cols], cosine, sine).astype(bf16)
-        key = key.reshape(head_shape)
-        value = packed[:, 2 * head_cols :].astype(bf16).reshape(head_shape)
-        mixed, log_sum = attend_forward(query, key, value, bias)
-        mixed = mixed.reshape(full_len, head_cols)
+        across_d, core_d, packed = lax.optimization_barrier((across_d, core_d, packed))
+        all_d = jnp.concatenate([own_d, core_d, across_d, send(across_d, "c")])
+        w_out, all_d = after(w_out, all_d)
+        query, key, value, mixed, logs = attend_forward(packed, cosine, sine, usable_row)
 
         hidden = inputs + valid * sum_four(dot(mixed, w_out))
         white_m, inv_m = whiten(hidden)
@@ -355,22 +428,22 @@
         grad_in = dot_left_t(all_m, d_upper).astype(bf16).reshape(planes, 2 * rows_in, width)
         sum_d = lax.psum_scatter(grad_down, "plane", scatter_dimension=0, tiled=True)[0]
         sum_i = lax.psum_scatter(grad_in, "plane", scatter_dimension=0, tiled=True)[0]
-        both = jnp.concatenate([sum_i, sum_d])
-        both_in = both[: 2 * rows_in].reshape(2, 2, 2, -1, width).transpose(1, 0, 2, 3, 4)
-        both = jnp.concatenate(
-            [both_in.reshape(2, rows_in, width), both[2 * rows_in :].reshape(2, ff_rows, width)],
-            axis=1,
-        )
-        both = pick(both, group, 0).astype(f32) + send(pick(both, 1 - group, 0), "g").astype(f32)
-        in_sums = both[:rows_in].reshape(2, 2, -1, width)
-        sum_down = both[rows_in:]
+        sum_i = sum_i.reshape(2, 2, 2, -1, width).transpose(1, 0, 2, 3, 4)
+        sum_i = sum_i.reshape(2, rows_in, width)
+        sum_d = sum_d.reshape(2, ff_rows, width)
+
+        def over_group(x):
+            return pick(x, group, 0).astype(f32) + send(pick(x, 1 - group, 0), "g").astype(f32)
+
+        sum_down = over_group(sum_d)
+        in_sums = over_group(sum_i).reshape(2, 2, -1, width)
         d_from_m, d_scale_m = whiten_back(d_normed_m, white_m, inv_m, scale_mlp)
         d_hidden = upstream + d_from_m
         all_da = gather_four((valid * d_hidden).astype(bf16))
         all_da, mlp_part = after(all_da, mlp_part)
         grad_out = dot_left_t(mixed, all_da).astype(bf16)
-        output = hidden + valid * sum_four(mlp_part.astype(f32))
-        output = moved(output.astype(bf16))[None]
+        mlp_part = mlp_part.reshape(2, 2, span, width)
+        out_core = send(mlp_part[:, 1], "c")
         if aligned:
             sum_out = reduce_rows(out_pieces(grad_out), down_axes, forwards + ("g",))
         else:
@@ -378,20 +451,24 @@
                 jnp.zeros((width, width), bf16), grad_out, (2 * core + side) * head_cols, 0
             )
             sum_out = reduce_rows(padded, natural, forwards + ("g", "t", "c"))
-        d_mixed = dot_right_t(all_da, w_out).astype(bf16).reshape(head_shape)
-        d_query, d_key, d_value = attend_backward(query, key, value, log_sum, d_mixed, bias)
-        d_packed = jnp.concatenate(
-            [
-                rotate(
-                    d_query.astype(bf16).astype(f32).reshape(full_len, head_cols), cosine, -sine
-                ).astype(bf16),
-                rotate(
-                    d_key.astype(bf16).astype(f32).reshape(full_len, head_cols), cosine, -sine
-                ).astype(bf16),
-                d_value.astype(bf16).reshape(full_len, head_cols),
-            ],
-            axis=1,
-        )
+        d_mixed = dot_right_t(all_da, w_out).astype(bf16)
+        halves = []
+        for pair in range(head_cols // PAIR):
+            halves.append(
+                attend_backward(query, key, value, logs, d_mixed, cosine, sine, usable_row, pair)
+            )
+            if pair == 0:
+                halves[0], d_mixed, out_core, sum_down = lax.optimization_barrier(
+                    (halves[0], d_mixed, out_core, sum_down)
+                )
+                mlp_sum = mlp_part[:, 0].astype(f32) + out_core.astype(f32)
+                output = mlp_sum[0] + send(mlp_sum[1].astype(bf16), "t").astype(f32)
+                output = (hidden + valid * output).astype(bf16)
+        d_packed = jnp.concatenate([half[k] for k in range(3) for half in halves], axis=1)
+        d_packed, output, sum_out, in_sums = lax.optimization_barrier(
+            (d_packed, output, sum_out, in_sums)
+        )
+        output = moved(output)[None]
         grad_qkv = dot_left_t(all_a, d_packed).astype(bf16)
         part = dot_right_t(d_packed, w_qkv).reshape(2, 2, span, width)
         from_core = send(part[:, 1].astype(bf16), "c")

time: 418 us -> 422 us (level)
  matrix products: 73.3 us -> 38.1 us
  Pallas kernels: 0 us -> 33.5 us
  other arithmetic: 56.9 us -> 33.9 us
  starting transfers between devices: 54.7 us -> 65.7 us
  waiting for transfers between devices: 192 us -> 203 us
    ppermute x56 -> x60, waiting for transfers between devices: 166 us -> 203 us  [swap(): return lax.ppermute(x, axis, [(i, i ^ mask) for i in range(size)])]
    dot_general x12 -> x0, matrix products: 34.4 us -> none  [the longest x2 15.8 us: attend_backward(): jnp.einsum('qhd,khd->hqk', d_block, value, preferred_element_type=f32)]
    pallas_call x0 -> x3, Pallas kernels: none -> 33.5 us  [the longest x2 20.2 us: attend_backward(): pl.pallas_call(attend_backward_kernel, grid=(1,), in_specs=[column] * 5 +...]
    all_gather x1, waiting for transfers between devices: 26.3 us -> 0.01 us  [per_device(): packs = lax.all_gather(packs, ('plane', 'group'), axis=0)]
    convert_element_type x5 -> x4, other arithmetic: 12.8 us -> 0.38 us  [the longest x1 0.2 us: per_device(): output = (hidden + valid * output).astype(bf16)]
    ppermute x56 -> x60, starting transfers between devices: 50.5 us -> 61.6 us  [swap(): return lax.ppermute(x, axis, [(i, i ^ mask) for i in range(size)])]
    reduce_sum x1 -> x0, other arithmetic: 4.34 us -> none  [attend_forward(): row_sum = jnp.sum(weights, axis=-1, keepdims=True)]
  transfers between devices with their start and end apart: 63 -> 67, of which waited for: 38 -> 35; matrix products, arithmetic and copies ran while one was open for 30% -> 18% of each run, Pallas kernels for 0% -> 8%
where the time goes in v2:
time: 422 us; the launch traced here: 414 us
  waiting for transfers between devices  203 us (48%)
  starting transfers between devices  65.7 us (16%)
  matrix products  38.1 us (9%)
  other arithmetic  33.9 us (8%)
  Pallas kernels  33.5 us (8%)
  local copies, waits for them, and re-layouts  22.4 us (5%)
  between operations  17.3 us (4%)
    ppermute x60, waiting for transfers between devices, swap(): return lax.ppermute(x, axis, [(i, i ^ mask) for i in range(size)])  203 us
    ppermute x60, starting transfers between devices, swap(): return lax.ppermute(x, axis, [(i, i ^ mask) for i in range(size)])  61.6 us
    pallas_call x2, Pallas kernels, attend_backward(): pl.pallas_call(attend_backward_kernel, grid=(1,), in_specs=[column] * 5 +...  20.2 us
    dot_general x4, matrix products, dot(): return jnp.dot(left, right, preferred_element_type=f32)  15 us
    pallas_call x1, Pallas kernels, attend_forward(): pl.pallas_call(attend_forward_kernel, grid=(pairs,), in_specs=[column(0),...  13.4 us
    dot_general x4, matrix products, dot_left_t(): lax.dot_general(left, right, (((0,), (0,)), ((), ())), preferred_element_...  11.6 us
    dot_general x4, matrix products, dot_right_t(): lax.dot_general(left, right, (((1,), (1,)), ((), ())), preferred_element_...  10.9 us
  transfers between devices with their start and end apart: 67, of which 35 were waited for; matrix products, arithmetic and copies ran while one was open for 18% of the time, Pallas kernels for 8%

profile of v2, /device:TPU:0, one launch (start us, length us, event | category | flops | bytes accessed | tf_op | source)
XLA Modules:
  0.0 414.2 jit_solution(13863275828412454106)
XLA Ops:
  14.6 5.5 %collective-permute-start.27 = (bf16[2,32,1024]{2,1,0:T(8,128)(2,1)S(1)}, bf16[2,32,1024]{2,1,0:T(8,128)(2,1)S(1)}, u32[]{:S(2)}, u32[]{:S(2)}) collective-permute-start(bf16[2,32,1024]{2,1,0:T(8,128)(2,1)S(1)} %get-tuple-element.130), channel_id=1, source_target_pairs={{0,4},{4,0},{1,5},{5,1},{2,6},{6,2},{3,7},{7,3},{8,12},{12,8},{9,1... | collective-permute-start | bytes 393224 | tf_op jit(solution)/shard_map/ppermute | solution.py:190
  20.2 1.9 multiply_sine_fusion
  23.8 1.6 collective-permute-start.2
  25.5 7.6 %collective-permute-done.2 = bf16[2,32,768]{2,1,0:T(8,128)(2,1)S(1)} collective-permute-done((bf16[2,32,768]{2,1,0:T(8,128)(2,1)S(1)}, bf16[2,32,768]{2,1,0:T(8,128)(2,1)S(1)}, u32[]{:S(2)}, u32[]{:S(2)}) %collective-permute-start.2) | collective-permute-done | bytes 98336 | tf_op jit(solution)/shard_map/ppermute | solution.py:190
  34.8 2.3 collective-permute-done.12
  38.7 2.7 collective-permute-done.13
  42.4 2.3 collective-permute-start.3
  44.7 2.8 collective-permute-done.14
  47.5 4.4 %collective-permute-done.15 = f32[2048]{0:T(1024)S(1)} collective-permute-done((f32[2048]{0:T(1024)S(1)}, f32[2048]{0:T(1024)S(1)}, u32[]{:S(2)}, u32[]{:S(2)}) %collective-permute-start.15) | collective-permute-done | bytes 8224 | tf_op jit(solution)/shard_map/ppermute | solution.py:190
  56.7 1.9 collective-permute-done.20
  61.1 1.8 collective-permute-start.17
  63.0 3.1 collective-permute-done.21
  66.2 2.6 collective-permute-start.5
  69.0 14.8 %collective-permute-done.22 = bf16[2,2,32,1024]{3,2,1,0:T(8,128)(2,1)S(1)} collective-permute-done((bf16[2,2,32,1024]{3,2,1,0:T(8,128)(2,1)S(1)}, bf16[2,2,32,1024]{3,2,1,0:T(8,128)(2,1)S(1)}, u32[]{:S(2)}, u32[]{:S(2)}) %collective-permute-start.22) | collective-permute-done | bytes 262176 | tf_op jit(solution)/shard_map/ppermute | solution.py:190
  83.8 3.0 collective-permute-start.7
  87.2 13.2 %collective-permute-done.7 = bf16[2,2,2,2,32,384]{5,4,2,1,3,0:T(8,128)(2,1)S(1)} collective-permute-done((bf16[2,2,2,2,32,384]{5,4,2,1,3,0:T(8,128)(2,1)S(1)}, bf16[2,2,2,2,32,384]{5,4,2,1,3,0:T(8,128)(2,1)S(1)}, u32[]{:S(2)}, u32[]{:S(2)}) %collective-permute-start.7) | collective-permute-done | bytes 393248 | tf_op jit(solution)/shard_map/ppermute | solution.py:190
  103.3 1.8 fusion.48.q_in.k_in.v_in
  105.1 19.7 %collective-permute-done.9 = bf16[256,1024]{1,0:T(8,128)(2,1)S(1)} collective-permute-done((bf16[256,1024]{1,0:T(8,128)(2,1)S(1)}, bf16[256,1024]{1,0:T(8,128)(2,1)S(1)}, u32[]{:S(2)}, u32[]{:S(2)}) %collective-permute-start.9) | collective-permute-done | bytes 524320 | tf_op jit(solution)/shard_map/ppermute | solution.py:190
  124.8 10.1 %collective-permute-done.23 = bf16[4,32,1024]{2,1,0:T(8,128)(2,1)S(1)} collective-permute-done((bf16[4,32,1024]{2,1,0:T(8,128)(2,1)S(1)}, bf16[4,32,1024]{2,1,0:T(8,128)(2,1)S(1)}, u32[]{:S(2)}, u32[]{:S(2)}) %collective-permute-start.23) | collective-permute-done | bytes 262176 | tf_op jit(solution)/shard_map/ppermute | solution.py:190
  135.0 13.4 %shard_map.187 = (bf16[1024,256]{1,0:T(8,128)(2,1)S(1)}, bf16[1024,256]{1,0:T(8,128)(2,1)S(1)}, bf16[1024,256]{1,0:T(8,128)(2,1)S(1)}, bf16[1024,256]{1,0:T(8,128)(2,1)S(1)}, f32[1024,256]{1,0:T(8,128)S(1)}) custom-call(f32[1024,768]{1,0:T(8,128)S(1)} %fusion.48.q_in.k_in.v_in, f32[1024,768]{1,0:T(8,128)S(1)} %fusion.48.q_in.k_in.v_in, ...), custom_call_target="tpu_custom_call" | custom-call | flops 4294967296 | bytes 6291456 | tf_op jit(solution)/shard_map/pallas_call | solution.py:147
  148.5 1.7 pad_maximum_fusion.1
  151.2 2.6 collective-permute-done.25
  154.4 2.5 collective-permute-start.26
  156.9 12.2 %collective-permute-done.26 = bf16[256,1024]{1,0:T(8,128)(2,1)S(1)} collective-permute-done((bf16[256,1024]{1,0:T(8,128)(2,1)S(1)}, bf16[256,1024]{1,0:T(8,128)(2,1)S(1)}, u32[]{:S(2)}, u32[]{:S(2)}) %collective-permute-start.26) | collective-permute-done | bytes 524320 | tf_op jit(solution)/shard_map/ppermute | solution.py:190
  171.5 1.7 collective-permute-start.30
  173.2 12.0 %collective-permute-done.30 = bf16[256,1024]{1,0:T(8,128)(2,1)} collective-permute-done((bf16[256,1024]{1,0:T(8,128)(2,1)}, bf16[256,1024]{1,0:T(8,128)(2,1)}, u32[]{:S(2)}, u32[]{:S(2)}) %collective-permute-start.30) | collective-permute-done | bytes 524320 | tf_op jit(solution)/shard_map/ppermute | solution.py:190
  185.2 4.1 fusion.73
  189.5 7.8 %fusion.3 = (f32[1024,1024]{1,0:T(8,128)}, bf16[1024,1024]{1,0:T(8,128)(2,1)S(1)}) fusion(bf16[1024,1024]{1,0:T(8,128)(2,1)S(1)} %bitcast.332, bf16[256,1024]{1,0:T(8,128)(2,1)} %collective-permute-done.31, bf16[256,1024]{1,0:T(8,128)(2,1)} %collective-permute-done.30, bf16[256,1024]{1,0:T(8,128)(2,1)} %collective-permute-done.29, ...), kind=kOutput, calls=%fused_computation.4 | convolution fusion | flops 2166358016 | bytes 10485760 | tf_op jit(solution)/shard_map/dot_general | solution.py:20
  197.4 3.7 convolution_convert_fusion.1
  201.4 6.0 %multiply_convert_fusion = bf16[1024,1024]{1,0:T(8,128)(2,1)S(1)} fusion(f32[1024,1024]{1,0:T(8,128)} %get-tuple-element.67, bf16[1024,1024]{1,0:T(8,128)(2,1)} %pad_maximum_fusion.1, bf16[1024,1024]{1,0:T(8,128)(2,1)} %bitcast.340), kind=kOutput, calls=%fused_computation.5 | convolution fusion | flops 2149580800 | bytes 10485760 | tf_op jit(solution)/shard_map/dot_general | solution.py:24
  207.4 2.4 fusion.78
  210.5 2.3 collective-permute-done.32
  216.8 5.2 %convolution_convert_fusion = bf16[1024,1024]{1,0:T(8,128)(2,1)} fusion(bf16[1024,1024]{1,0:T(8,128)(2,1)S(1)} %multiply_convert_fusion, bf16[256,1024]{1,0:T(8,128)(2,1)} %collective-permute-done.31, bf16[256,1024]{1,0:T(8,128)(2,1)} %collective-permute-done.30, bf16[256,1024]{1,0:T(8,128)(2,1)} %collective-permute-done.29, ...), kind=kOutput, calls=%fused_computation.22 | convolution fusion | flops 2156920832 | bytes 6291456 | tf_op jit(solution)/shard_map/dot_general | solution.py:28
  222.1 7.8 %collective-permute-done.33 = bf16[256,1024]{1,0:T(8,128)(2,1)} collective-permute-done((bf16[256,1024]{1,0:T(8,128)(2,1)}, bf16[256,1024]{1,0:T(8,128)(2,1)}, u32[]{:S(2)}, u32[]{:S(2)}) %collective-permute-start.33) | collective-permute-done | bytes 524320 | tf_op jit(solution)/shard_map/ppermute | solution.py:190
  229.8 2.2 multiply_reduce_fusion
  232.1 3.1 multiply_convert_fusion.2
  237.3 11.4 %collective-permute-done.35 = bf16[256,1024]{1,0:T(8,128)(2,1)S(1)} collective-permute-done((bf16[256,1024]{1,0:T(8,128)(2,1)}, bf16[256,1024]{1,0:T(8,128)(2,1)S(1)}, u32[]{:S(2)}, u32[]{:S(2)}) %collective-permute-start.35) | collective-permute-done | bytes 524320 | tf_op jit(solution)/shard_map/ppermute | solution.py:190
  248.7 4.7 %convolution_convert_fusion.2 = bf16[1024,1024]{1,0:T(8,128)(2,1)S(1)} fusion(bf16[1024,1024]{1,0:T(8,128)(2,1)} %copy-done.52, bf16[1024,1024]{1,0:T(8,128)(2,1)} %bitcast.341), kind=kOutput, calls=%fused_computation.24 | convolution fusion | flops 2148532224 | bytes 6291456 | tf_op jit(solution)/shard_map/dot_general | solution.py:20
  258.7 6.0 %collective-permute-done.40 = bf16[4,32,1024]{2,1,0:T(8,128)(2,1)S(1)} collective-permute-done((bf16[4,32,1024]{2,1,0:T(8,128)(2,1)S(1)}, bf16[4,32,1024]{2,1,0:T(8,128)(2,1)S(1)}, u32[]{:S(2)}, u32[]{:S(2)}) %collective-permute-start.40) | collective-permute-done | bytes 262176 | tf_op jit(solution)/shard_map/ppermute | solution.py:190
  265.6 10.8 %collective-permute-done.41 = bf16[2,2,32,1024]{3,2,1,0:T(8,128)(2,1)S(1)} collective-permute-done((bf16[2,2,32,1024]{3,2,1,0:T(8,128)(2,1)S(1)}, bf16[2,2,32,1024]{3,2,1,0:T(8,128)(2,1)S(1)}, u32[]{:S(2)}, u32[]{:S(2)}) %collective-permute-start.41) | collective-permute-done | bytes 262176 | tf_op jit(solution)/shard_map/ppermute | solution.py:190
  277.7 10.2 %shard_map.188 = (bf16[1024,128]{1,0:T(8,128)(2,1)S(1)}, bf16[1024,128]{1,0:T(8,128)(2,1)S(1)}, bf16[1024,128]{1,0:T(8,128)(2,1)S(1)}) custom-call(bf16[1024,256]{1,0:T(8,128)(2,1)S(1)} %copy-done.1, bf16[1024,256]{1,0:T(8,128)(2,1)S(1)} %copy-done.4, bf16[1024,256]{1,0:T(8,128)(2,1)S(1)} %copy-done.7, f32[1024,256]{1,0:T(8,128)S(1)} %get-tuple-element.60.logs, ...), custom_call_target="tpu_custom_call" | custom-call | flops 5368709120 | bytes 3145728 | tf_op jit(solution)/shard_map/pallas_call | solution.py:168
  288.6 1.7 dynamic-slice_bitcast_fusion.4
  290.3 2.9 collective-permute-start.38
  293.2 13.5 %collective-permute-done.43 = bf16[32,1024]{1,0:T(8,128)(2,1)} collective-permute-done((bf16[32,1024]{1,0:T(8,128)(2,1)}, bf16[32,1024]{1,0:T(8,128)(2,1)}, u32[]{:S(2)}, u32[]{:S(2)}) %collective-permute-start.43) | collective-permute-done | bytes 65568 | tf_op jit(solution)/shard_map/ppermute | solution.py:190
  309.6 2.8 collective-permute-done.38
  312.3 1.9 convert_add_fusion.7
  314.3 1.7 convert_add_fusion
  316.2 10.0 %shard_map.189 = (bf16[1024,128]{1,0:T(8,128)(2,1)S(1)}, bf16[1024,128]{1,0:T(8,128)(2,1)S(1)}, bf16[1024,128]{1,0:T(8,128)(2,1)S(1)}) custom-call(bf16[1024,256]{1,0:T(8,128)(2,1)S(1)} %copy-done.2, bf16[1024,256]{1,0:T(8,128)(2,1)S(1)} %copy-done.5, bf16[1024,256]{1,0:T(8,128)(2,1)S(1)} %copy-done.8, f32[1024,256]{1,0:T(8,128)S(1)} %get-tuple-element.60.logs, ...), custom_call_target="tpu_custom_call" | custom-call | flops 5368709120 | bytes 3145728 | tf_op jit(solution)/shard_map/pallas_call | solution.py:168
  328.4 1.8 fusion.79
  330.3 2.1 copy-done.16
  334.0 1.7 collective-permute-start.45
  337.2 1.9 convolution_convert_fusion.3
  339.1 3.8 collective-permute-done.63
  348.8 1.7 fusion.4
  351.3 3.4 collective-permute-done.57
  357.1 2.9 collective-permute-done.47
  360.6 5.4 %collective-permute-start.49 = (f32[1,2048]{1,0:T(1,128)S(1)}, f32[1,2048]{1,0:T(1,128)S(1)}, u32[]{:S(2)}, u32[]{:S(2)}) collective-permute-start(f32[1,2048]{1,0:T(1,128)S(1)} %pad_maximum_fusion.10), channel_id=1, source_target_pairs={{0,4},{4,0},{1,5},{5,1},{2,6},{6,2},{3,7},{7,3},{8,12},{12,8},{9,1... | collective-permute-start | bytes 24584 | tf_op jit(solution)/shard_map/ppermute | solution.py:190
  367.5 3.0 collective-permute-done.50
  370.5 1.8 collective-permute-start.51
  373.5 1.6 collective-permute-done.51
  378.6 1.8 collective-permute-start.56
  382.0 14.1 %collective-permute-done.59 = bf16[2,2,32,384]{3,2,1,0:T(8,128)(2,1)S(1)} collective-permute-done((bf16[2,2,32,384]{3,2,1,0:T(8,128)(2,1)S(1)}, bf16[2,2,32,384]{3,2,1,0:T(8,128)(2,1)S(1)}, u32[]{:S(2)}, u32[]{:S(2)}) %collective-permute-start.59) | collective-permute-done | bytes 98336 | tf_op jit(solution)/shard_map/ppermute | solution.py:190
  397.4 1.7 collective-permute-start.53
  399.2 2.7 collective-permute-done.53
  (361 shorter events, 74.4 us)
Async XLA Ops:
  7.2 178.0 %all-gather.3.cloned.1.call-start = ((), (), s32[]{:S(2)}) async-start(), calls=%async_computation.2 | async-start | bytes 4718592 | tf_op jit(solution)/shard_map/all_gather | solution.py:353
  9.9 13.8 %collective-permute-start.1 = (bf16[2,32,768]{2,1,0:T(8,128)(2,1)S(1)}, bf16[2,32,768]{2,1,0:T(8,128)(2,1)S(1)}, u32[]{:S(2)}, u32[]{:S(2)}) collective-permute-start(bf16[2,32,768]{2,1,0:T(8,128)(2,1)S(1)} %get-tuple-element.138), channel_id=1, source_target_pairs={{0,4},{4,0},{1,5},{5,1},{2,6},{6,2},{3,7},{7,3},{8,12},{12,8},{9,1... | collective-permute-start | bytes 294920 | tf_op jit(solution)/shard_map/ppermute | solution.py:190
  12.5 9.6 %collective-permute-start = (f32[1,1408]{1,0:T(1,128)S(1)}, f32[1,1408]{1,0:T(1,128)S(1)}, u32[]{:S(2)}, u32[]{:S(2)}) collective-permute-start(f32[1,1408]{1,0:T(1,128)S(1)} %pad_maximum_fusion.11), channel_id=1, source_target_pairs={{0,4},{4,0},{1,5},{5,1},{2,6},{6,2},{3,7},{7,3},{8,12},{12,8},{9,1... | collective-permute-start | bytes 16904 | tf_op jit(solution)/shard_map/ppermute | solution.py:190
  12.6 47.5 %collective-permute-start.11 = (bf16[256,1024]{1,0:T(8,128)(2,1)}, bf16[256,1024]{1,0:T(8,128)(2,1)S(1)}, u32[]{:S(2)}, u32[]{:S(2)}) collective-permute-start(bf16[256,1024]{1,0:T(8,128)(2,1)} %bitcast.360), channel_id=1, source_target_pairs={{2,4},{4,2},{3,5},{5,3},{10,12},{12,10},{11,13},{13,11},{18,20},{2... | collective-permute-start | bytes 1572872 | tf_op jit(solution)/shard_map/ppermute | solution.py:234
  14.6 10.9 %collective-permute-start.27 = (bf16[2,32,1024]{2,1,0:T(8,128)(2,1)S(1)}, bf16[2,32,1024]{2,1,0:T(8,128)(2,1)S(1)}, u32[]{:S(2)}, u32[]{:S(2)}) collective-permute-start(bf16[2,32,1024]{2,1,0:T(8,128)(2,1)S(1)} %get-tuple-element.130), channel_id=1, source_target_pairs={{0,4},{4,0},{1,5},{5,1},{2,6},{6,2},{3,7},{7,3},{8,12},{12,8},{9,1... | collective-permute-start | bytes 393224 | tf_op jit(solution)/shard_map/ppermute | solution.py:190
  23.8 9.3 %collective-permute-start.2 = (bf16[2,32,768]{2,1,0:T(8,128)(2,1)S(1)}, bf16[2,32,768]{2,1,0:T(8,128)(2,1)S(1)}, u32[]{:S(2)}, u32[]{:S(2)}) collective-permute-start(bf16[2,32,768]{2,1,0:T(8,128)(2,1)S(1)} %get-tuple-element.136), channel_id=1, source_target_pairs={{0,1},{1,0},{2,3},{3,2},{4,5},{5,4},{6,7},{7,6},{8,9},{9,8},{10,11... | collective-permute-start | bytes 294920 | tf_op jit(solution)/shard_map/ppermute | solution.py:190
  33.1 4.0 collective-permute-start.12
  34.7 12.8 %collective-permute-start.28 = (bf16[2,32,1024]{2,1,0:T(8,128)(2,1)S(1)}, bf16[2,32,1024]{2,1,0:T(8,128)(2,1)S(1)}, u32[]{:S(2)}, u32[]{:S(2)}) collective-permute-start(bf16[2,32,1024]{2,1,0:T(8,128)(2,1)S(1)} %get-tuple-element.128), channel_id=1, source_target_pairs={{0,1},{1,0},{2,3},{3,2},{4,5},{5,4},{6,7},{7,6},{8,9},{9,8},{10,11... | collective-permute-start | bytes 393224 | tf_op jit(solution)/shard_map/ppermute | solution.py:190
  37.1 4.3 %collective-permute-start.13 = (bf16[2,8,2048]{2,1,0:T(8,128)(2,1)S(1)}, bf16[2,8,2048]{2,1,0:T(8,128)(2,1)S(1)}, u32[]{:S(2)}, u32[]{:S(2)}) collective-permute-start(bf16[2,8,2048]{2,1,0:T(8,128)(2,1)S(1)} %maximum_select_fusion.25), channel_id=1, source_target_pairs={{0,16},{8,24},{16,0},{24,8},{1,17},{9,25},{17,1},{25,9},{2,18},{10... | collective-permute-start | bytes 196616 | tf_op jit(solution)/shard_map/ppermute | solution.py:190
  41.7 5.8 %collective-permute-start.14 = (f32[2048]{0:T(1024)S(1)}, f32[2048]{0:T(1024)S(1)}, u32[]{:S(2)}, u32[]{:S(2)}) collective-permute-start(f32[2048]{0:T(1024)S(1)} %bitcast.396), channel_id=1, source_target_pairs={{0,2},{2,0},{1,3},{3,1},{4,6},{6,4},{5,7},{7,5},{8,10},{10,8},{9,1... | collective-permute-start | bytes 24584 | tf_op jit(solution)/shard_map/ppermute | solution.py:190
  42.4 10.7 %collective-permute-start.3 = (bf16[2,2,32,768]{3,2,0,1:T(8,128)(2,1)S(1)}, bf16[2,2,32,768]{3,2,0,1:T(8,128)(2,1)S(1)}, u32[]{:S(2)}, u32[]{:S(2)}) collective-permute-start(bf16[2,2,32,768]{3,2,0,1:T(8,128)(2,1)S(1)} %maximum_select_fusion.17), channel_id=1, source_target_pairs={{0,2},{2,0},{1,3},{3,1},{4,6},{6,4},{5,7},{7,5},{8,10},{10,8},{9,1... | collective-permute-start | bytes 589832 | tf_op jit(solution)/shard_map/ppermute | solution.py:190
  47.5 4.5 %collective-permute-start.15 = (f32[2048]{0:T(1024)S(1)}, f32[2048]{0:T(1024)S(1)}, u32[]{:S(2)}, u32[]{:S(2)}) collective-permute-start(f32[2048]{0:T(1024)S(1)} %add.299), channel_id=1, source_target_pairs={{0,1},{1,0},{2,3},{3,2},{4,5},{5,4},{6,7},{7,6},{8,9},{9,8},{10,11... | collective-permute-start | bytes 24584 | tf_op jit(solution)/shard_map/ppermute | solution.py:190
  52.8 235.8 %reduce-scatter.7.cloned.1.call-start = ((), (), s32[]{:S(2)}) async-start(), calls=%async_computation.3 | async-start | bytes 2621440
  53.2 5.4 %collective-permute-start.20 = (bf16[32,1024]{1,0:T(8,128)(2,1)S(1)}, bf16[32,1024]{1,0:T(8,128)(2,1)S(1)}, u32[]{:S(2)}, u32[]{:S(2)}) collective-permute-start(bf16[32,1024]{1,0:T(8,128)(2,1)S(1)} %copy-done.30), channel_id=1, source_target_pairs={{0,2},{2,0},{1,3},{3,1},{4,6},{6,4},{5,7},{7,5},{8,10},{10,8},{9,1... | collective-permute-start | bytes 196616 | tf_op jit(solution)/shard_map/ppermute | solution.py:190
  53.4 7.7 %collective-permute-start.4 = (bf16[2,2,2,32,384]{4,3,1,0,2:T(8,128)(2,1)S(1)}, bf16[2,2,2,32,384]{4,3,1,0,2:T(8,128)(2,1)S(1)}, u32[]{:S(2)}, u32[]{:S(2)}) collective-permute-start(bf16[2,2,2,32,384]{4,3,1,0,2:T(8,128)(2,1)S(1)} %get-tuple-element.122), channel_id=1, source_target_pairs={{0,8},{8,0},{16,24},{24,16},{1,9},{9,1},{17,25},{25,17},{2,10},{10... | collective-permute-start | bytes 589832 | tf_op jit(solution)/shard_map/ppermute | solution.py:190
  54.5 14.3 %collective-permute-start.6 = (bf16[2,2,2,32,384]{4,3,1,0,2:T(8,128)(2,1)S(1)}, bf16[2,2,2,32,384]{4,3,1,0,2:T(8,128)(2,1)S(1)}, u32[]{:S(2)}, u32[]{:S(2)}) collective-permute-start(bf16[2,2,2,32,384]{4,3,1,0,2:T(8,128)(2,1)S(1)} %get-tuple-element.121), channel_id=1, source_target_pairs={{0,16},{8,24},{16,0},{24,8},{1,17},{9,25},{17,1},{25,9},{2,18},{10... | collective-permute-start | bytes 589832 | tf_op jit(solution)/shard_map/ppermute | solution.py:190
  56.0 30.8 %collective-permute-start.8 = (bf16[256,1024]{1,0:T(8,128)(2,1)S(1)}, bf16[256,1024]{1,0:T(8,128)(2,1)S(1)}, u32[]{:S(2)}, u32[]{:S(2)}) collective-permute-start(bf16[256,1024]{1,0:T(8,128)(2,1)S(1)} %bitcast.363), channel_id=1, source_target_pairs={{2,4},{4,2},{3,5},{5,3},{10,12},{12,10},{11,13},{13,11},{18,20},{2... | collective-permute-start | bytes 1572872 | tf_op jit(solution)/shard_map/ppermute | solution.py:234
  58.6 7.5 %collective-permute-start.21 = (bf16[2,32,1024]{2,1,0:T(8,128)(2,1)S(1)}, bf16[2,32,1024]{2,1,0:T(8,128)(2,1)S(1)}, u32[]{:S(2)}, u32[]{:S(2)}) collective-permute-start(bf16[2,32,1024]{2,1,0:T(8,128)(2,1)S(1)} %maximum_select_fusion.22), channel_id=1, source_target_pairs={{0,8},{8,0},{16,24},{24,16},{1,9},{9,1},{17,25},{25,17},{2,10},{10... | collective-permute-start | bytes 393224 | tf_op jit(solution)/shard_map/ppermute | solution.py:190
  61.0 26.1 %collective-permute-start.18 = (bf16[256,1024]{1,0:T(8,128)(2,1)S(1)}, bf16[256,1024]{1,0:T(8,128)(2,1)S(1)}, u32[]{:S(2)}, u32[]{:S(2)}) collective-permute-start(bf16[256,1024]{1,0:T(8,128)(2,1)S(1)} %fusion.13), channel_id=1, source_target_pairs={{0,1},{1,0},{2,3},{3,2},{4,5},{5,4},{6,7},{7,6},{8,9},{9,8},{10,11... | collective-permute-start | bytes 1572872 | tf_op jit(solution)/shard_map/ppermute | solution.py:190
  61.1 42.1 %collective-permute-start.17 = (bf16[256,1024]{1,0:T(8,128)(2,1)S(1)}, bf16[256,1024]{1,0:T(8,128)(2,1)S(1)}, u32[]{:S(2)}, u32[]{:S(2)}) collective-permute-start(bf16[256,1024]{1,0:T(8,128)(2,1)S(1)} %fusion.13), channel_id=1, source_target_pairs={{0,4},{4,0},{1,5},{5,1},{2,6},{6,2},{3,7},{7,3},{8,12},{12,8},{9,1... | collective-permute-start | bytes 1572872 | tf_op jit(solution)/shard_map/ppermute | solution.py:190
  66.2 20.8 %collective-permute-start.5 = (bf16[2,2,2,2,32,384]{5,4,2,1,3,0:T(8,128)(2,1)S(1)}, bf16[2,2,2,2,32,384]{5,4,2,1,3,0:T(8,128)(2,1)S(1)}, u32[]{:S(2)}, u32[]{:S(2)}) collective-permute-start(bf16[2,2,2,2,32,384]{5,4,2,1,3,0:T(8,128)(2,1)S(1)} %maximum_select_fusion.7), channel_id=1, source_target_pairs={{0,16},{8,24},{16,0},{24,8},{1,17},{9,25},{17,1},{25,9},{2,18},{10... | collective-permute-start | bytes 1179656 | tf_op jit(solution)/shard_map/ppermute | solution.py:190
  68.8 15.1 %collective-permute-start.22 = (bf16[2,2,32,1024]{3,2,1,0:T(8,128)(2,1)S(1)}, bf16[2,2,32,1024]{3,2,1,0:T(8,128)(2,1)S(1)}, u32[]{:S(2)}, u32[]{:S(2)}) collective-permute-start(bf16[2,2,32,1024]{3,2,1,0:T(8,128)(2,1)S(1)} %maximum_select_fusion.11), channel_id=1, source_target_pairs={{0,16},{8,24},{16,0},{24,8},{1,17},{9,25},{17,1},{25,9},{2,18},{10... | collective-permute-start | bytes 786440 | tf_op jit(solution)/shard_map/ppermute | solution.py:190
  83.8 16.6 %collective-permute-start.7 = (bf16[2,2,2,2,32,384]{5,4,2,1,3,0:T(8,128)(2,1)S(1)}, bf16[2,2,2,2,32,384]{5,4,2,1,3,0:T(8,128)(2,1)S(1)}, u32[]{:S(2)}, u32[]{:S(2)}) collective-permute-start(bf16[2,2,2,2,32,384]{5,4,2,1,3,0:T(8,128)(2,1)S(1)} %maximum_select_fusion.9), channel_id=1, source_target_pairs={{0,8},{8,0},{16,24},{24,16},{1,9},{9,1},{17,25},{25,17},{2,10},{10... | collective-permute-start | bytes 1179656 | tf_op jit(solution)/shard_map/ppermute | solution.py:190
  87.1 16.1 %collective-permute-start.19 = (bf16[256,1024]{1,0:T(8,128)(2,1)S(1)}, bf16[256,1024]{1,0:T(8,128)(2,1)S(1)}, u32[]{:S(2)}, u32[]{:S(2)}) collective-permute-start(bf16[256,1024]{1,0:T(8,128)(2,1)S(1)} %collective-permute-done.18), channel_id=1, source_target_pairs={{0,4},{4,0},{1,5},{5,1},{2,6},{6,2},{3,7},{7,3},{8,12},{12,8},{9,1... | collective-permute-start | bytes 1572872 | tf_op jit(solution)/shard_map/ppermute | solution.py:190
  100.9 4.2 %collective-permute-start.10 = (bf16[256,1024]{1,0:T(8,128)(2,1)S(1)}, bf16[256,1024]{1,0:T(8,128)(2,1)S(1)}, u32[]{:S(2)}, u32[]{:S(2)}) collective-permute-start(bf16[256,1024]{1,0:T(8,128)(2,1)S(1)} %fusion.21), channel_id=1, source_target_pairs={{0,4},{4,0},{1,5},{5,1},{2,6},{6,2},{3,7},{7,3},{8,12},{12,8},{9,1... | collective-permute-start | bytes 1572872 | tf_op jit(solution)/shard_map/ppermute | solution.py:190
  101.1 23.7 %collective-permute-start.9 = (bf16[256,1024]{1,0:T(8,128)(2,1)S(1)}, bf16[256,1024]{1,0:T(8,128)(2,1)S(1)}, u32[]{:S(2)}, u32[]{:S(2)}) collective-permute-start(bf16[256,1024]{1,0:T(8,128)(2,1)S(1)} %fusion.21), channel_id=1, source_target_pairs={{0,1},{1,0},{2,3},{3,2},{4,5},{5,4},{6,7},{7,6},{8,9},{9,8},{10,11... | collective-permute-start | bytes 1572872 | tf_op jit(solution)/shard_map/ppermute | solution.py:190
  102.6 32.4 %collective-permute-start.23 = (bf16[4,32,1024]{2,1,0:T(8,128)(2,1)S(1)}, bf16[4,32,1024]{2,1,0:T(8,128)(2,1)S(1)}, u32[]{:S(2)}, u32[]{:S(2)}) collective-permute-start(bf16[4,32,1024]{2,1,0:T(8,128)(2,1)S(1)} %get-tuple-element.114), channel_id=1, source_target_pairs={{0,1},{1,0},{2,3},{3,2},{4,5},{5,4},{6,7},{7,6},{8,9},{9,8},{10,11... | collective-permute-start | bytes 786440 | tf_op jit(solution)/shard_map/ppermute | solution.py:190
  124.8 23.6 %collective-permute-start.24 = (bf16[256,1024]{1,0:T(8,128)(2,1)S(1)}, bf16[256,1024]{1,0:T(8,128)(2,1)S(1)}, u32[]{:S(2)}, u32[]{:S(2)}) collective-permute-start(bf16[256,1024]{1,0:T(8,128)(2,1)S(1)} %collective-permute-done.9), channel_id=1, source_target_pairs={{0,4},{4,0},{1,5},{5,1},{2,6},{6,2},{3,7},{7,3},{8,12},{12,8},{9,1... | collective-permute-start | bytes 1572872 | tf_op jit(solution)/shard_map/ppermute | solution.py:190
  154.4 14.8 %collective-permute-start.26 = (bf16[256,1024]{1,0:T(8,128)(2,1)S(1)}, bf16[256,1024]{1,0:T(8,128)(2,1)S(1)}, u32[]{:S(2)}, u32[]{:S(2)}) collective-permute-start(bf16[256,1024]{1,0:T(8,128)(2,1)S(1)} %fusion.38), channel_id=1, source_target_pairs={{0,1},{1,0},{2,3},{3,2},{4,5},{5,4},{6,7},{7,6},{8,9},{9,8},{10,11... | collective-permute-start | bytes 1572872 | tf_op jit(solution)/shard_map/ppermute | solution.py:190
  171.5 13.7 %collective-permute-start.30 = (bf16[256,1024]{1,0:T(8,128)(2,1)}, bf16[256,1024]{1,0:T(8,128)(2,1)}, u32[]{:S(2)}, u32[]{:S(2)}) collective-permute-start(bf16[256,1024]{1,0:T(8,128)(2,1)} %multiply_convert_fusion.3), channel_id=1, source_target_pairs={{0,1},{1,0},{2,3},{3,2},{4,5},{5,4},{6,7},{7,6},{8,9},{9,8},{10,11... | collective-permute-start | bytes 1572872 | tf_op jit(solution)/shard_map/ppermute | solution.py:190
  173.2 16.3 %collective-permute-start.29 = (bf16[256,1024]{1,0:T(8,128)(2,1)}, bf16[256,1024]{1,0:T(8,128)(2,1)}, u32[]{:S(2)}, u32[]{:S(2)}) collective-permute-start(bf16[256,1024]{1,0:T(8,128)(2,1)} %multiply_convert_fusion.3), channel_id=1, source_target_pairs={{0,4},{4,0},{1,5},{5,1},{2,6},{6,2},{3,7},{7,3},{8,12},{12,8},{9,1... | collective-permute-start | bytes 1572872 | tf_op jit(solution)/shard_map/ppermute | solution.py:190
  185.2 4.3 %collective-permute-start.31 = (bf16[256,1024]{1,0:T(8,128)(2,1)}, bf16[256,1024]{1,0:T(8,128)(2,1)}, u32[]{:S(2)}, u32[]{:S(2)}) collective-permute-start(bf16[256,1024]{1,0:T(8,128)(2,1)} %collective-permute-done.30), channel_id=1, source_target_pairs={{0,4},{4,0},{1,5},{5,1},{2,6},{6,2},{3,7},{7,3},{8,12},{12,8},{9,1... | collective-permute-start | bytes 1572872 | tf_op jit(solution)/shard_map/ppermute | solution.py:190
  201.2 107.1 %reduce-scatter.9.cloned.1.call-start = ((), (), s32[]{:S(2)}) async-start(), calls=%async_computation.4 | async-start | bytes 2621440
  209.9 2.9 collective-permute-start.32
  215.3 14.5 %collective-permute-start.33 = (bf16[256,1024]{1,0:T(8,128)(2,1)}, bf16[256,1024]{1,0:T(8,128)(2,1)}, u32[]{:S(2)}, u32[]{:S(2)}) collective-permute-start(bf16[256,1024]{1,0:T(8,128)(2,1)} %fusion.39), channel_id=1, source_target_pairs={{0,1},{1,0},{2,3},{3,2},{4,5},{5,4},{6,7},{7,6},{8,9},{9,8},{10,11... | collective-permute-start | bytes 1572872 | tf_op jit(solution)/shard_map/ppermute | solution.py:190
  235.2 13.6 %collective-permute-start.35 = (bf16[256,1024]{1,0:T(8,128)(2,1)}, bf16[256,1024]{1,0:T(8,128)(2,1)S(1)}, u32[]{:S(2)}, u32[]{:S(2)}) collective-permute-start(bf16[256,1024]{1,0:T(8,128)(2,1)} %get-tuple-element.95), channel_id=1, source_target_pairs={{0,1},{1,0},{2,3},{3,2},{4,5},{5,4},{6,7},{7,6},{8,9},{9,8},{10,11... | collective-permute-start | bytes 1572872 | tf_op jit(solution)/shard_map/ppermute | solution.py:190
  237.3 16.1 %collective-permute-start.34 = (bf16[256,1024]{1,0:T(8,128)(2,1)}, bf16[256,1024]{1,0:T(8,128)(2,1)S(1)}, u32[]{:S(2)}, u32[]{:S(2)}) collective-permute-start(bf16[256,1024]{1,0:T(8,128)(2,1)} %get-tuple-element.95), channel_id=1, source_target_pairs={{0,4},{4,0},{1,5},{5,1},{2,6},{6,2},{3,7},{7,3},{8,12},{12,8},{9,1... | collective-permute-start | bytes 1572872 | tf_op jit(solution)/shard_map/ppermute | solution.py:190
  248.7 4.7 %collective-permute-start.36 = (bf16[256,1024]{1,0:T(8,128)(2,1)S(1)}, bf16[256,1024]{1,0:T(8,128)(2,1)S(1)}, u32[]{:S(2)}, u32[]{:S(2)}) collective-permute-start(bf16[256,1024]{1,0:T(8,128)(2,1)S(1)} %collective-permute-done.35), channel_id=1, source_target_pairs={{0,4},{4,0},{1,5},{5,1},{2,6},{6,2},{3,7},{7,3},{8,12},{12,8},{9,1... | collective-permute-start | bytes 1572872 | tf_op jit(solution)/shard_map/ppermute | solution.py:190
  255.9 8.8 %collective-permute-start.40 = (bf16[4,32,1024]{2,1,0:T(8,128)(2,1)S(1)}, bf16[4,32,1024]{2,1,0:T(8,128)(2,1)S(1)}, u32[]{:S(2)}, u32[]{:S(2)}) collective-permute-start(bf16[4,32,1024]{2,1,0:T(8,128)(2,1)S(1)} %get-tuple-element.112), channel_id=1, source_target_pairs={{0,1},{1,0},{2,3},{3,2},{4,5},{5,4},{6,7},{7,6},{8,9},{9,8},{10,11... | collective-permute-start | bytes 786440 | tf_op jit(solution)/shard_map/ppermute | solution.py:190
  258.5 55.8 %collective-permute-start.37 = (bf16[2,256,1024]{2,1,0:T(8,128)(2,1)}, bf16[2,256,1024]{2,1,0:T(8,128)(2,1)}, u32[]{:S(2)}, u32[]{:S(2)}) collective-permute-start(bf16[2,256,1024]{2,1,0:T(8,128)(2,1)} %slice_bitcast_fusion.4), channel_id=1, source_target_pairs={{0,4},{4,0},{1,5},{5,1},{2,6},{6,2},{3,7},{7,3},{8,12},{12,8},{9,1... | collective-permute-start | bytes 3145736 | tf_op jit(solution)/shard_map/ppermute | solution.py:190
  264.8 11.7 %collective-permute-start.41 = (bf16[2,2,32,1024]{3,2,1,0:T(8,128)(2,1)S(1)}, bf16[2,2,32,1024]{3,2,1,0:T(8,128)(2,1)S(1)}, u32[]{:S(2)}, u32[]{:S(2)}) collective-permute-start(bf16[2,2,32,1024]{3,2,1,0:T(8,128)(2,1)S(1)} %dynamic-slice_bitcast_fusion.2), channel_id=1, source_target_pairs={{0,8},{8,0},{16,24},{24,16},{1,9},{9,1},{17,25},{25,17},{2,10},{10... | collective-permute-start | bytes 786440 | tf_op jit(solution)/shard_map/ppermute | solution.py:190
  276.5 11.4 %collective-permute-start.42 = (bf16[2,32,1024]{2,1,0:T(8,128)(2,1)S(1)}, bf16[2,32,1024]{2,1,0:T(8,128)(2,1)S(1)}, u32[]{:S(2)}, u32[]{:S(2)}) collective-permute-start(bf16[2,32,1024]{2,1,0:T(8,128)(2,1)S(1)} %dynamic-slice_bitcast_fusion.12), channel_id=1, source_target_pairs={{0,16},{8,24},{16,0},{24,8},{1,17},{9,25},{17,1},{25,9},{2,18},{10... | collective-permute-start | bytes 393224 | tf_op jit(solution)/shard_map/ppermute | solution.py:190
  288.6 18.1 %collective-permute-start.43 = (bf16[32,1024]{1,0:T(8,128)(2,1)}, bf16[32,1024]{1,0:T(8,128)(2,1)}, u32[]{:S(2)}, u32[]{:S(2)}) collective-permute-start(bf16[32,1024]{1,0:T(8,128)(2,1)} %dynamic-slice_bitcast_fusion.24), channel_id=1, source_target_pairs={{0,2},{2,0},{1,3},{3,1},{4,6},{6,4},{5,7},{7,5},{8,10},{10,8},{9,1... | collective-permute-start | bytes 196616 | tf_op jit(solution)/shard_map/ppermute | solution.py:190
  290.3 22.1 %collective-permute-start.38 = (bf16[128,1024]{1,0:T(8,128)(2,1)}, bf16[128,1024]{1,0:T(8,128)(2,1)}, u32[]{:S(2)}, u32[]{:S(2)}) collective-permute-start(bf16[128,1024]{1,0:T(8,128)(2,1)} %dynamic-slice_bitcast_fusion.4), channel_id=1, source_target_pairs={{0,2},{2,0},{1,3},{3,1},{4,6},{6,4},{5,7},{7,5},{8,10},{10,8},{9,1... | collective-permute-start | bytes 786440 | tf_op jit(solution)/shard_map/ppermute | solution.py:190
  309.5 17.1 %collective-permute-start.44 = (bf16[128,1024]{1,0:T(8,128)(2,1)S(1)}, bf16[128,1024]{1,0:T(8,128)(2,1)S(1)}, u32[]{:S(2)}, u32[]{:S(2)}) collective-permute-start(bf16[128,1024]{1,0:T(8,128)(2,1)S(1)} %dynamic-slice_bitcast_fusion.1), channel_id=1, source_target_pairs={{0,2},{2,0},{1,3},{3,1},{4,6},{6,4},{5,7},{7,5},{8,10},{10,8},{9,1... | collective-permute-start | bytes 786440 | tf_op jit(solution)/shard_map/ppermute | solution.py:190
  316.1 12.0 %collective-permute-start.39 = (bf16[256,1024]{1,0:T(8,128)(2,1)S(1)}, bf16[256,1024]{1,0:T(8,128)(2,1)S(1)}, u32[]{:S(2)}, u32[]{:S(2)}) collective-permute-start(bf16[256,1024]{1,0:T(8,128)(2,1)S(1)} %fusion.40), channel_id=1, source_target_pairs={{0,1},{1,0},{2,3},{3,2},{4,5},{5,4},{6,7},{7,6},{8,9},{9,8},{10,11... | collective-permute-start | bytes 1572872 | tf_op jit(solution)/shard_map/ppermute | solution.py:190
  328.3 7.4 %collective-permute-start.62 = (bf16[2,32,1024]{2,1,0:T(8,128)(2,1)S(1)}, bf16[2,32,1024]{2,1,0:T(8,128)(2,1)S(1)}, u32[]{:S(2)}, u32[]{:S(2)}) collective-permute-start(bf16[2,32,1024]{2,1,0:T(8,128)(2,1)S(1)} %get-tuple-element.126), channel_id=1, source_target_pairs={{0,4},{4,0},{1,5},{5,1},{2,6},{6,2},{3,7},{7,3},{8,12},{12,8},{9,1... | collective-permute-start | bytes 393224 | tf_op jit(solution)/shard_map/ppermute | solution.py:190
  333.5 13.1 %collective-permute-start.46 = (bf16[2,256,1024]{2,1,0:T(8,128)(2,1)}, bf16[2,256,1024]{2,1,0:T(8,128)(2,1)}, u32[]{:S(2)}, u32[]{:S(2)}) collective-permute-start(bf16[2,256,1024]{2,1,0:T(8,128)(2,1)} %fusion.24), channel_id=1, source_target_pairs={{0,4},{4,0},{1,5},{5,1},{2,6},{6,2},{3,7},{7,3},{8,12},{12,8},{9,1... | collective-permute-start | bytes 3145736 | tf_op jit(solution)/shard_map/ppermute | solution.py:190
  334.0 11.8 %collective-permute-start.45 = (bf16[256,1024]{1,0:T(8,128)(2,1)S(1)}, bf16[256,1024]{1,0:T(8,128)(2,1)}, u32[]{:S(2)}, u32[]{:S(2)}) collective-permute-start(bf16[256,1024]{1,0:T(8,128)(2,1)S(1)} %fusion.29), channel_id=1, source_target_pairs={{2,4},{4,2},{3,5},{5,3},{10,12},{12,10},{11,13},{13,11},{18,20},{2... | collective-permute-start | bytes 1572872 | tf_op jit(solution)/shard_map/ppermute | solution.py:234
  335.8 7.1 %collective-permute-start.63 = (bf16[2,32,1024]{2,1,0:T(8,128)(2,1)S(1)}, bf16[2,32,1024]{2,1,0:T(8,128)(2,1)S(1)}, u32[]{:S(2)}, u32[]{:S(2)}) collective-permute-start(bf16[2,32,1024]{2,1,0:T(8,128)(2,1)S(1)} %get-tuple-element.124), channel_id=1, source_target_pairs={{0,1},{1,0},{2,3},{3,2},{4,5},{5,4},{6,7},{7,6},{8,9},{9,8},{10,11... | collective-permute-start | bytes 393224 | tf_op jit(solution)/shard_map/ppermute | solution.py:190
  346.9 7.8 %collective-permute-start.57 = (bf16[2,2,2,2,32,384]{5,4,3,2,1,0:T(8,128)(2,1)S(1)}, bf16[2,2,2,2,32,384]{5,4,3,2,1,0:T(8,128)(2,1)S(1)}, u32[]{:S(2)}, u32[]{:S(2)}) collective-permute-start(bf16[2,2,2,2,32,384]{5,4,3,2,1,0:T(8,128)(2,1)S(1)} %dynamic-slice_bitcast_fusion), channel_id=1, source_target_pairs={{0,16},{8,24},{16,0},{24,8},{1,17},{9,25},{17,1},{25,9},{2,18},{10... | collective-permute-start | bytes 1179656 | tf_op jit(solution)/shard_map/ppermute | solution.py:190
  348.4 7.8 %collective-permute-start.54 = (bf16[2,2,2,2,32,384]{5,4,3,1,2,0:T(8,128)(2,1)S(1)}, bf16[2,2,2,2,32,384]{5,4,3,1,2,0:T(8,128)(2,1)S(1)}, u32[]{:S(2)}, u32[]{:S(2)}) collective-permute-start(bf16[2,2,2,2,32,384]{5,4,3,1,2,0:T(8,128)(2,1)S(1)} %bitcast.369), channel_id=1, source_target_pairs={{0,8},{8,0},{16,24},{24,16},{1,9},{9,1},{17,25},{25,17},{2,10},{10... | collective-permute-start | bytes 1179656 | tf_op jit(solution)/shard_map/ppermute | solution.py:190
  350.6 9.4 %collective-permute-start.47 = (bf16[256,1024]{1,0:T(8,128)(2,1)S(1)}, bf16[256,1024]{1,0:T(8,128)(2,1)S(1)}, u32[]{:S(2)}, u32[]{:S(2)}) collective-permute-start(bf16[256,1024]{1,0:T(8,128)(2,1)S(1)} %fusion.41), channel_id=1, source_target_pairs={{0,1},{1,0},{2,3},{3,2},{4,5},{5,4},{6,7},{7,6},{8,9},{9,8},{10,11... | collective-permute-start | bytes 1572872 | tf_op jit(solution)/shard_map/ppermute | solution.py:190
  354.9 22.3 %collective-permute-start.58 = (bf16[2,2,2,32,384]{4,3,2,1,0:T(8,128)(2,1)S(1)}, bf16[2,2,2,32,384]{4,3,2,1,0:T(8,128)(2,1)S(1)}, u32[]{:S(2)}, u32[]{:S(2)}) collective-permute-start(bf16[2,2,2,32,384]{4,3,2,1,0:T(8,128)(2,1)S(1)} %dynamic-slice_bitcast_fusion.6), channel_id=1, source_target_pairs={{0,8},{8,0},{16,24},{24,16},{1,9},{9,1},{17,25},{25,17},{2,10},{10... | collective-permute-start | bytes 589832 | tf_op jit(solution)/shard_map/ppermute | solution.py:190
  356.4 22.1 %collective-permute-start.55 = (bf16[2,2,2,32,384]{4,3,2,0,1:T(8,128)(2,1)S(1)}, bf16[2,2,2,32,384]{4,3,2,0,1:T(8,128)(2,1)S(1)}, u32[]{:S(2)}, u32[]{:S(2)}) collective-permute-start(bf16[2,2,2,32,384]{4,3,2,0,1:T(8,128)(2,1)S(1)} %dynamic-slice_bitcast_fusion.7), channel_id=1, source_target_pairs={{0,16},{8,24},{16,0},{24,8},{1,17},{9,25},{17,1},{25,9},{2,18},{10... | collective-permute-start | bytes 589832 | tf_op jit(solution)/shard_map/ppermute | solution.py:190
  360.6 6.2 %collective-permute-start.49 = (f32[1,2048]{1,0:T(1,128)S(1)}, f32[1,2048]{1,0:T(1,128)S(1)}, u32[]{:S(2)}, u32[]{:S(2)}) collective-permute-start(f32[1,2048]{1,0:T(1,128)S(1)} %pad_maximum_fusion.10), channel_id=1, source_target_pairs={{0,4},{4,0},{1,5},{5,1},{2,6},{6,2},{3,7},{7,3},{8,12},{12,8},{9,1... | collective-permute-start | bytes 24584 | tf_op jit(solution)/shard_map/ppermute | solution.py:190
  366.8 3.7 collective-permute-start.50
  370.5 4.6 %collective-permute-start.51 = (f32[1,2048]{1,0:T(1,128)S(1)}, f32[1,2048]{1,0:T(1,128)S(1)}, u32[]{:S(2)}, u32[]{:S(2)}) collective-permute-start(f32[1,2048]{1,0:T(1,128)S(1)} %add.341), channel_id=1, source_target_pairs={{0,2},{2,0},{1,3},{3,1},{4,6},{6,4},{5,7},{7,5},{8,10},{10,8},{9,1... | collective-permute-start | bytes 24584 | tf_op jit(solution)/shard_map/ppermute | solution.py:190
  372.8 33.6 %collective-permute-start.48 = (bf16[256,1024]{1,0:T(8,128)(2,1)S(1)}, bf16[256,1024]{1,0:T(8,128)(2,1)S(1)}, u32[]{:S(2)}, u32[]{:S(2)}) collective-permute-start(bf16[256,1024]{1,0:T(8,128)(2,1)S(1)} %fusion.18), channel_id=1, source_target_pairs={{2,4},{4,2},{3,5},{5,3},{10,12},{12,10},{11,13},{13,11},{18,20},{2... | collective-permute-start | bytes 1572872 | tf_op jit(solution)/shard_map/ppermute | solution.py:234
  375.6 6.4 %collective-permute-start.52 = (f32[2,8,2048]{2,1,0:T(8,128)S(1)}, f32[2,8,2048]{2,1,0:T(8,128)S(1)}, u32[]{:S(2)}, u32[]{:S(2)}) collective-permute-start(f32[2,8,2048]{2,1,0:T(8,128)S(1)} %dynamic-slice_bitcast_fusion.11), channel_id=1, source_target_pairs={{0,16},{8,24},{16,0},{24,8},{1,17},{9,25},{17,1},{25,9},{2,18},{10... | collective-permute-start | bytes 393224 | tf_op jit(solution)/shard_map/ppermute | solution.py:190
  377.2 18.9 %collective-permute-start.59 = (bf16[2,2,32,384]{3,2,1,0:T(8,128)(2,1)S(1)}, bf16[2,2,32,384]{3,2,1,0:T(8,128)(2,1)S(1)}, u32[]{:S(2)}, u32[]{:S(2)}) collective-permute-start(bf16[2,2,32,384]{3,2,1,0:T(8,128)(2,1)S(1)} %dynamic-slice_bitcast_fusion.18), channel_id=1, source_target_pairs={{0,2},{2,0},{1,3},{3,1},{4,6},{6,4},{5,7},{7,5},{8,10},{10,8},{9,1... | collective-permute-start | bytes 294920 | tf_op jit(solution)/shard_map/ppermute | solution.py:190
  378.6 18.6 %collective-permute-start.56 = (bf16[2,2,32,384]{3,2,1,0:T(8,128)(2,1)S(1)}, bf16[2,2,32,384]{3,2,1,0:T(8,128)(2,1)S(1)}, u32[]{:S(2)}, u32[]{:S(2)}) collective-permute-start(bf16[2,2,32,384]{3,2,1,0:T(8,128)(2,1)S(1)} %dynamic-slice_bitcast_fusion.19), channel_id=1, source_target_pairs={{0,2},{2,0},{1,3},{3,1},{4,6},{6,4},{5,7},{7,5},{8,10},{10,8},{9,1... | collective-permute-start | bytes 294920 | tf_op jit(solution)/shard_map/ppermute | solution.py:190
  397.4 4.5 %collective-permute-start.53 = (f32[8,2048]{1,0:T(8,128)S(1)}, f32[8,2048]{1,0:T(8,128)S(1)}, u32[]{:S(2)}, u32[]{:S(2)}) collective-permute-start(f32[8,2048]{1,0:T(8,128)S(1)} %dynamic-slice_bitcast_fusion.23), channel_id=1, source_target_pairs={{0,8},{8,0},{16,24},{24,16},{1,9},{9,1},{17,25},{25,17},{2,10},{10... | collective-permute-start | bytes 196616 | tf_op jit(solution)/shard_map/ppermute | solution.py:190
  399.1 4.9 %collective-permute-start.61 = (bf16[2,32,768]{2,1,0:T(8,128)(2,1)S(1)}, bf16[2,32,768]{2,1,0:T(8,128)(2,1)S(1)}, u32[]{:S(2)}, u32[]{:S(2)}) collective-permute-start(bf16[2,32,768]{2,1,0:T(8,128)(2,1)S(1)} %get-tuple-element.132), channel_id=1, source_target_pairs={{0,1},{1,0},{2,3},{3,2},{4,5},{5,4},{6,7},{7,6},{8,9},{9,8},{10,11... | collective-permute-start | bytes 294920 | tf_op jit(solution)/shard_map/ppermute | solution.py:190
  (56 other events, 708.9 us)
Sparse Core Ops, SparseCore 0:
  52.9 85.4 all-gather.2
  201.3 32.5 reduce-scatter.6
  236.9 38.6 reduce-scatter.8
